TPU v7x, 512 devices: a whole 4x8x8 slice. The times are simulated.
512 devices in a mesh: dp: 32 (over x, y), tensor: 16 (over z, core).
Axes of the slice: x: 4, y: 8, z: 8, core: 2. Of those that a mesh axis runs over, the one named last changes fastest.
Arguments:
- features: bfloat16 [16384, 1280], P('dp'), may hold values from -6 to 6
- class_bias: float32 [12288], P('tensor')
- logits: bfloat16 [16384, 12288], P('dp', 'tensor'), may hold values from -12 to 12
- tile_lists: int32 [512, 2], P('dp'), may hold values from 0 to 31, all different within a row; in each aligned block of 16 rows (0 to 15, 16 to 31, ...) at most 2 rows name the same one
- valid_counts: int32 [32], P('dp'), may hold values from 192 to 512, as said below
Outputs:
- log_labels: float32 [16384, 12288], P('dp', 'tensor')
Inputs may be any that keep to these rules, and one draw needn't show every extreme that they name: `tile_lists`: each row names 2 different tiles; among the 16 rows of one index of dp no tile is named more than 2 times. `valid_counts`: some tile is fully valid.
All inputs are finite; a program needn't handle non-finite values.
Results may differ from a plain program's by a relative error of at most 0.0005.
Values may be sent and summed in bfloat16 or wider, within the bound.
No kernel may reach another device: no remote copies, remote signals or barrier semaphores. Data moves between devices by JAX's collectives and lax.ppermute only.
A program may use at most 128 MiB of HBM per device.

v0:
```python
import math

import jax
import jax.numpy as jnp
from jax import lax
from jax.sharding import PartitionSpec as P

SWEEPS = 2


ALPHA = 0.75
SOFTMAX_TEMPER = 0.05
EPSILON = 1e-06


def unitnorm_rows(features):
    wide = features.astype(jnp.float32)
    scale = lax.rsqrt(jnp.mean(wide * wide, axis=1, keepdims=True) + EPSILON)
    return (wide * scale / math.sqrt(wide.shape[1])).astype(jnp.bfloat16)


def on_device(features, class_bias, logits, tile_lists, valid_counts):
    adjusted = logits.astype(jnp.float32) + class_bias[None, :]
    exponentials = jnp.exp(adjusted)
    row_totals = lax.psum(jnp.sum(exponentials, axis=1), "tensor")
    prior = (exponentials / row_totals[:, None]).astype(jnp.bfloat16)
    normalized = unitnorm_rows(features)
    devices = lax.axis_size("dp")
    capacity = max(2, 64 // devices)
    slot_count = devices * capacity
    block_count, tile_count = tile_lists.shape
    block_rows = normalized.shape[0] // block_count
    feature_width = normalized.shape[1]
    owners = tile_lists.reshape(-1)
    requests = owners.shape[0]
    owner_hits = (owners[:, None] == jnp.arange(devices, dtype=jnp.int32)[None, :]).astype(
        jnp.int32
    )
    earlier = jnp.sum((jnp.cumsum(owner_hits, axis=0) - owner_hits) * owner_hits, axis=1)
    position = owners * capacity + earlier
    matches = position[None, :] == jnp.arange(slot_count, dtype=jnp.int32)[:, None]
    filled = jnp.any(matches, axis=1)
    source = jnp.sum(jnp.where(matches, jnp.arange(requests, dtype=jnp.int32)[None, :], 0), axis=1)
    query_blocks = normalized.reshape(block_count, block_rows, feature_width)
    outgoing = jnp.where(
        filled[:, None, None], query_blocks[source // tile_count], jnp.zeros((), jnp.bfloat16)
    )
    outgoing = outgoing.reshape(devices, capacity, block_rows, feature_width)
    arrived = lax.all_to_all(outgoing, "dp", split_axis=0, concat_axis=0, tiled=True)
    affinity_scores = (
        jnp.einsum("scqd,md->scqm", arrived, normalized, preferred_element_type=jnp.float32)
        / SOFTMAX_TEMPER
    )
    columns = jnp.arange(normalized.shape[0], dtype=jnp.int32)
    weights = jnp.where(columns < valid_counts[0], jnp.exp(affinity_scores), 0.0).astype(
        jnp.bfloat16
    )
    tile_sums = jnp.sum(weights.astype(jnp.float32), axis=3)
    returned_sums = lax.all_to_all(tile_sums, "dp", split_axis=0, concat_axis=0, tiled=True)
    picked_sums = returned_sums.reshape(slot_count, block_rows)[position]
    denominator = jnp.sum(picked_sums.reshape(block_count, tile_count, block_rows), axis=1).reshape(
        -1
    )
    prior_float = prior.astype(jnp.float32)
    label_matrix = prior
    spread = prior_float
    for sweep_index in range(SWEEPS):
        partial_sums = jnp.einsum(
            "scqm,mk->scqk", weights, label_matrix, preferred_element_type=jnp.float32
        ).astype(jnp.bfloat16)
        returned = lax.all_to_all(partial_sums, "dp", split_axis=0, concat_axis=0, tiled=True)
        picked = returned.reshape(slot_count, block_rows, -1)[position].astype(jnp.float32)
        numerator = jnp.sum(picked.reshape(block_count, tile_count, block_rows, -1), axis=1)
        numerator = numerator.reshape(denominator.shape[0], -1)
        spread = ALPHA * numerator / denominator[:, None] + (1.0 - ALPHA) * prior_float
        label_matrix = spread.astype(jnp.bfloat16)
    return jnp.log(spread)


def solution(mesh):
    in_specs = (P("dp", None), P("tensor"), P("dp", "tensor"), P("dp", None), P("dp"))
    out_specs = P("dp", "tensor")
    return jax.shard_map(
        on_device, mesh=mesh, in_specs=in_specs, out_specs=out_specs, check_vma=False
    )
```

profile of v0, /device:TPU:6, one launch (start us, length us, event | category | flops | bytes accessed | tf_op | source)
XLA Modules:
  0.0 334.9 jit_solution(8672162783912418541)
XLA Ops:
  0.0 0.0 copy-start.3
  0.0 0.9 copy.10
  0.9 0.1 reshape.143
  1.0 0.1 fusion.12
  1.0 0.1 reduce_window_sum.11
  1.1 0.2 select_reduce_fusion.1
  1.3 0.1 select_reduce_fusion
  1.4 0.1 fusion.11
  1.5 1.6 fusion
  3.2 0.0 copy-done.3
  3.2 0.4 fusion.2
  3.5 0.1 broadcast_in_dim.47
  3.6 3.2 gather_fusion
  6.8 5.2 %broadcast_select_fusion = bf16[32,2,32,1280]{3,2,1,0:T(8,128)(2,1)} fusion(bf16[32,2,32,1280]{3,2,1,0:T(8,128)(2,1)} %bitcast.65, pred[32,2]{1,0:T(8,128)(4,1)S(1)} %broadcast_in_dim.47), kind=kLoop, calls=%fused_computation.4 | loop fusion | flops 2621440 | bytes 10485824 | tf_op jit(solution)/shard_map/jit(_where)/select_n | solution.py:45
  12.1 0.0 copy-start
  12.1 0.0 copy-start.4
  12.1 10.6 %all-to-all-start = ((bf16[32,2,32,1280]{3,2,1,0:T(8,128)(2,1)}), bf16[32,2,32,1280]{3,2,1,0:T(8,128)(2,1)}, u32[]{:S(2)}, u32[]{:S(2)}) async-start(bf16[32,2,32,1280]{3,2,1,0:T(8,128)(2,1)} %broadcast_select_fusion), calls=%async_computation | async-start | bytes 10485760 | tf_op jit(solution)/shard_map/all_to_all | solution.py:49
  23.3 0.0 copy-done
  23.4 0.0 copy-done.4
  23.4 0.3 fusion.7
  23.7 32.9 %psum.7 = f32[512]{0:T(512)S(1)} all-reduce(f32[512]{0:T(512)S(1)} %fusion.7), channel_id=1, replica_groups=mesh['dp'=32,'tensor'=16] {'tensor'}, use_global_device_ids=true, to_apply=%region_6.7 | all-reduce | flops 512 | bytes 4096 | tf_op jit(solution)/shard_map/psum | solution.py:25
  56.6 81.3 %all-to-all-done = bf16[32,2,32,1280]{3,2,1,0:T(8,128)(2,1)} async-done(((bf16[32,2,32,1280]{3,2,1,0:T(8,128)(2,1)}), bf16[32,2,32,1280]{3,2,1,0:T(8,128)(2,1)}, u32[]{:S(2)}, u32[]{:S(2)}) %all-to-all-start) | async-done | bytes 5242912 | tf_op jit(solution)/shard_map/all_to_all | solution.py:49
  137.8 7.4 %convert_reduce_fusion = (f32[32,2,32]{2,1,0:T(2,128)}, bf16[32,2,32,512]{3,2,1,0:T(8,128)(2,1)}) fusion(bf16[32,2,32,1280]{3,2,1,0:T(8,128)(2,1)} %all-to-all-done, bf16[512,1280]{1,0:T(8,128)(2,1)S(1)} %fusion.2, pred[512]{0:T(512)(128)(4,1)S(1)} %iota_compare_fusion.2), kind=kOutput, calls=%fused_computation.5 | convolution fusion | flops 2689595392 | bytes 8659456 | tf_op jit(solution)/shard_map/scqd,md->scqm/dot_general | solution.py:51
  145.2 10.5 %all-to-all-start.2 = ((f32[32,2,32]{2,1,0:T(2,128)}), f32[32,2,32]{2,1,0:T(2,128)S(1)}, u32[]{:S(2)}, u32[]{:S(2)}) async-start(f32[32,2,32]{2,1,0:T(2,128)} %get-tuple-element.5), calls=%async_computation.2 | async-start | bytes 65536 | tf_op jit(solution)/shard_map/all_to_all | solution.py:59
  155.8 5.2 %convolution_convert_fusion.1 = bf16[32,2,32,768]{3,2,1,0:T(8,128)(2,1)} fusion(bf16[32,2,32,512]{3,2,1,0:T(8,128)(2,1)} %get-tuple-element.6, bf16[512,768]{1,0:T(8,128)(2,1)S(1)} %copy-done, f32[512]{0:T(512)S(1)} %psum.7, f32[768]{0:T(1024)S(1)} %copy-done.4), kind=kOutput, calls=%fused_computation.15 | convolution fusion | flops 1613758464 | bytes 6034432 | tf_op jit(solution)/shard_map/scqm,mk->scqk/dot_general | solution.py:68
  160.9 0.0 copy-start.5
  160.9 2.8 all-to-all-done.2
  163.8 7.1 %all-to-all-start.1 = ((bf16[32,2,32,768]{3,2,1,0:T(8,128)(2,1)}), bf16[32,2,32,768]{3,2,1,0:T(8,128)(2,1)S(1)}, u32[]{:S(2)}, u32[]{:S(2)}) async-start(bf16[32,2,32,768]{3,2,1,0:T(8,128)(2,1)} %convolution_convert_fusion.1), calls=%async_computation.1 | async-start | bytes 6291456 | tf_op jit(solution)/shard_map/all_to_all | solution.py:71
  170.9 0.0 copy-done.5
  170.9 0.1 copy.11
  171.0 0.1 mul.62
  171.1 0.6 gather_fusion.2
  171.7 0.1 div.63
  171.8 70.8 %all-to-all-done.1 = bf16[32,2,32,768]{3,2,1,0:T(8,128)(2,1)S(1)} async-done(((bf16[32,2,32,768]{3,2,1,0:T(8,128)(2,1)}), bf16[32,2,32,768]{3,2,1,0:T(8,128)(2,1)S(1)}, u32[]{:S(2)}, u32[]{:S(2)}) %all-to-all-start.1) | async-done | bytes 3145760 | tf_op jit(solution)/shard_map/all_to_all | solution.py:71
  242.6 1.8 gather_fusion.1
  244.4 1.9 convert_reduce_fusion.2
  246.3 0.0 copy-start.1
  246.3 0.1 broadcast_multiply_fusion.1
  246.4 1.0 copy-done.1
  247.4 0.0 copy-start.6
  247.4 0.5 fusion.6
  247.9 1.1 copy-done.6
  249.0 1.8 convolution_convert_fusion
  250.8 77.4 %all_to_all.20 = bf16[32,2,32,768]{3,2,1,0:T(8,128)(2,1)S(1)} all-to-all(bf16[32,2,32,768]{3,2,1,0:T(8,128)(2,1)S(1)} %convolution_convert_fusion), channel_id=1, replica_groups=mesh['dp'=32,'tensor'=16] {'dp'}, dimensions={0} | all-to-all | bytes 6291456 | tf_op jit(solution)/shard_map/all_to_all | solution.py:71
  328.3 1.8 gather_fusion.3
  330.0 1.9 convert_reduce_fusion.1
  331.9 0.0 copy-start.2
  331.9 0.1 broadcast_multiply_fusion
  332.1 1.0 copy-done.2
  333.1 1.8 fusion.4
  (9 shorter events, 0.1 us)
Async XLA Ops:
  0.0 3.2 copy-start.3
  12.1 11.3 %copy-start = (bf16[512,768]{1,0:T(8,128)(2,1)S(1)}, bf16[512,768]{1,0:T(8,128)(2,1)}, u32[]{:S(2)}) copy-start(bf16[512,768]{1,0:T(8,128)(2,1)} %param.7) | copy-start | bytes 2359300
  12.1 11.3 %copy-start.4 = (f32[768]{0:T(1024)S(1)}, f32[768]{0:T(1024)}, u32[]{:S(2)}) copy-start(f32[768]{0:T(1024)} %param.6) | copy-start | bytes 9220
  12.1 125.8 %all-to-all-start = ((bf16[32,2,32,1280]{3,2,1,0:T(8,128)(2,1)}), bf16[32,2,32,1280]{3,2,1,0:T(8,128)(2,1)}, u32[]{:S(2)}, u32[]{:S(2)}) async-start(bf16[32,2,32,1280]{3,2,1,0:T(8,128)(2,1)} %broadcast_select_fusion), calls=%async_computation | async-start | bytes 10485760 | tf_op jit(solution)/shard_map/all_to_all | solution.py:49
  145.2 18.6 %all-to-all-start.2 = ((f32[32,2,32]{2,1,0:T(2,128)}), f32[32,2,32]{2,1,0:T(2,128)S(1)}, u32[]{:S(2)}, u32[]{:S(2)}) async-start(f32[32,2,32]{2,1,0:T(2,128)} %get-tuple-element.5), calls=%async_computation.2 | async-start | bytes 65536 | tf_op jit(solution)/shard_map/all_to_all | solution.py:59
  160.9 9.9 %copy-start.5 = (s32[16,2]{0,1:T(2,128)S(1)}, s32[16,2]{0,1:T(2,128)}, u32[]{:S(2)}) copy-start(s32[16,2]{0,1:T(2,128)} %param.8) | copy-start | bytes 388
  163.8 78.8 %all-to-all-start.1 = ((bf16[32,2,32,768]{3,2,1,0:T(8,128)(2,1)}), bf16[32,2,32,768]{3,2,1,0:T(8,128)(2,1)S(1)}, u32[]{:S(2)}, u32[]{:S(2)}) async-start(bf16[32,2,32,768]{3,2,1,0:T(8,128)(2,1)} %convolution_convert_fusion.1), calls=%async_computation.1 | async-start | bytes 6291456 | tf_op jit(solution)/shard_map/all_to_all | solution.py:71
  246.3 1.1 copy-start.1
  247.4 1.6 copy-start.6
  331.9 1.1 copy-start.2
where the time goes:
time: 338 us; the launch traced here: 335 us
  waiting for transfers between devices  155 us (46%)
  blocking collectives  110 us (33%)
  starting transfers between devices  28.2 us (8%)
  other arithmetic  14.5 us (4%)
  matrix products  14.4 us (4%)
  local copies, waits for them, and re-layouts  11.7 us (3%)
    all_to_all x1, waiting for transfers between devices, on_device(): lax.all_to_all(outgoing, 'dp', split_axis=0, concat_axis=0, tiled=True)  81.3 us
    all_to_all x1, blocking collectives, on_device(): lax.all_to_all(partial_sums, 'dp', split_axis=0, concat_axis=0, tiled=True)  77.4 us
    all_to_all x1, waiting for transfers between devices, on_device(): lax.all_to_all(partial_sums, 'dp', split_axis=0, concat_axis=0, tiled=True)  70.8 us
    psum x1, blocking collectives, on_device(): row_totals = lax.psum(jnp.sum(exponentials, axis=1), 'tensor')  32.9 us
    all_to_all x1, starting transfers between devices, on_device(): lax.all_to_all(outgoing, 'dp', split_axis=0, concat_axis=0, tiled=True)  10.6 us
    all_to_all x1, starting transfers between devices, on_device(): lax.all_to_all(tile_sums, 'dp', split_axis=0, concat_axis=0, tiled=True)  10.5 us
    dot_general x1, matrix products, on_device(): jnp.einsum('scqd,md->scqm', arrived, normalized, preferred_element_type=j...  7.38 us
    all_to_all x1, starting transfers between devices, on_device(): lax.all_to_all(partial_sums, 'dp', split_axis=0, concat_axis=0, tiled=True)  7.08 us
  transfers between devices with their start and end apart: 3, of which 3 were waited for; matrix products, arithmetic and copies ran while one was open for 2% of the time, Pallas kernels for 0%

commit v1 on v0

v1 whole, which is shorter than its diff:
```python
import math

import jax
import jax.numpy as jnp
from jax import lax
from jax.experimental import pallas as pl
from jax.experimental.pallas import tpu as pltpu
from jax.sharding import Mesh
from jax.sharding import PartitionSpec as P

ALPHA = 0.75
SOFTMAX_TEMPER = 0.05
EPSILON = 1e-06

NX, NY, NZ, NC = 4, 8, 8, 2
TILES = NX * NY
TILE = 512
QB = 32
NBLK = 16
NT = 2
PER = NBLK * NT
SLOTS = TILES * 2
SUB = 2
ROWS_C = QB // NC
BF = jnp.bfloat16
F32 = jnp.float32


def unitnorm_rows(features):
    wide = features.astype(F32)
    scale = lax.rsqrt(jnp.mean(wide * wide, axis=-1, keepdims=True) + EPSILON)
    return (wide * scale / math.sqrt(wide.shape[-1])).astype(BF)


def sweep_kernel(index_ref, w_ref, prior_ref, own, after, oppa, oppb, before, out_ref, held, sems):
    y = pl.program_id(0)

    @pl.when(y == 0)
    def _():
        half = NY // 2
        places = (
            (own, 0, NY),
            (after, NY, NY),
            (oppa, 2 * NY, half),
            (oppb, 2 * NY + half, half),
            (before, 3 * NY, NY),
        )
        copies = [
            pltpu.make_async_copy(src, held.at[pl.ds(at, n)], sems.at[i])
            for i, (src, at, n) in enumerate(places)
        ]
        for copy in copies:
            copy.start()
        for copy in copies:
            copy.wait()

    classes = out_ref.shape[1]
    lanes = lax.broadcasted_iota(jnp.int32, (classes, 128), 1) // QB
    for group in range(NBLK // 4):
        total = None
        for k in range(NT):
            weights = jnp.concatenate(
                [
                    w_ref[c, pl.ds((4 * group + b) * ROWS_C, ROWS_C), pl.ds(k * TILE, TILE)]
                    for b in range(4)
                    for c in range(NC)
                ],
                axis=0,
            )
            labels = jnp.concatenate(
                [held[index_ref[y * PER + (4 * group + b) * NT + k]] for b in range(4)], axis=0
            )
            sums = lax.dot_general(
                labels, weights, (((1,), (1,)), ((), ())), preferred_element_type=F32
            )
            total = sums if total is None else total + sums
        picked = total[:classes]
        for b in range(1, 4):
            picked = jnp.where(lanes == b, total[b * classes : (b + 1) * classes], picked)
        at = pl.ds(128 * group, 128)
        prior = prior_ref[0, :, at].astype(F32)
        out_ref[0, :, at] = (picked + (1.0 - ALPHA) * prior).astype(BF)


def sweep(index, weights, prior, pieces):
    ny, classes, rows = prior.shape
    return pl.pallas_call(
        sweep_kernel,
        grid_spec=pltpu.PrefetchScalarGridSpec(
            num_scalar_prefetch=1,
            grid=(ny,),
            in_specs=[
                pl.BlockSpec((NC,) + weights.shape[1:], lambda y, _: (y, 0, 0)),
                pl.BlockSpec((1, classes, rows), lambda y, _: (y, 0, 0)),
            ]
            + [pl.BlockSpec(memory_space=pl.ANY)] * len(pieces),
            out_specs=pl.BlockSpec((1, classes, rows), lambda y, _: (y, 0, 0)),
            scratch_shapes=[
                pltpu.VMEM((TILES, classes, rows), BF),
                pltpu.SemaphoreType.DMA((len(pieces),)),
            ],
        ),
        out_shape=jax.ShapeDtypeStruct(prior.shape, BF),
        compiler_params=pltpu.CompilerParams(vmem_limit_bytes=24 << 20),
        cost_estimate=pl.CostEstimate(
            flops=2 * ny * rows * NT * TILE * classes * 4,
            bytes_accessed=weights.size * 2 + 4 * prior.size * 2,
            transcendentals=0,
        ),
    )(index, weights, prior, *pieces)


def around_x(mine):
    forward = [(i, (i + 1) % NX) for i in range(NX)]
    backward = [(i, (i - 1) % NX) for i in range(NX)]
    before = lax.ppermute(mine, "x", forward)
    after = lax.ppermute(mine, "x", backward)
    half = NY // 2
    oppa = lax.ppermute(before[:half], "x", forward)
    oppb = lax.ppermute(after[half:], "x", backward)
    return mine, after, oppa, oppb, before


def on_device(features, class_bias, logits, tile_lists, valid_counts):
    width = features.shape[1]
    rows, classes = logits.shape
    z, core, x = lax.axis_index("z"), lax.axis_index("c"), lax.axis_index("x")

    owners = tile_lists.reshape(PER)
    order = jnp.arange(PER, dtype=jnp.int32)
    same = (owners[:, None] == owners[None, :]) & (order[None, :] < order[:, None])
    position = owners * 2 + jnp.sum(same.astype(jnp.int32), axis=1)
    hits = position.reshape(NBLK, NT)[:, :, None] == jnp.arange(SLOTS, dtype=jnp.int32)
    hits = hits.astype(BF)

    row = core * ROWS_C + z * SUB
    mine = lax.dynamic_slice_in_dim(features.reshape(NBLK, QB, width), row, SUB, axis=1)
    outgoing = jnp.einsum(
        "bs,bf->sf",
        hits.sum(axis=1),
        mine.reshape(NBLK, SUB * width),
        preferred_element_type=F32,
    ).astype(BF)
    arrived = lax.all_to_all(
        outgoing.reshape(TILES, 2 * SUB, width), ("x", "y"), 0, 0, tiled=True
    )

    adjusted = logits.astype(F32) + class_bias[None, :]
    part = jnp.sum(jnp.exp(adjusted), axis=1)
    parts = lax.all_to_all(
        jnp.broadcast_to(part, (NZ * NC, rows)), ("z", "c"), 0, 0, tiled=True
    )
    totals = jnp.sum(parts, axis=0)
    prior = (jnp.exp(adjusted) / totals[:, None]).astype(BF)
    prior = prior.T.reshape(NY, classes // NY, rows)
    prior = lax.all_to_all(prior, "y", 0, 0, tiled=True)

    memory = unitnorm_rows(features)
    queries = unitnorm_rows(arrived.reshape(SLOTS * SUB, width))
    scores = lax.dot_general(
        queries, memory, (((1,), (1,)), ((), ())), preferred_element_type=F32
    ) / SOFTMAX_TEMPER
    columns = jnp.arange(TILE, dtype=jnp.int32)
    scored = jnp.where(columns < valid_counts[0], jnp.exp(scores), 0.0).astype(BF)
    back = lax.all_to_all(
        scored.reshape(TILES, 2 * SUB, TILE), ("x", "y"), 0, 0, tiled=True
    ).reshape(SLOTS, SUB * TILE)
    chosen = jnp.einsum("bks,sf->bkf", hits, back, preferred_element_type=F32)
    chosen = chosen.reshape(NBLK, NT, SUB, TILE)
    denominator = jnp.sum(chosen, axis=(1, 3), keepdims=True)
    scaled = (ALPHA * chosen / denominator).astype(BF)
    scaled = scaled.transpose(0, 2, 1, 3).reshape(NBLK, SUB, NT * TILE)

    over_z = lax.all_to_all(
        jnp.broadcast_to(scaled, (NZ,) + scaled.shape), "z", 0, 0, tiled=True
    )
    over_z = over_z.transpose(1, 0, 2, 3).reshape(NBLK * ROWS_C, NT * TILE)
    names = jnp.zeros((16, NT * TILE), BF).at[0, :PER].set(owners.astype(BF))
    piece = jnp.concatenate([over_z, names], axis=0)
    weights = lax.all_gather(piece, ("y", "c"), axis=0, tiled=False)

    named = weights[::NC, NBLK * ROWS_C, :PER].astype(jnp.int32)
    index = ((named // NY - x) % NX) * NY + named % NY
    index = index.reshape(NY * PER)

    labels = sweep(index, weights, prior, around_x(prior))
    spread = sweep(index, weights, prior, around_x(labels))
    spread = lax.all_to_all(spread, "y", 0, 0, tiled=True)
    return jnp.log(spread.reshape(classes, rows).T.astype(F32))


def solution(mesh):
    split = Mesh(mesh.devices.reshape(NX, NY, NZ, NC), ("x", "y", "z", "c"))
    dp, tensor = ("x", "y"), ("z", "c")
    in_specs = (P(dp, None), P(tensor), P(dp, tensor), P(dp, None), P(dp))
    return jax.shard_map(
        on_device, mesh=split, in_specs=in_specs, out_specs=P(dp, tensor), check_vma=False
    )
```

time: 338 us -> 249 us (0.74)
  waiting for transfers between devices: 155 us -> 71.2 us
  blocking collectives: 110 us -> 81.5 us
  Pallas kernels: 0 us -> 18.1 us
  starting transfers between devices: 28.2 us -> 45.4 us
  between operations: 0.85 us -> 14.3 us
  matrix products: 14.4 us -> 1.22 us
  other arithmetic: 14.5 us -> 4.24 us
    all_to_all x3 -> x2, waiting for transfers between devices: 155 us -> 25.7 us  [the longest x1 15 us: on_device(): lax.all_to_all(jnp.broadcast_to(scaled, (NZ,) + scaled.shape), 'z', 0, 0,...]
    ppermute x0 -> x8, waiting for transfers between devices: none -> 45.5 us  [the longest x2 27.3 us: around_x(): before = lax.ppermute(mine, 'x', forward)]
    psum x1 -> x0, blocking collectives: 32.9 us -> none  [on_device(): row_totals = lax.psum(jnp.sum(exponentials, axis=1), 'tensor')]
    ppermute x0 -> x8, starting transfers between devices: none -> 24.8 us  [the longest x2 8.7 us: around_x(): oppa = lax.ppermute(before[:half], 'x', forward)]
    pallas_call x0 -> x2, Pallas kernels: none -> 18.1 us  [sweep(): pl.pallas_call(sweep_kernel, grid_spec=pltpu.PrefetchScalarGridSpec(num_s...]
    dot_general x3, matrix products: 14.4 us -> 1.22 us  [the longest x1 0.67 us: on_device(): lax.dot_general(queries, memory, (((1,), (1,)), ((), ())), preferred_elem...]
    all_to_all x3 -> x2, starting transfers between devices: 28.2 us -> 20.6 us  [the longest x1 10.3 us: on_device(): lax.all_to_all(jnp.broadcast_to(scaled, (NZ,) + scaled.shape), 'z', 0, 0,...]
    gather x4 -> x0, local copies, waits for them, and re-layouts: 7.35 us -> none  [the longest x2 3.58 us: on_device(): returned.reshape(slot_count, block_rows, -1)[position].astype(jnp.float32)]
  transfers between devices with their start and end apart: 3 -> 11, of which waited for: 3 -> 8; matrix products, arithmetic and copies ran while one was open for 2% -> 1% of each run, Pallas kernels for 0% -> 0%
where the time goes in v1:
time: 249 us; the launch traced here: 248 us
  blocking collectives  81.5 us (33%)
  waiting for transfers between devices  71.2 us (29%)
  starting transfers between devices  45.4 us (18%)
  Pallas kernels  18.1 us (7%)
  between operations  14.3 us (6%)
  local copies, waits for them, and re-layouts  11.9 us (5%)
  other arithmetic  4.24 us (2%)
    all_to_all x1, blocking collectives, on_device(): prior = lax.all_to_all(prior, 'y', 0, 0, tiled=True)  34.9 us
    ppermute x2, waiting for transfers between devices, around_x(): before = lax.ppermute(mine, 'x', forward)  27.3 us
    all_to_all x1, blocking collectives, on_device(): spread = lax.all_to_all(spread, 'y', 0, 0, tiled=True)  21.4 us
    pallas_call x2, Pallas kernels, sweep(): pl.pallas_call(sweep_kernel, grid_spec=pltpu.PrefetchScalarGridSpec(num_s...  18.1 us
    all_to_all x1, waiting for transfers between devices, on_device(): lax.all_to_all(jnp.broadcast_to(scaled, (NZ,) + scaled.shape), 'z', 0, 0,...  15 us
    all_to_all x1, blocking collectives, on_device(): lax.all_to_all(scored.reshape(TILES, 2 * SUB, TILE), ('x', 'y'), 0, 0, ti...  14.9 us
    ppermute x2, waiting for transfers between devices, around_x(): oppb = lax.ppermute(after[half:], 'x', backward)  11 us
    all_to_all x1, waiting for transfers between devices, on_device(): lax.all_to_all(outgoing.reshape(TILES, 2 * SUB, width), ('x', 'y'), 0, 0,...  10.7 us
  transfers between devices with their start and end apart: 11, of which 8 were waited for; matrix products, arithmetic and copies ran while one was open for 1% of the time, Pallas kernels for 0%

profile of v1, /device:TPU:6, one launch (start us, length us, event | category | flops | bytes accessed | tf_op | source)
XLA Modules:
  0.0 247.8 jit_solution(14747323175835324830)
XLA Ops:
  6.5 0.9 copy.67
  7.4 0.1 eq.31
  7.5 0.2 convert_reduce_fusion
  7.7 0.1 reduce_sum.69
  7.7 0.1 copy.68
  7.8 0.8 multiply_add_fusion
  8.6 0.1 fusion.32
  8.7 1.1 constant_dynamic-slice_fusion
  9.8 0.3 convolution_convert_fusion
  10.0 0.9 reshape.115
  11.0 10.2 %all-to-all-start = ((bf16[32,4,1280]{2,1,0:T(4,128)(2,1)}), bf16[32,4,1280]{2,1,0:T(4,128)(2,1)S(1)}, u32[]{:S(2)}, u32[]{:S(2)}) async-start(bf16[32,4,1280]{2,1,0:T(4,128)(2,1)} %reshape.115), calls=%async_computation | async-start | bytes 655360 | tf_op jit(solution)/shard_map/all_to_all | solution.py:144
  21.9 0.3 fusion
  22.2 10.7 %all-to-all-done = bf16[32,4,1280]{2,1,0:T(4,128)(2,1)S(1)} async-done(((bf16[32,4,1280]{2,1,0:T(4,128)(2,1)}), bf16[32,4,1280]{2,1,0:T(4,128)(2,1)S(1)}, u32[]{:S(2)}, u32[]{:S(2)}) %all-to-all-start) | async-done | bytes 327712 | tf_op jit(solution)/shard_map/all_to_all | solution.py:144
  32.9 0.2 multiply_reduce_fusion
  33.2 0.1 rsqrt.20
  33.3 0.7 fusion.17
  34.0 14.9 %all_to_all.31 = bf16[32,4,512]{2,1,0:T(4,128)(2,1)S(1)} all-to-all(bf16[32,4,512]{2,1,0:T(4,128)(2,1)S(1)} %reshape.116), channel_id=1, replica_groups=mesh['x'=4,'y'=8,'z'=8,'c'=2] {'x','y'}, dimensions={0} | all-to-all | bytes 262144 | tf_op jit(solution)/shard_map/all_to_all | solution.py:165
  48.9 0.1 reshape.117
  49.0 0.3 fusion.38
  49.3 0.1 fusion.27
  49.4 0.1 copy.78
  49.5 1.1 broadcast_in_dim.14
  50.6 10.3 %all-to-all-start.2 = ((bf16[8,16,2,1024]{3,2,1,0:T(2,128)(2,1)}), bf16[8,16,2,1024]{3,2,1,0:T(2,128)(2,1)S(1)}, u32[]{:S(2)}, u32[]{:S(2)}) async-start(bf16[8,16,2,1024]{3,2,1,0:T(2,128)(2,1)} %broadcast_in_dim.14), calls=%async_computation.2 | async-start | bytes 1048576 | tf_op jit(solution)/shard_map/all_to_all | solution.py:174
  60.9 0.0 all-gather.3.cloned.1.call-start
  61.0 0.1 copy.73
  61.1 0.1 convert_element_type.81
  61.2 15.0 %all-to-all-done.2 = bf16[8,16,2,1024]{3,2,1,0:T(2,128)(2,1)S(1)} async-done(((bf16[8,16,2,1024]{3,2,1,0:T(2,128)(2,1)}), bf16[8,16,2,1024]{3,2,1,0:T(2,128)(2,1)S(1)}, u32[]{:S(2)}, u32[]{:S(2)}) %all-to-all-start.2) | async-done | bytes 524320 | tf_op jit(solution)/shard_map/all_to_all | solution.py:174
  76.2 0.5 copy.72
  76.6 0.0 copy-start.1
  76.7 0.0 copy-start.3
  76.7 0.2 reshape.119
  76.9 0.8 fusion.22
  77.7 0.0 all-gather.3.cloned.1.call-update
  77.7 0.0 copy-done.1
  77.8 0.3 fusion.3
  78.1 10.3 %all_to_all.32 = f32[16,1,512]{2,1,0:T(1,128)S(1)} all-to-all(f32[16,1,512]{2,1,0:T(1,128)S(1)} %broadcast_in_dim.26), channel_id=1, replica_groups=mesh['x'=4,'y'=8,'z'=8,'c'=2] {'z','c'}, dimensions={0} | all-to-all | bytes 65536 | tf_op jit(solution)/shard_map/all_to_all | solution.py:150
  88.4 0.3 fusion.21
  88.8 0.3 copy.75
  89.0 34.9 %all_to_all.33.prior_ref.own = bf16[8,96,512]{2,1,0:T(8,128)(2,1)S(1)} all-to-all(bf16[8,96,512]{2,1,0:T(8,128)(2,1)S(1)} %bitcast.39), channel_id=1, replica_groups=mesh['x'=4,'y'=8,'z'=8,'c'=2] {'y'}, dimensions={0} | all-to-all | bytes 1572864 | tf_op jit(solution)/shard_map/all_to_all | solution.py:156
  123.9 4.0 %collective-permute-start.1 = (bf16[8,96,512]{2,1,0:T(8,128)(2,1)S(1)}, bf16[8,96,512]{2,1,0:T(8,128)(2,1)S(1)}, u32[]{:S(2)}, u32[]{:S(2)}) collective-permute-start(bf16[8,96,512]{2,1,0:T(8,128)(2,1)S(1)} %all_to_all.33.prior_ref.own), channel_id=1, source_target_pairs={{0,128},{128,256},{256,384},{384,0},{1,129},{129,257},{257,385},{3... | collective-permute-start | bytes 2359304 | tf_op jit(solution)/shard_map/ppermute | solution.py:116
  127.9 1.9 collective-permute-start
  129.8 14.6 %collective-permute-done.1.before = bf16[8,96,512]{2,1,0:T(8,128)(2,1)S(1)} collective-permute-done((bf16[8,96,512]{2,1,0:T(8,128)(2,1)S(1)}, bf16[8,96,512]{2,1,0:T(8,128)(2,1)S(1)}, u32[]{:S(2)}, u32[]{:S(2)}) %collective-permute-start.1) | collective-permute-done | bytes 786464 | tf_op jit(solution)/shard_map/ppermute | solution.py:116
  144.5 5.3 %collective-permute-start.2 = (bf16[4,96,512]{2,1,0:T(8,128)(2,1)S(1)}, bf16[4,96,512]{2,1,0:T(8,128)(2,1)S(1)}, u32[]{:S(2)}, u32[]{:S(2)}) collective-permute-start(bf16[4,96,512]{2,1,0:T(8,128)(2,1)S(1)} %slice.36), channel_id=1, source_target_pairs={{0,128},{128,256},{256,384},{384,0},{1,129},{129,257},{257,385},{3... | collective-permute-start | bytes 1179656 | tf_op jit(solution)/shard_map/ppermute | solution.py:119
  149.8 0.8 slice.37
  150.6 1.9 collective-permute-start.3
  152.5 0.0 all-gather.3.cloned.1.call-done
  152.6 0.7 convert_reduce_fusion.1
  153.3 0.1 reshape.122
  153.4 3.3 %collective-permute-done.2.oppa = bf16[4,96,512]{2,1,0:T(8,128)(2,1)S(1)} collective-permute-done((bf16[4,96,512]{2,1,0:T(8,128)(2,1)S(1)}, bf16[4,96,512]{2,1,0:T(8,128)(2,1)S(1)}, u32[]{:S(2)}, u32[]{:S(2)}) %collective-permute-start.2) | collective-permute-done | bytes 393248 | tf_op jit(solution)/shard_map/ppermute | solution.py:119
  156.7 6.4 %collective-permute-done.3.oppb = bf16[4,96,512]{2,1,0:T(8,128)(2,1)S(1)} collective-permute-done((bf16[4,96,512]{2,1,0:T(8,128)(2,1)}, bf16[4,96,512]{2,1,0:T(8,128)(2,1)S(1)}, u32[]{:S(2)}, u32[]{:S(2)}) %collective-permute-start.3) | collective-permute-done | bytes 393248 | tf_op jit(solution)/shard_map/ppermute | solution.py:120
  163.1 3.5 %copy-done = bf16[4352,1024]{1,0:T(8,128)(2,1)S(1)} copy-done((bf16[4352,1024]{1,0:T(8,128)(2,1)S(1)}, bf16[4352,1024]{1,0:T(8,128)(2,1)}, u32[]{:S(2)}) %copy-start) | copy-done | bytes 8912920
  166.6 9.0 %shard_map.55.own = bf16[8,96,512]{2,1,0:T(8,128)(2,1)S(1)} custom-call(s32[256]{0:T(256)S(1)} %fusion.35.index_ref, bf16[16,272,1024]{2,1,0:T(8,128)(2,1)S(1)} %bitcast.36, bf16[8,96,512]{2,1,0:T(8,128)(2,1)S(1)} %all_to_all.33.prior_ref.own, bf16[8,96,512]{2,1,0:T(8,128)(2,1)S(1)} %all_to_all.33.prior_ref.own, ...), custom_call_target="tpu_custom_call" | custom-call | flops 3221225472 | bytes 12058624 | tf_op jit(solution)/shard_map/pallas_call | solution.py:87
  175.7 1.9 collective-permute-start.5
  177.6 3.9 %collective-permute-start.4 = (bf16[8,96,512]{2,1,0:T(8,128)(2,1)S(1)}, bf16[8,96,512]{2,1,0:T(8,128)(2,1)S(1)}, u32[]{:S(2)}, u32[]{:S(2)}) collective-permute-start(bf16[8,96,512]{2,1,0:T(8,128)(2,1)S(1)} %shard_map.55.own), channel_id=1, source_target_pairs={{0,384},{128,0},{256,128},{384,256},{1,385},{129,1},{257,129},{385... | collective-permute-start | bytes 2359304 | tf_op jit(solution)/shard_map/ppermute | solution.py:117
  181.5 12.7 %collective-permute-done.5.before = bf16[8,96,512]{2,1,0:T(8,128)(2,1)S(1)} collective-permute-done((bf16[8,96,512]{2,1,0:T(8,128)(2,1)S(1)}, bf16[8,96,512]{2,1,0:T(8,128)(2,1)S(1)}, u32[]{:S(2)}, u32[]{:S(2)}) %collective-permute-start.5) | collective-permute-done | bytes 786464 | tf_op jit(solution)/shard_map/ppermute | solution.py:116
  194.3 3.4 %collective-permute-start.6 = (bf16[4,96,512]{2,1,0:T(8,128)(2,1)S(1)}, bf16[4,96,512]{2,1,0:T(8,128)(2,1)S(1)}, u32[]{:S(2)}, u32[]{:S(2)}) collective-permute-start(bf16[4,96,512]{2,1,0:T(8,128)(2,1)S(1)} %slice.38), channel_id=1, source_target_pairs={{0,128},{128,256},{256,384},{384,0},{1,129},{129,257},{257,385},{3... | collective-permute-start | bytes 1179656 | tf_op jit(solution)/shard_map/ppermute | solution.py:119
  197.7 0.0 collective-permute-done.4.after
  197.7 2.4 collective-permute-start.7
  200.2 3.8 %collective-permute-done.6.oppa = bf16[4,96,512]{2,1,0:T(8,128)(2,1)S(1)} collective-permute-done((bf16[4,96,512]{2,1,0:T(8,128)(2,1)S(1)}, bf16[4,96,512]{2,1,0:T(8,128)(2,1)S(1)}, u32[]{:S(2)}, u32[]{:S(2)}) %collective-permute-start.6) | collective-permute-done | bytes 393248 | tf_op jit(solution)/shard_map/ppermute | solution.py:119
  204.0 4.7 %collective-permute-done.7.oppb = bf16[4,96,512]{2,1,0:T(8,128)(2,1)S(1)} collective-permute-done((bf16[4,96,512]{2,1,0:T(8,128)(2,1)S(1)}, bf16[4,96,512]{2,1,0:T(8,128)(2,1)S(1)}, u32[]{:S(2)}, u32[]{:S(2)}) %collective-permute-start.7) | collective-permute-done | bytes 393248 | tf_op jit(solution)/shard_map/ppermute | solution.py:120
  208.6 9.0 %shard_map.56 = bf16[8,96,512]{2,1,0:T(8,128)(2,1)S(1)} custom-call(s32[256]{0:T(256)S(1)} %fusion.35.index_ref, bf16[16,272,1024]{2,1,0:T(8,128)(2,1)S(1)} %bitcast.37, bf16[8,96,512]{2,1,0:T(8,128)(2,1)S(1)} %all_to_all.33.prior_ref.own, bf16[8,96,512]{2,1,0:T(8,128)(2,1)S(1)} %shard_map.55.own, bf16[8,96,512]{2,1,0:T(8,128)(2,1)S(1)} %collective-permute-done.4.after, ...), custom_call_target="tpu_custom_call" | custom-call | flops 3221225472 | bytes 12058624 | tf_op jit(solution)/shard_map/pallas_call | solution.py:87
  217.7 21.4 %all_to_all.34 = bf16[8,96,512]{2,1,0:T(8,128)(2,1)S(1)} all-to-all(bf16[8,96,512]{2,1,0:T(8,128)(2,1)S(1)} %shard_map.56), channel_id=1, replica_groups=mesh['x'=4,'y'=8,'z'=8,'c'=2] {'y'}, dimensions={0} | all-to-all | bytes 1572864 | tf_op jit(solution)/shard_map/all_to_all | solution.py:188
  239.1 0.2 convert_log_fusion
  239.3 1.6 copy.76
  (18 shorter events, 0.3 us)
Async XLA Ops:
  6.5 15.3 %copy-start.2 = (bf16[512,1280]{1,0:T(8,128)(2,1)S(1)}, bf16[512,1280]{1,0:T(8,128)(2,1)}, u32[]{:S(2)}) copy-start(bf16[512,1280]{1,0:T(8,128)(2,1)} %param.7) | copy-start | bytes 3932164
  11.0 21.9 %all-to-all-start = ((bf16[32,4,1280]{2,1,0:T(4,128)(2,1)}), bf16[32,4,1280]{2,1,0:T(4,128)(2,1)S(1)}, u32[]{:S(2)}, u32[]{:S(2)}) async-start(bf16[32,4,1280]{2,1,0:T(4,128)(2,1)} %reshape.115), calls=%async_computation | async-start | bytes 655360 | tf_op jit(solution)/shard_map/all_to_all | solution.py:144
  50.6 25.6 %all-to-all-start.2 = ((bf16[8,16,2,1024]{3,2,1,0:T(2,128)(2,1)}), bf16[8,16,2,1024]{3,2,1,0:T(2,128)(2,1)S(1)}, u32[]{:S(2)}, u32[]{:S(2)}) async-start(bf16[8,16,2,1024]{3,2,1,0:T(2,128)(2,1)} %broadcast_in_dim.14), calls=%async_computation.2 | async-start | bytes 1048576 | tf_op jit(solution)/shard_map/all_to_all | solution.py:174
  60.9 91.6 %all-gather.3.cloned.1.call-start = ((), (), s32[]{:S(2)}) async-start(), calls=%async_computation.6 | async-start | bytes 9469952 | tf_op jit(solution)/shard_map/all_gather | solution.py:180
  76.6 1.1 copy-start.1
  76.7 1.1 copy-start.3
  123.9 20.5 %collective-permute-start.1 = (bf16[8,96,512]{2,1,0:T(8,128)(2,1)S(1)}, bf16[8,96,512]{2,1,0:T(8,128)(2,1)S(1)}, u32[]{:S(2)}, u32[]{:S(2)}) collective-permute-start(bf16[8,96,512]{2,1,0:T(8,128)(2,1)S(1)} %all_to_all.33.prior_ref.own), channel_id=1, source_target_pairs={{0,128},{128,256},{256,384},{384,0},{1,129},{129,257},{257,385},{3... | collective-permute-start | bytes 2359304 | tf_op jit(solution)/shard_map/ppermute | solution.py:116
  127.9 21.9 %collective-permute-start = (bf16[8,96,512]{2,1,0:T(8,128)(2,1)S(1)}, bf16[8,96,512]{2,1,0:T(8,128)(2,1)S(1)}, u32[]{:S(2)}, u32[]{:S(2)}) collective-permute-start(bf16[8,96,512]{2,1,0:T(8,128)(2,1)S(1)} %all_to_all.33.prior_ref.own), channel_id=1, source_target_pairs={{0,384},{128,0},{256,128},{384,256},{1,385},{129,1},{257,129},{385... | collective-permute-start | bytes 2359304 | tf_op jit(solution)/shard_map/ppermute | solution.py:117
  144.5 12.3 %collective-permute-start.2 = (bf16[4,96,512]{2,1,0:T(8,128)(2,1)S(1)}, bf16[4,96,512]{2,1,0:T(8,128)(2,1)S(1)}, u32[]{:S(2)}, u32[]{:S(2)}) collective-permute-start(bf16[4,96,512]{2,1,0:T(8,128)(2,1)S(1)} %slice.36), channel_id=1, source_target_pairs={{0,128},{128,256},{256,384},{384,0},{1,129},{129,257},{257,385},{3... | collective-permute-start | bytes 1179656 | tf_op jit(solution)/shard_map/ppermute | solution.py:119
  150.6 12.5 %collective-permute-start.3 = (bf16[4,96,512]{2,1,0:T(8,128)(2,1)}, bf16[4,96,512]{2,1,0:T(8,128)(2,1)S(1)}, u32[]{:S(2)}, u32[]{:S(2)}) collective-permute-start(bf16[4,96,512]{2,1,0:T(8,128)(2,1)} %slice.37), channel_id=1, source_target_pairs={{0,384},{128,0},{256,128},{384,256},{1,385},{129,1},{257,129},{385... | collective-permute-start | bytes 1179656 | tf_op jit(solution)/shard_map/ppermute | solution.py:120
  163.1 3.5 %copy-start = (bf16[4352,1024]{1,0:T(8,128)(2,1)S(1)}, bf16[4352,1024]{1,0:T(8,128)(2,1)}, u32[]{:S(2)}) copy-start(bf16[4352,1024]{1,0:T(8,128)(2,1)} %all-gather.3.cloned.1.call-done) | copy-start | bytes 26738692
  175.7 18.6 %collective-permute-start.5 = (bf16[8,96,512]{2,1,0:T(8,128)(2,1)S(1)}, bf16[8,96,512]{2,1,0:T(8,128)(2,1)S(1)}, u32[]{:S(2)}, u32[]{:S(2)}) collective-permute-start(bf16[8,96,512]{2,1,0:T(8,128)(2,1)S(1)} %shard_map.55.own), channel_id=1, source_target_pairs={{0,128},{128,256},{256,384},{384,0},{1,129},{129,257},{257,385},{3... | collective-permute-start | bytes 2359304 | tf_op jit(solution)/shard_map/ppermute | solution.py:116
  177.6 20.1 %collective-permute-start.4 = (bf16[8,96,512]{2,1,0:T(8,128)(2,1)S(1)}, bf16[8,96,512]{2,1,0:T(8,128)(2,1)S(1)}, u32[]{:S(2)}, u32[]{:S(2)}) collective-permute-start(bf16[8,96,512]{2,1,0:T(8,128)(2,1)S(1)} %shard_map.55.own), channel_id=1, source_target_pairs={{0,384},{128,0},{256,128},{384,256},{1,385},{129,1},{257,129},{385... | collective-permute-start | bytes 2359304 | tf_op jit(solution)/shard_map/ppermute | solution.py:117
  194.3 9.7 %collective-permute-start.6 = (bf16[4,96,512]{2,1,0:T(8,128)(2,1)S(1)}, bf16[4,96,512]{2,1,0:T(8,128)(2,1)S(1)}, u32[]{:S(2)}, u32[]{:S(2)}) collective-permute-start(bf16[4,96,512]{2,1,0:T(8,128)(2,1)S(1)} %slice.38), channel_id=1, source_target_pairs={{0,128},{128,256},{256,384},{384,0},{1,129},{129,257},{257,385},{3... | collective-permute-start | bytes 1179656 | tf_op jit(solution)/shard_map/ppermute | solution.py:119
  197.7 10.9 %collective-permute-start.7 = (bf16[4,96,512]{2,1,0:T(8,128)(2,1)S(1)}, bf16[4,96,512]{2,1,0:T(8,128)(2,1)S(1)}, u32[]{:S(2)}, u32[]{:S(2)}) collective-permute-start(bf16[4,96,512]{2,1,0:T(8,128)(2,1)S(1)} %slice.39), channel_id=1, source_target_pairs={{0,384},{128,0},{256,128},{384,256},{1,385},{129,1},{257,129},{385... | collective-permute-start | bytes 1179656 | tf_op jit(solution)/shard_map/ppermute | solution.py:120
Sparse Core Ops, SparseCore 0:
  77.9 69.2 all-gather.2

commit v2 on v1

--- a/solution.py
+++ b/solution.py
@@ -32,7 +32,7 @@
     return (wide * scale / math.sqrt(wide.shape[-1])).astype(BF)
 
 
-def sweep_kernel(index_ref, w_ref, prior_ref, own, after, oppa, oppb, before, out_ref, held, sems):
+def sweep_kernel(index_ref, me_ref, w_ref, prior_ref, own, after, oppa, oppb, before, out_ref, held, sems):
     y = pl.program_id(0)
 
     @pl.when(y == 0)
@@ -82,19 +82,19 @@
         out_ref[0, :, at] = (picked + (1.0 - ALPHA) * prior).astype(BF)
 
 
-def sweep(index, weights, prior, pieces):
+def sweep(index, me, weights, prior, pieces):
     ny, classes, rows = prior.shape
     return pl.pallas_call(
         sweep_kernel,
         grid_spec=pltpu.PrefetchScalarGridSpec(
-            num_scalar_prefetch=1,
+            num_scalar_prefetch=2,
             grid=(ny,),
             in_specs=[
-                pl.BlockSpec((NC,) + weights.shape[1:], lambda y, _: (y, 0, 0)),
-                pl.BlockSpec((1, classes, rows), lambda y, _: (y, 0, 0)),
+                pl.BlockSpec((NC,) + weights.shape[1:], lambda y, _, me: (y, 0, 0)),
+                pl.BlockSpec((1, classes, rows), lambda y, _, me: ((me[0] - y + NY) % NY, 0, 0)),
             ]
             + [pl.BlockSpec(memory_space=pl.ANY)] * len(pieces),
-            out_specs=pl.BlockSpec((1, classes, rows), lambda y, _: (y, 0, 0)),
+            out_specs=pl.BlockSpec((1, classes, rows), lambda y, _, me: (y, 0, 0)),
             scratch_shapes=[
                 pltpu.VMEM((TILES, classes, rows), BF),
                 pltpu.SemaphoreType.DMA((len(pieces),)),
@@ -107,7 +107,7 @@
             bytes_accessed=weights.size * 2 + 4 * prior.size * 2,
             transcendentals=0,
         ),
-    )(index, weights, prior, *pieces)
+    )(index, me, weights, prior, *pieces)
 
 
 def around_x(mine):
@@ -121,10 +121,30 @@
     return mine, after, oppa, oppb, before
 
 
+def over_y(pieces):
+    y = lax.axis_index("y")
+    turned = lax.dynamic_slice_in_dim(jnp.concatenate([pieces, pieces]), y, NY, axis=0)
+    got = [turned[0]]
+    for d in range(1, NY):
+        got.append(lax.ppermute(turned[d], "y", [(i, (i + d) % NY) for i in range(NY)]))
+    return jnp.stack(got)
+
+
+def turned_totals(totals):
+    x, y = lax.axis_index("x"), lax.axis_index("y")
+    grid = totals.reshape(NX, NY, -1)
+    grid = lax.dynamic_slice_in_dim(jnp.concatenate([grid, grid], axis=0), x, NX, axis=0)
+    grid = jnp.flip(grid, axis=1)
+    return lax.dynamic_slice_in_dim(
+        jnp.concatenate([grid, grid], axis=1), NY - 1 - y, NY, axis=1
+    )
+
+
 def on_device(features, class_bias, logits, tile_lists, valid_counts):
     width = features.shape[1]
     rows, classes = logits.shape
-    z, core, x = lax.axis_index("z"), lax.axis_index("c"), lax.axis_index("x")
+    x, y = lax.axis_index("x"), lax.axis_index("y")
+    z, core = lax.axis_index("z"), lax.axis_index("c")
 
     owners = tile_lists.reshape(PER)
     order = jnp.arange(PER, dtype=jnp.int32)
@@ -141,19 +161,12 @@
         mine.reshape(NBLK, SUB * width),
         preferred_element_type=F32,
     ).astype(BF)
+    outgoing, raw = lax.optimization_barrier((outgoing, logits))
     arrived = lax.all_to_all(
         outgoing.reshape(TILES, 2 * SUB, width), ("x", "y"), 0, 0, tiled=True
     )
 
-    adjusted = logits.astype(F32) + class_bias[None, :]
-    part = jnp.sum(jnp.exp(adjusted), axis=1)
-    parts = lax.all_to_all(
-        jnp.broadcast_to(part, (NZ * NC, rows)), ("z", "c"), 0, 0, tiled=True
-    )
-    totals = jnp.sum(parts, axis=0)
-    prior = (jnp.exp(adjusted) / totals[:, None]).astype(BF)
-    prior = prior.T.reshape(NY, classes // NY, rows)
-    prior = lax.all_to_all(prior, "y", 0, 0, tiled=True)
+    raw = over_y(raw.T.reshape(NY, classes // NY, rows))
 
     memory = unitnorm_rows(features)
     queries = unitnorm_rows(arrived.reshape(SLOTS * SUB, width))
@@ -162,6 +175,8 @@
     ) / SOFTMAX_TEMPER
     columns = jnp.arange(TILE, dtype=jnp.int32)
     scored = jnp.where(columns < valid_counts[0], jnp.exp(scores), 0.0).astype(BF)
+    scored, raw = lax.optimization_barrier((scored, raw))
+    raw = around_x(raw)
     back = lax.all_to_all(
         scored.reshape(TILES, 2 * SUB, TILE), ("x", "y"), 0, 0, tiled=True
     ).reshape(SLOTS, SUB * TILE)
@@ -174,17 +189,39 @@
     over_z = lax.all_to_all(
         jnp.broadcast_to(scaled, (NZ,) + scaled.shape), "z", 0, 0, tiled=True
     )
+    over_z, after, before = lax.optimization_barrier((over_z, raw[1], raw[4]))
+    raw = raw[0], after, raw[2], raw[3], before
     over_z = over_z.transpose(1, 0, 2, 3).reshape(NBLK * ROWS_C, NT * TILE)
     names = jnp.zeros((16, NT * TILE), BF).at[0, :PER].set(owners.astype(BF))
     piece = jnp.concatenate([over_z, names], axis=0)
     weights = lax.all_gather(piece, ("y", "c"), axis=0, tiled=False)
 
-    named = weights[::NC, NBLK * ROWS_C, :PER].astype(jnp.int32)
-    index = ((named // NY - x) % NX) * NY + named % NY
-    index = index.reshape(NY * PER)
-
-    labels = sweep(index, weights, prior, around_x(prior))
-    spread = sweep(index, weights, prior, around_x(labels))
+    adjusted = logits.astype(F32) + class_bias[None, :]
+    part = jnp.sum(jnp.exp(adjusted), axis=1)
+    part, _ = lax.optimization_barrier((part, piece))
+    parts = lax.all_to_all(
+        jnp.broadcast_to(part, (NZ * NC, rows)), ("z", "c"), 0, 0, tiled=True
+    )
+    totals = jnp.sum(parts, axis=0)
+    totals = lax.all_to_all(
+        jnp.broadcast_to(totals, (TILES, rows)), ("x", "y"), 0, 0, tiled=True
+    )
+    totals = turned_totals(totals)
+
+    bias = lax.dynamic_slice_in_dim(class_bias.reshape(NY, classes // NY), y, 1, axis=0)
+    bias = bias.reshape(1, classes // NY, 1)
+    half = NY // 2
+    sums = totals[0], totals[1], totals[2, :half], totals[2, half:], totals[3]
+    priors = tuple(
+        (jnp.exp(r.astype(F32) + bias) / t[:, None, :]).astype(BF) for r, t in zip(raw, sums)
+    )
+
+    named = weights[::NC, NBLK * ROWS_C, :PER].astype(jnp.int32).reshape(NY * PER)
+    at_x, at_y = (named // NY - x) % NX * NY, named % NY
+    me = y.reshape(1)
+
+    labels = sweep(at_x + (y - at_y) % NY, me, weights, priors[0], priors)
+    spread = sweep(at_x + at_y, me, weights, priors[0], around_x(labels))
     spread = lax.all_to_all(spread, "y", 0, 0, tiled=True)
     return jnp.log(spread.reshape(classes, rows).T.astype(F32))
 

time: 249 us -> 267 us (1.072)
  starting transfers between devices: 45.4 us -> 82.6 us
  blocking collectives: 81.5 us -> 57.2 us
  local copies, waits for them, and re-layouts: 11.9 us -> 18.3 us
  waiting for transfers between devices: 71.2 us -> 67.2 us
    all_to_all x1 -> x0, blocking collectives: 34.9 us -> none  [on_device(): prior = lax.all_to_all(prior, 'y', 0, 0, tiled=True)]
    ppermute x0 -> x7, starting transfers between devices: none -> 30.7 us  [over_y(): lax.ppermute(turned[d], 'y', [(i, (i + d) % NY) for i in range(NY)])]
    all_gather x1, waiting for transfers between devices: 0.02 us -> 18.9 us  [on_device(): weights = lax.all_gather(piece, ('y', 'c'), axis=0, tiled=False)]
    all_to_all x1, waiting for transfers between devices: 15 us -> 0.01 us  [on_device(): lax.all_to_all(jnp.broadcast_to(scaled, (NZ,) + scaled.shape), 'z', 0, 0,...]
    ppermute x2, waiting for transfers between devices: 0.01 us -> 12.2 us  [around_x(): after = lax.ppermute(mine, 'x', backward)]
    all_to_all x1, waiting for transfers between devices: 10.7 us -> 0.01 us  [on_device(): lax.all_to_all(outgoing.reshape(TILES, 2 * SUB, width), ('x', 'y'), 0, 0,...]
    ppermute x2, waiting for transfers between devices: 27.3 us -> 17 us  [around_x(): before = lax.ppermute(mine, 'x', forward)]
    all_to_all x0 -> x1, starting transfers between devices: none -> 7.19 us  [on_device(): lax.all_to_all(jnp.broadcast_to(totals, (TILES, rows)), ('x', 'y'), 0, 0,...]
  transfers between devices with their start and end apart: 11 -> 19, of which waited for: 8 -> 9; matrix products, arithmetic and copies ran while one was open for 1% -> 4% of each run, Pallas kernels for 0% -> 0%
where the time goes in v2:
time: 267 us; the launch traced here: 266 us
  starting transfers between devices  82.6 us (31%)
  waiting for transfers between devices  67.2 us (25%)
  blocking collectives  57.2 us (21%)
  local copies, waits for them, and re-layouts  18.3 us (7%)
  Pallas kernels  18.2 us (7%)
  between operations  14.5 us (5%)
  other arithmetic  6.78 us (3%)
    ppermute x7, starting transfers between devices, over_y(): lax.ppermute(turned[d], 'y', [(i, (i + d) % NY) for i in range(NY)])  30.7 us
    all_to_all x1, blocking collectives, on_device(): spread = lax.all_to_all(spread, 'y', 0, 0, tiled=True)  25.8 us
    all_gather x1, waiting for transfers between devices, on_device(): weights = lax.all_gather(piece, ('y', 'c'), axis=0, tiled=False)  18.9 us
    pallas_call x2, Pallas kernels, sweep(): pl.pallas_call(sweep_kernel, grid_spec=pltpu.PrefetchScalarGridSpec(num_s...  18.2 us
    ppermute x2, waiting for transfers between devices, around_x(): before = lax.ppermute(mine, 'x', forward)  17 us
    all_to_all x1, blocking collectives, on_device(): lax.all_to_all(scored.reshape(TILES, 2 * SUB, TILE), ('x', 'y'), 0, 0, ti...  17 us
    all_to_all x1, blocking collectives, on_device(): lax.all_to_all(jnp.broadcast_to(part, (NZ * NC, rows)), ('z', 'c'), 0, 0,...  14.5 us
    ppermute x2, waiting for transfers between devices, around_x(): after = lax.ppermute(mine, 'x', backward)  12.2 us
  transfers between devices with their start and end apart: 19, of which 9 were waited for; matrix products, arithmetic and copies ran while one was open for 4% of the time, Pallas kernels for 0%

profile of v2, /device:TPU:6, one launch (start us, length us, event | category | flops | bytes accessed | tf_op | source)
XLA Modules:
  0.0 266.0 jit_solution(17971738605655567893)
XLA Ops:
  6.5 1.1 constant_dynamic-slice_fusion.1
  7.6 0.8 copy.67
  8.5 0.2 convert_reduce_fusion
  8.8 0.8 multiply_add_fusion
  9.7 0.3 convolution_convert_fusion
  9.9 1.4 copy.69
  11.4 0.3 fusion.20
  11.7 0.7 slice_bitcast_fusion
  12.4 3.5 %collective-permute-start = (bf16[96,512]{1,0:T(8,128)(2,1)S(1)}, bf16[96,512]{1,0:T(8,128)(2,1)S(1)}, u32[]{:S(2)}, u32[]{:S(2)}) collective-permute-start(bf16[96,512]{1,0:T(8,128)(2,1)S(1)} %get-tuple-element.41), channel_id=1, source_target_pairs={{0,16},{16,32},{32,48},{48,64},{64,80},{80,96},{96,112},{112,0},{1... | collective-permute-start | bytes 294920 | tf_op jit(solution)/shard_map/ppermute | solution.py:129
  15.8 4.5 %collective-permute-start.1 = (bf16[96,512]{1,0:T(8,128)(2,1)S(1)}, bf16[96,512]{1,0:T(8,128)(2,1)S(1)}, u32[]{:S(2)}, u32[]{:S(2)}) collective-permute-start(bf16[96,512]{1,0:T(8,128)(2,1)S(1)} %get-tuple-element.40), channel_id=1, source_target_pairs={{0,32},{16,48},{32,64},{48,80},{64,96},{80,112},{96,0},{112,16},{1... | collective-permute-start | bytes 294920 | tf_op jit(solution)/shard_map/ppermute | solution.py:129
  20.4 4.9 %collective-permute-start.2 = (bf16[96,512]{1,0:T(8,128)(2,1)S(1)}, bf16[96,512]{1,0:T(8,128)(2,1)S(1)}, u32[]{:S(2)}, u32[]{:S(2)}) collective-permute-start(bf16[96,512]{1,0:T(8,128)(2,1)S(1)} %get-tuple-element.39), channel_id=1, source_target_pairs={{0,48},{16,64},{32,80},{48,96},{64,112},{80,0},{96,16},{112,32},{1... | collective-permute-start | bytes 294920 | tf_op jit(solution)/shard_map/ppermute | solution.py:129
  25.3 3.8 %collective-permute-start.3 = (bf16[96,512]{1,0:T(8,128)(2,1)S(1)}, bf16[96,512]{1,0:T(8,128)(2,1)S(1)}, u32[]{:S(2)}, u32[]{:S(2)}) collective-permute-start(bf16[96,512]{1,0:T(8,128)(2,1)S(1)} %get-tuple-element.38), channel_id=1, source_target_pairs={{0,64},{16,80},{32,96},{48,112},{64,0},{80,16},{96,32},{112,48},{1... | collective-permute-start | bytes 294920 | tf_op jit(solution)/shard_map/ppermute | solution.py:129
  29.1 5.2 %collective-permute-start.4 = (bf16[96,512]{1,0:T(8,128)(2,1)S(1)}, bf16[96,512]{1,0:T(8,128)(2,1)S(1)}, u32[]{:S(2)}, u32[]{:S(2)}) collective-permute-start(bf16[96,512]{1,0:T(8,128)(2,1)S(1)} %get-tuple-element.37), channel_id=1, source_target_pairs={{0,80},{16,96},{32,112},{48,0},{64,16},{80,32},{96,48},{112,64},{1... | collective-permute-start | bytes 294920 | tf_op jit(solution)/shard_map/ppermute | solution.py:129
  34.3 0.9 reshape.135
  35.2 8.5 %all-to-all-start = ((bf16[32,4,1280]{2,1,0:T(4,128)(2,1)}), bf16[32,4,1280]{2,1,0:T(4,128)(2,1)S(1)}, u32[]{:S(2)}, u32[]{:S(2)}) async-start(bf16[32,4,1280]{2,1,0:T(4,128)(2,1)} %reshape.135), calls=%async_computation | async-start | bytes 655360 | tf_op jit(solution)/shard_map/all_to_all | solution.py:165
  43.8 0.3 fusion
  44.8 5.5 %collective-permute-start.5 = (bf16[96,512]{1,0:T(8,128)(2,1)S(1)}, bf16[96,512]{1,0:T(8,128)(2,1)S(1)}, u32[]{:S(2)}, u32[]{:S(2)}) collective-permute-start(bf16[96,512]{1,0:T(8,128)(2,1)S(1)} %get-tuple-element.36), channel_id=1, source_target_pairs={{0,96},{16,112},{32,0},{48,16},{64,32},{80,48},{96,64},{112,80},{1... | collective-permute-start | bytes 294920 | tf_op jit(solution)/shard_map/ppermute | solution.py:129
  50.3 0.7 bitcast_dynamic-update-slice_fusion.6
  51.0 3.4 %collective-permute-start.6 = (bf16[96,512]{1,0:T(8,128)(2,1)S(1)}, bf16[96,512]{1,0:T(8,128)(2,1)S(1)}, u32[]{:S(2)}, u32[]{:S(2)}) collective-permute-start(bf16[96,512]{1,0:T(8,128)(2,1)S(1)} %get-tuple-element.35), channel_id=1, source_target_pairs={{0,112},{16,0},{32,16},{48,32},{64,48},{80,64},{96,80},{112,96},{1... | collective-permute-start | bytes 294920 | tf_op jit(solution)/shard_map/ppermute | solution.py:129
  54.3 0.7 bitcast_dynamic-update-slice_fusion.5
  55.0 0.6 bitcast_dynamic-update-slice_fusion.4
  55.6 0.6 bitcast_dynamic-update-slice_fusion.3
  56.3 0.6 bitcast_dynamic-update-slice_fusion.2
  56.9 0.6 bitcast_dynamic-update-slice_fusion.1
  57.6 0.6 bitcast_dynamic-update-slice_fusion
  58.2 0.2 multiply_reduce_fusion
  58.7 0.7 fusion.16
  59.4 17.0 %all_to_all.32 = bf16[32,4,512]{2,1,0:T(4,128)(2,1)S(1)} all-to-all(bf16[32,4,512]{2,1,0:T(4,128)(2,1)S(1)} %reshape.137), channel_id=1, replica_groups=mesh['x'=4,'y'=8,'z'=8,'c'=2] {'x','y'}, dimensions={0} | all-to-all | bytes 262144 | tf_op jit(solution)/shard_map/all_to_all | solution.py:180
  76.5 0.3 fusion.43
  77.0 1.1 broadcast_in_dim.27
  78.1 10.3 %all-to-all-start.2 = ((bf16[8,16,2,1024]{3,2,1,0:T(2,128)(2,1)}), bf16[8,16,2,1024]{3,2,1,0:T(2,128)(2,1)S(1)}, u32[]{:S(2)}, u32[]{:S(2)}) async-start(bf16[8,16,2,1024]{3,2,1,0:T(2,128)(2,1)} %broadcast_in_dim.27), calls=%async_computation.2 | async-start | bytes 1048576 | tf_op jit(solution)/shard_map/all_to_all | solution.py:189
  88.4 2.7 %collective-permute-start.7 = (bf16[8,96,512]{2,1,0:T(8,128)(2,1)}, bf16[8,96,512]{2,1,0:T(8,128)(2,1)S(1)}, u32[]{:S(2)}, u32[]{:S(2)}) collective-permute-start(bf16[8,96,512]{2,1,0:T(8,128)(2,1)} %bitcast_dynamic-update-slice_fusion), channel_id=1, source_target_pairs={{0,384},{128,0},{256,128},{384,256},{1,385},{129,1},{257,129},{385... | collective-permute-start | bytes 2359304 | tf_op jit(solution)/shard_map/ppermute | solution.py:117
  91.1 4.4 %collective-permute-start.8 = (bf16[8,96,512]{2,1,0:T(8,128)(2,1)}, bf16[8,96,512]{2,1,0:T(8,128)(2,1)S(1)}, u32[]{:S(2)}, u32[]{:S(2)}) collective-permute-start(bf16[8,96,512]{2,1,0:T(8,128)(2,1)} %bitcast_dynamic-update-slice_fusion), channel_id=1, source_target_pairs={{0,128},{128,256},{256,384},{384,0},{1,129},{129,257},{257,385},{3... | collective-permute-start | bytes 2359304 | tf_op jit(solution)/shard_map/ppermute | solution.py:116
  95.7 12.2 %collective-permute-done.7 = bf16[8,96,512]{2,1,0:T(8,128)(2,1)S(1)} collective-permute-done((bf16[8,96,512]{2,1,0:T(8,128)(2,1)}, bf16[8,96,512]{2,1,0:T(8,128)(2,1)S(1)}, u32[]{:S(2)}, u32[]{:S(2)}) %collective-permute-start.7) | collective-permute-done | bytes 786464 | tf_op jit(solution)/shard_map/ppermute | solution.py:117
  107.9 1.3 collective-permute-done.8
  109.2 0.5 copy.73
  109.7 0.2 reshape.140
  109.9 0.8 fusion.21
  110.8 0.3 exponential_reduce_fusion
  111.2 14.5 %all_to_all.33 = f32[16,1,512]{2,1,0:T(1,128)S(1)} all-to-all(f32[16,1,512]{2,1,0:T(1,128)S(1)} %broadcast_in_dim.28), channel_id=1, replica_groups=mesh['x'=4,'y'=8,'z'=8,'c'=2] {'z','c'}, dimensions={0} | all-to-all | bytes 65536 | tf_op jit(solution)/shard_map/all_to_all | solution.py:202
  125.7 0.7 broadcast_in_dim.29
  126.4 7.2 %all-to-all-start.4 = ((f32[32,1,512]{2,1,0:T(1,128)}), f32[32,1,512]{2,1,0:T(1,128)S(1)}, u32[]{:S(2)}, u32[]{:S(2)}) async-start(f32[32,1,512]{2,1,0:T(1,128)} %broadcast_in_dim.29), calls=%async_computation.4 | async-start | bytes 131072 | tf_op jit(solution)/shard_map/all_to_all | solution.py:206
  133.7 2.7 %collective-permute-start.10 = (bf16[4,96,512]{2,1,0:T(8,128)(2,1)S(1)}, bf16[4,96,512]{2,1,0:T(8,128)(2,1)S(1)}, u32[]{:S(2)}, u32[]{:S(2)}) collective-permute-start(bf16[4,96,512]{2,1,0:T(8,128)(2,1)S(1)} %slice.100), channel_id=1, source_target_pairs={{0,384},{128,0},{256,128},{384,256},{1,385},{129,1},{257,129},{385... | collective-permute-start | bytes 1179656 | tf_op jit(solution)/shard_map/ppermute | solution.py:120
  136.5 4.3 %collective-permute-start.9 = (bf16[4,96,512]{2,1,0:T(8,128)(2,1)S(1)}, bf16[4,96,512]{2,1,0:T(8,128)(2,1)S(1)}, u32[]{:S(2)}, u32[]{:S(2)}) collective-permute-start(bf16[4,96,512]{2,1,0:T(8,128)(2,1)S(1)} %slice.98), channel_id=1, source_target_pairs={{0,128},{128,256},{256,384},{384,0},{1,129},{129,257},{257,385},{3... | collective-permute-start | bytes 1179656 | tf_op jit(solution)/shard_map/ppermute | solution.py:119
  140.8 1.4 all-to-all-done.4
  142.4 5.5 %collective-permute-done.10 = bf16[4,96,512]{2,1,0:T(8,128)(2,1)S(1)} collective-permute-done((bf16[4,96,512]{2,1,0:T(8,128)(2,1)S(1)}, bf16[4,96,512]{2,1,0:T(8,128)(2,1)S(1)}, u32[]{:S(2)}, u32[]{:S(2)}) %collective-permute-start.10) | collective-permute-done | bytes 393248 | tf_op jit(solution)/shard_map/ppermute | solution.py:120
  147.9 1.1 collective-permute-done.9
  149.0 0.4 divide_convert_fusion.3
  149.4 2.1 divide_convert_fusion
  151.5 18.9 %all-gather.3.cloned.1.call-done = bf16[4352,1024]{1,0:T(8,128)(2,1)} async-done(((bf16[272,1024]{1,0:T(8,128)(2,1)}), bf16[4352,1024]{1,0:T(8,128)(2,1)}) %all-gather.3.cloned.1.call-update) | async-done | bytes 8912912 | tf_op jit(solution)/shard_map/all_gather | solution.py:197
  170.4 0.7 convert_reduce_fusion.1
  171.3 3.5 %copy-done = bf16[4352,1024]{1,0:T(8,128)(2,1)S(1)} copy-done((bf16[4352,1024]{1,0:T(8,128)(2,1)S(1)}, bf16[4352,1024]{1,0:T(8,128)(2,1)}, u32[]{:S(2)}) %copy-start) | copy-done | bytes 8912920
  174.8 9.1 %shard_map.55.own = bf16[8,96,512]{2,1,0:T(8,128)(2,1)S(1)} custom-call(s32[256]{0:T(256)S(1)} %get-tuple-element.33.index_ref, s32[1]{0:T(128)} %bitcast.25.me_ref, bf16[16,272,1024]{2,1,0:T(8,128)(2,1)S(1)} %bitcast.79, bf16[8,96,512]{2,1,0:T(8,128)(2,1)S(1)} %get-tuple-element.52.prior_ref.own, bf16[8,96,512]{2,1,0:T(8,128)(2,1)S(1)} %get-tuple-element.52.prior_ref.own, ...), custom_call_target="tpu_custom_call" | custom-call | flops 3221225472 | bytes 12058624 | tf_op jit(solution)/shard_map/pallas_call | solution.py:87
  183.9 2.5 collective-permute-start.12
  186.3 3.4 %collective-permute-start.11 = (bf16[8,96,512]{2,1,0:T(8,128)(2,1)S(1)}, bf16[8,96,512]{2,1,0:T(8,128)(2,1)S(1)}, u32[]{:S(2)}, u32[]{:S(2)}) collective-permute-start(bf16[8,96,512]{2,1,0:T(8,128)(2,1)S(1)} %shard_map.55.own), channel_id=1, source_target_pairs={{0,384},{128,0},{256,128},{384,256},{1,385},{129,1},{257,129},{385... | collective-permute-start | bytes 2359304 | tf_op jit(solution)/shard_map/ppermute | solution.py:117
  189.7 15.7 %collective-permute-done.12.before = bf16[8,96,512]{2,1,0:T(8,128)(2,1)S(1)} collective-permute-done((bf16[8,96,512]{2,1,0:T(8,128)(2,1)S(1)}, bf16[8,96,512]{2,1,0:T(8,128)(2,1)S(1)}, u32[]{:S(2)}, u32[]{:S(2)}) %collective-permute-start.12) | collective-permute-done | bytes 786464 | tf_op jit(solution)/shard_map/ppermute | solution.py:116
  205.5 3.7 %collective-permute-start.13 = (bf16[4,96,512]{2,1,0:T(8,128)(2,1)S(1)}, bf16[4,96,512]{2,1,0:T(8,128)(2,1)S(1)}, u32[]{:S(2)}, u32[]{:S(2)}) collective-permute-start(bf16[4,96,512]{2,1,0:T(8,128)(2,1)S(1)} %slice.103), channel_id=1, source_target_pairs={{0,128},{128,256},{256,384},{384,0},{1,129},{129,257},{257,385},{3... | collective-permute-start | bytes 1179656 | tf_op jit(solution)/shard_map/ppermute | solution.py:119
  209.2 2.2 collective-permute-start.14
  211.4 6.4 %collective-permute-done.13.oppa = bf16[4,96,512]{2,1,0:T(8,128)(2,1)S(1)} collective-permute-done((bf16[4,96,512]{2,1,0:T(8,128)(2,1)S(1)}, bf16[4,96,512]{2,1,0:T(8,128)(2,1)S(1)}, u32[]{:S(2)}, u32[]{:S(2)}) %collective-permute-start.13) | collective-permute-done | bytes 393248 | tf_op jit(solution)/shard_map/ppermute | solution.py:119
  217.8 4.6 %collective-permute-done.14.oppb = bf16[4,96,512]{2,1,0:T(8,128)(2,1)S(1)} collective-permute-done((bf16[4,96,512]{2,1,0:T(8,128)(2,1)S(1)}, bf16[4,96,512]{2,1,0:T(8,128)(2,1)S(1)}, u32[]{:S(2)}, u32[]{:S(2)}) %collective-permute-start.14) | collective-permute-done | bytes 393248 | tf_op jit(solution)/shard_map/ppermute | solution.py:120
  222.5 9.1 %shard_map.56 = bf16[8,96,512]{2,1,0:T(8,128)(2,1)S(1)} custom-call(s32[256]{0:T(256)S(1)} %fusion.41.index_ref, s32[1]{0:T(128)} %bitcast.25.me_ref, bf16[16,272,1024]{2,1,0:T(8,128)(2,1)S(1)} %bitcast.80, bf16[8,96,512]{2,1,0:T(8,128)(2,1)S(1)} %get-tuple-element.52.prior_ref.own, bf16[8,96,512]{2,1,0:T(8,128)(2,1)S(1)} %shard_map.55.own, ...), custom_call_target="tpu_custom_call" | custom-call | flops 3221225472 | bytes 12058624 | tf_op jit(solution)/shard_map/pallas_call | solution.py:87
  231.6 25.8 %all_to_all.34 = bf16[8,96,512]{2,1,0:T(8,128)(2,1)S(1)} all-to-all(bf16[8,96,512]{2,1,0:T(8,128)(2,1)S(1)} %shard_map.56), channel_id=1, replica_groups=mesh['x'=4,'y'=8,'z'=8,'c'=2] {'y'}, dimensions={0} | all-to-all | bytes 1572864 | tf_op jit(solution)/shard_map/all_to_all | solution.py:225
  257.3 0.2 convert_log_fusion
  257.6 1.6 copy.76
  (61 shorter events, 1.7 us)
Async XLA Ops:
  11.7 32.1 %copy-start.6 = (bf16[512,1280]{1,0:T(8,128)(2,1)S(1)}, bf16[512,1280]{1,0:T(8,128)(2,1)}, u32[]{:S(2)}) copy-start(bf16[512,1280]{1,0:T(8,128)(2,1)} %param.7) | copy-start | bytes 3932164
  12.4 32.4 %collective-permute-start = (bf16[96,512]{1,0:T(8,128)(2,1)S(1)}, bf16[96,512]{1,0:T(8,128)(2,1)S(1)}, u32[]{:S(2)}, u32[]{:S(2)}) collective-permute-start(bf16[96,512]{1,0:T(8,128)(2,1)S(1)} %get-tuple-element.41), channel_id=1, source_target_pairs={{0,16},{16,32},{32,48},{48,64},{64,80},{80,96},{96,112},{112,0},{1... | collective-permute-start | bytes 294920 | tf_op jit(solution)/shard_map/ppermute | solution.py:129
  15.8 35.1 %collective-permute-start.1 = (bf16[96,512]{1,0:T(8,128)(2,1)S(1)}, bf16[96,512]{1,0:T(8,128)(2,1)S(1)}, u32[]{:S(2)}, u32[]{:S(2)}) collective-permute-start(bf16[96,512]{1,0:T(8,128)(2,1)S(1)} %get-tuple-element.40), channel_id=1, source_target_pairs={{0,32},{16,48},{32,64},{48,80},{64,96},{80,112},{96,0},{112,16},{1... | collective-permute-start | bytes 294920 | tf_op jit(solution)/shard_map/ppermute | solution.py:129
  20.4 34.6 %collective-permute-start.2 = (bf16[96,512]{1,0:T(8,128)(2,1)S(1)}, bf16[96,512]{1,0:T(8,128)(2,1)S(1)}, u32[]{:S(2)}, u32[]{:S(2)}) collective-permute-start(bf16[96,512]{1,0:T(8,128)(2,1)S(1)} %get-tuple-element.39), channel_id=1, source_target_pairs={{0,48},{16,64},{32,80},{48,96},{64,112},{80,0},{96,16},{112,32},{1... | collective-permute-start | bytes 294920 | tf_op jit(solution)/shard_map/ppermute | solution.py:129
  25.3 30.3 %collective-permute-start.3 = (bf16[96,512]{1,0:T(8,128)(2,1)S(1)}, bf16[96,512]{1,0:T(8,128)(2,1)S(1)}, u32[]{:S(2)}, u32[]{:S(2)}) collective-permute-start(bf16[96,512]{1,0:T(8,128)(2,1)S(1)} %get-tuple-element.38), channel_id=1, source_target_pairs={{0,64},{16,80},{32,96},{48,112},{64,0},{80,16},{96,32},{112,48},{1... | collective-permute-start | bytes 294920 | tf_op jit(solution)/shard_map/ppermute | solution.py:129
  29.1 27.2 %collective-permute-start.4 = (bf16[96,512]{1,0:T(8,128)(2,1)S(1)}, bf16[96,512]{1,0:T(8,128)(2,1)S(1)}, u32[]{:S(2)}, u32[]{:S(2)}) collective-permute-start(bf16[96,512]{1,0:T(8,128)(2,1)S(1)} %get-tuple-element.37), channel_id=1, source_target_pairs={{0,80},{16,96},{32,112},{48,0},{64,16},{80,32},{96,48},{112,64},{1... | collective-permute-start | bytes 294920 | tf_op jit(solution)/shard_map/ppermute | solution.py:129
  35.2 23.1 %all-to-all-start = ((bf16[32,4,1280]{2,1,0:T(4,128)(2,1)}), bf16[32,4,1280]{2,1,0:T(4,128)(2,1)S(1)}, u32[]{:S(2)}, u32[]{:S(2)}) async-start(bf16[32,4,1280]{2,1,0:T(4,128)(2,1)} %reshape.135), calls=%async_computation | async-start | bytes 655360 | tf_op jit(solution)/shard_map/all_to_all | solution.py:165
  44.8 12.2 %collective-permute-start.5 = (bf16[96,512]{1,0:T(8,128)(2,1)S(1)}, bf16[96,512]{1,0:T(8,128)(2,1)S(1)}, u32[]{:S(2)}, u32[]{:S(2)}) collective-permute-start(bf16[96,512]{1,0:T(8,128)(2,1)S(1)} %get-tuple-element.36), channel_id=1, source_target_pairs={{0,96},{16,112},{32,0},{48,16},{64,32},{80,48},{96,64},{112,80},{1... | collective-permute-start | bytes 294920 | tf_op jit(solution)/shard_map/ppermute | solution.py:129
  51.0 6.6 %collective-permute-start.6 = (bf16[96,512]{1,0:T(8,128)(2,1)S(1)}, bf16[96,512]{1,0:T(8,128)(2,1)S(1)}, u32[]{:S(2)}, u32[]{:S(2)}) collective-permute-start(bf16[96,512]{1,0:T(8,128)(2,1)S(1)} %get-tuple-element.35), channel_id=1, source_target_pairs={{0,112},{16,0},{32,16},{48,32},{64,48},{80,64},{96,80},{112,96},{1... | collective-permute-start | bytes 294920 | tf_op jit(solution)/shard_map/ppermute | solution.py:129
  78.1 31.2 %all-to-all-start.2 = ((bf16[8,16,2,1024]{3,2,1,0:T(2,128)(2,1)}), bf16[8,16,2,1024]{3,2,1,0:T(2,128)(2,1)S(1)}, u32[]{:S(2)}, u32[]{:S(2)}) async-start(bf16[8,16,2,1024]{3,2,1,0:T(2,128)(2,1)} %broadcast_in_dim.27), calls=%async_computation.2 | async-start | bytes 1048576 | tf_op jit(solution)/shard_map/all_to_all | solution.py:189
  88.4 82.0 %all-gather.3.cloned.1.call-start = ((), (), s32[]{:S(2)}) async-start(), calls=%async_computation.6 | async-start | bytes 9469952 | tf_op jit(solution)/shard_map/all_gather | solution.py:197
  88.4 19.5 %collective-permute-start.7 = (bf16[8,96,512]{2,1,0:T(8,128)(2,1)}, bf16[8,96,512]{2,1,0:T(8,128)(2,1)S(1)}, u32[]{:S(2)}, u32[]{:S(2)}) collective-permute-start(bf16[8,96,512]{2,1,0:T(8,128)(2,1)} %bitcast_dynamic-update-slice_fusion), channel_id=1, source_target_pairs={{0,384},{128,0},{256,128},{384,256},{1,385},{129,1},{257,129},{385... | collective-permute-start | bytes 2359304 | tf_op jit(solution)/shard_map/ppermute | solution.py:117
  91.1 18.1 %collective-permute-start.8 = (bf16[8,96,512]{2,1,0:T(8,128)(2,1)}, bf16[8,96,512]{2,1,0:T(8,128)(2,1)S(1)}, u32[]{:S(2)}, u32[]{:S(2)}) collective-permute-start(bf16[8,96,512]{2,1,0:T(8,128)(2,1)} %bitcast_dynamic-update-slice_fusion), channel_id=1, source_target_pairs={{0,128},{128,256},{256,384},{384,0},{1,129},{129,257},{257,385},{3... | collective-permute-start | bytes 2359304 | tf_op jit(solution)/shard_map/ppermute | solution.py:116
  107.9 25.7 %copy-start.2 = (bf16[8,96,512]{2,1,0:T(8,128)(2,1)}, bf16[8,96,512]{2,1,0:T(8,128)(2,1)S(1)}, u32[]{:S(2)}) copy-start(bf16[8,96,512]{2,1,0:T(8,128)(2,1)S(1)} %collective-permute-done.7) | copy-start | bytes 2359300
  109.2 27.2 %copy-start.4 = (bf16[8,96,512]{2,1,0:T(8,128)(2,1)}, bf16[8,96,512]{2,1,0:T(8,128)(2,1)S(1)}, u32[]{:S(2)}) copy-start(bf16[8,96,512]{2,1,0:T(8,128)(2,1)S(1)} %collective-permute-done.8) | copy-start | bytes 2359300
  109.7 1.1 copy-start.1
  109.7 1.1 copy-start.7
  126.4 15.8 %all-to-all-start.4 = ((f32[32,1,512]{2,1,0:T(1,128)}), f32[32,1,512]{2,1,0:T(1,128)S(1)}, u32[]{:S(2)}, u32[]{:S(2)}) async-start(f32[32,1,512]{2,1,0:T(1,128)} %broadcast_in_dim.29), calls=%async_computation.4 | async-start | bytes 131072 | tf_op jit(solution)/shard_map/all_to_all | solution.py:206
  133.7 14.2 %collective-permute-start.10 = (bf16[4,96,512]{2,1,0:T(8,128)(2,1)S(1)}, bf16[4,96,512]{2,1,0:T(8,128)(2,1)S(1)}, u32[]{:S(2)}, u32[]{:S(2)}) collective-permute-start(bf16[4,96,512]{2,1,0:T(8,128)(2,1)S(1)} %slice.100), channel_id=1, source_target_pairs={{0,384},{128,0},{256,128},{384,256},{1,385},{129,1},{257,129},{385... | collective-permute-start | bytes 1179656 | tf_op jit(solution)/shard_map/ppermute | solution.py:120
  136.5 12.6 %collective-permute-start.9 = (bf16[4,96,512]{2,1,0:T(8,128)(2,1)S(1)}, bf16[4,96,512]{2,1,0:T(8,128)(2,1)S(1)}, u32[]{:S(2)}, u32[]{:S(2)}) collective-permute-start(bf16[4,96,512]{2,1,0:T(8,128)(2,1)S(1)} %slice.98), channel_id=1, source_target_pairs={{0,128},{128,256},{256,384},{384,0},{1,129},{129,257},{257,385},{3... | collective-permute-start | bytes 1179656 | tf_op jit(solution)/shard_map/ppermute | solution.py:119
  142.3 7.1 %copy-start.3 = (bf16[8,96,512]{2,1,0:T(8,128)(2,1)S(1)}, bf16[8,96,512]{2,1,0:T(8,128)(2,1)}, u32[]{:S(2)}) copy-start(bf16[8,96,512]{2,1,0:T(8,128)(2,1)} %copy-done.2) | copy-start | bytes 2359300
  142.3 7.1 %copy-start.5 = (bf16[8,96,512]{2,1,0:T(8,128)(2,1)S(1)}, bf16[8,96,512]{2,1,0:T(8,128)(2,1)}, u32[]{:S(2)}) copy-start(bf16[8,96,512]{2,1,0:T(8,128)(2,1)} %copy-done.4) | copy-start | bytes 2359300
  171.2 3.5 %copy-start = (bf16[4352,1024]{1,0:T(8,128)(2,1)S(1)}, bf16[4352,1024]{1,0:T(8,128)(2,1)}, u32[]{:S(2)}) copy-start(bf16[4352,1024]{1,0:T(8,128)(2,1)} %all-gather.3.cloned.1.call-done) | copy-start | bytes 26738692
  183.9 21.6 %collective-permute-start.12 = (bf16[8,96,512]{2,1,0:T(8,128)(2,1)S(1)}, bf16[8,96,512]{2,1,0:T(8,128)(2,1)S(1)}, u32[]{:S(2)}, u32[]{:S(2)}) collective-permute-start(bf16[8,96,512]{2,1,0:T(8,128)(2,1)S(1)} %shard_map.55.own), channel_id=1, source_target_pairs={{0,128},{128,256},{256,384},{384,0},{1,129},{129,257},{257,385},{3... | collective-permute-start | bytes 2359304 | tf_op jit(solution)/shard_map/ppermute | solution.py:116
  186.3 22.8 %collective-permute-start.11 = (bf16[8,96,512]{2,1,0:T(8,128)(2,1)S(1)}, bf16[8,96,512]{2,1,0:T(8,128)(2,1)S(1)}, u32[]{:S(2)}, u32[]{:S(2)}) collective-permute-start(bf16[8,96,512]{2,1,0:T(8,128)(2,1)S(1)} %shard_map.55.own), channel_id=1, source_target_pairs={{0,384},{128,0},{256,128},{384,256},{1,385},{129,1},{257,129},{385... | collective-permute-start | bytes 2359304 | tf_op jit(solution)/shard_map/ppermute | solution.py:117
  205.5 12.3 %collective-permute-start.13 = (bf16[4,96,512]{2,1,0:T(8,128)(2,1)S(1)}, bf16[4,96,512]{2,1,0:T(8,128)(2,1)S(1)}, u32[]{:S(2)}, u32[]{:S(2)}) collective-permute-start(bf16[4,96,512]{2,1,0:T(8,128)(2,1)S(1)} %slice.103), channel_id=1, source_target_pairs={{0,128},{128,256},{256,384},{384,0},{1,129},{129,257},{257,385},{3... | collective-permute-start | bytes 1179656 | tf_op jit(solution)/shard_map/ppermute | solution.py:119
  209.2 13.3 %collective-permute-start.14 = (bf16[4,96,512]{2,1,0:T(8,128)(2,1)S(1)}, bf16[4,96,512]{2,1,0:T(8,128)(2,1)S(1)}, u32[]{:S(2)}, u32[]{:S(2)}) collective-permute-start(bf16[4,96,512]{2,1,0:T(8,128)(2,1)S(1)} %slice.104), channel_id=1, source_target_pairs={{0,384},{128,0},{256,128},{384,256},{1,385},{129,1},{257,129},{385... | collective-permute-start | bytes 1179656 | tf_op jit(solution)/shard_map/ppermute | solution.py:120
Sparse Core Ops, SparseCore 0:
  110.9 59.4 all-gather.2

commit v3 on v1

--- a/solution.py
+++ b/solution.py
@@ -1,3 +1,4 @@
+import functools
 import math
 
 import jax
@@ -21,7 +22,7 @@
 PER = NBLK * NT
 SLOTS = TILES * 2
 SUB = 2
-ROWS_C = QB // NC
+PARTS = 2
 BF = jnp.bfloat16
 F32 = jnp.float32
 
@@ -32,23 +33,23 @@
     return (wide * scale / math.sqrt(wide.shape[-1])).astype(BF)
 
 
-def sweep_kernel(index_ref, w_ref, prior_ref, own, after, oppa, oppb, before, out_ref, held, sems):
+def sweep_kernel(first, counts, index_ref, *refs):
+    n_weights, n_labels = counts
+    w_refs, prior_ref, refs = refs[:n_weights], refs[n_weights], refs[n_weights + 1 :]
+    labels_refs, (out_ref, held, sems) = refs[: 5 * n_labels], refs[5 * n_labels :]
     y = pl.program_id(0)
 
     @pl.when(y == 0)
     def _():
-        half = NY // 2
-        places = (
-            (own, 0, NY),
-            (after, NY, NY),
-            (oppa, 2 * NY, half),
-            (oppb, 2 * NY + half, half),
-            (before, 3 * NY, NY),
-        )
-        copies = [
-            pltpu.make_async_copy(src, held.at[pl.ds(at, n)], sems.at[i])
-            for i, (src, at, n) in enumerate(places)
-        ]
+        half, lanes = NY // 2, TILE // n_labels
+        at = (0, NY, 2 * NY, 2 * NY + half, 3 * NY)
+        copies = []
+        for i, src in enumerate(labels_refs):
+            part, piece = divmod(i, 5)
+            dst = held.at[
+                pl.ds(at[piece], src.shape[0]), :, pl.ds(part * lanes, lanes)
+            ]
+            copies.append(pltpu.make_async_copy(src, dst, sems.at[i]))
         for copy in copies:
             copy.start()
         for copy in copies:
@@ -56,19 +57,15 @@
 
     classes = out_ref.shape[1]
     lanes = lax.broadcasted_iota(jnp.int32, (classes, 128), 1) // QB
-    for group in range(NBLK // 4):
+    per_part = w_refs[0].shape[1] * NC // QB
+    for group in range(n_weights * per_part // 4):
+        part, local = divmod(group * 4, per_part)
         total = None
         for k in range(NT):
-            weights = jnp.concatenate(
-                [
-                    w_ref[c, pl.ds((4 * group + b) * ROWS_C, ROWS_C), pl.ds(k * TILE, TILE)]
-                    for b in range(4)
-                    for c in range(NC)
-                ],
+            weights = block_rows(w_refs[part], local, per_part, k)
+            labels = jnp.concatenate(
+                [held[index_ref[y * PER + (first + 4 * group + b) * NT + k]] for b in range(4)],
                 axis=0,
-            )
-            labels = jnp.concatenate(
-                [held[index_ref[y * PER + (4 * group + b) * NT + k]] for b in range(4)], axis=0
             )
             sums = lax.dot_general(
                 labels, weights, (((1,), (1,)), ((), ())), preferred_element_type=F32
@@ -82,32 +79,46 @@
         out_ref[0, :, at] = (picked + (1.0 - ALPHA) * prior).astype(BF)
 
 
-def sweep(index, weights, prior, pieces):
-    ny, classes, rows = prior.shape
+def block_rows(w_ref, block, per_part, k):
+    each = per_part // NC
+    core, at = divmod(block, each)
+    columns = pl.ds(k * TILE, TILE)
+    if at + 4 <= each:
+        return w_ref[core, pl.ds(at * QB, 4 * QB), columns]
+    return jnp.concatenate(
+        [w_ref[(block + b) // each, pl.ds((block + b) % each * QB, QB), columns] for b in range(4)],
+        axis=0,
+    )
+
+
+def sweep(index, weights, first, prior, lane_block, pieces):
+    ny, classes, _ = prior.shape
+    rows = len(weights) * NC * weights[0].shape[1]
+    flat = [piece for part in pieces for piece in part]
     return pl.pallas_call(
-        sweep_kernel,
+        functools.partial(sweep_kernel, first, (len(weights), len(pieces))),
         grid_spec=pltpu.PrefetchScalarGridSpec(
             num_scalar_prefetch=1,
             grid=(ny,),
             in_specs=[
-                pl.BlockSpec((NC,) + weights.shape[1:], lambda y, _: (y, 0, 0)),
-                pl.BlockSpec((1, classes, rows), lambda y, _: (y, 0, 0)),
+                pl.BlockSpec((NC,) + w.shape[1:], lambda y, _: (y, 0, 0)) for w in weights
             ]
-            + [pl.BlockSpec(memory_space=pl.ANY)] * len(pieces),
+            + [pl.BlockSpec((1, classes, rows), lambda y, _: (y, 0, lane_block))]
+            + [pl.BlockSpec(memory_space=pl.ANY)] * len(flat),
             out_specs=pl.BlockSpec((1, classes, rows), lambda y, _: (y, 0, 0)),
             scratch_shapes=[
-                pltpu.VMEM((TILES, classes, rows), BF),
-                pltpu.SemaphoreType.DMA((len(pieces),)),
+                pltpu.VMEM((TILES, classes, TILE), BF),
+                pltpu.SemaphoreType.DMA((len(flat),)),
             ],
         ),
-        out_shape=jax.ShapeDtypeStruct(prior.shape, BF),
-        compiler_params=pltpu.CompilerParams(vmem_limit_bytes=24 << 20),
+        out_shape=jax.ShapeDtypeStruct((ny, classes, rows), BF),
+        compiler_params=pltpu.CompilerParams(vmem_limit_bytes=40 << 20),
         cost_estimate=pl.CostEstimate(
             flops=2 * ny * rows * NT * TILE * classes * 4,
-            bytes_accessed=weights.size * 2 + 4 * prior.size * 2,
+            bytes_accessed=sum(w.size for w in weights) * 2 + 4 * prior.size * 2,
             transcendentals=0,
         ),
-    )(index, weights, prior, *pieces)
+    )(index, *weights, prior, *flat)
 
 
 def around_x(mine):
@@ -133,7 +144,7 @@
     hits = position.reshape(NBLK, NT)[:, :, None] == jnp.arange(SLOTS, dtype=jnp.int32)
     hits = hits.astype(BF)
 
-    row = core * ROWS_C + z * SUB
+    row = (z * NC + core) * SUB
     mine = lax.dynamic_slice_in_dim(features.reshape(NBLK, QB, width), row, SUB, axis=1)
     outgoing = jnp.einsum(
         "bs,bf->sf",
@@ -154,6 +165,9 @@
     prior = (jnp.exp(adjusted) / totals[:, None]).astype(BF)
     prior = prior.T.reshape(NY, classes // NY, rows)
     prior = lax.all_to_all(prior, "y", 0, 0, tiled=True)
+    lists = lax.all_to_all(
+        jnp.broadcast_to(owners, (NY, PER)), "y", 0, 0, tiled=True
+    )
 
     memory = unitnorm_rows(features)
     queries = unitnorm_rows(arrived.reshape(SLOTS * SUB, width))
@@ -171,20 +185,24 @@
     scaled = (ALPHA * chosen / denominator).astype(BF)
     scaled = scaled.transpose(0, 2, 1, 3).reshape(NBLK, SUB, NT * TILE)
 
-    over_z = lax.all_to_all(
-        jnp.broadcast_to(scaled, (NZ,) + scaled.shape), "z", 0, 0, tiled=True
-    )
-    over_z = over_z.transpose(1, 0, 2, 3).reshape(NBLK * ROWS_C, NT * TILE)
-    names = jnp.zeros((16, NT * TILE), BF).at[0, :PER].set(owners.astype(BF))
-    piece = jnp.concatenate([over_z, names], axis=0)
-    weights = lax.all_gather(piece, ("y", "c"), axis=0, tiled=False)
-
-    named = weights[::NC, NBLK * ROWS_C, :PER].astype(jnp.int32)
-    index = ((named // NY - x) % NX) * NY + named % NY
-    index = index.reshape(NY * PER)
-
-    labels = sweep(index, weights, prior, around_x(prior))
-    spread = sweep(index, weights, prior, around_x(labels))
+    own = lax.all_gather(scaled, ("z", "c"), axis=0, tiled=False)
+    own, prior = lax.optimization_barrier((own, prior))
+    count = NBLK // PARTS // NC
+    gathered = []
+    for part in range(PARTS):
+        piece = lax.dynamic_slice_in_dim(own, (part * NC + core) * count, count, axis=1)
+        piece = piece.transpose(1, 0, 2, 3).reshape(count * QB, NT * TILE)
+        gathered.append(lax.all_gather(piece, ("y", "c"), axis=0, tiled=False))
+
+    named = lists.reshape(NY * PER)
+    index = (named // NY - x) % NX * NY + named % NY
+
+    priors = around_x(prior)
+    each = [
+        sweep(index, [w], part * NBLK // PARTS, prior, part, [priors])
+        for part, w in enumerate(gathered)
+    ]
+    spread = sweep(index, gathered, 0, prior, 0, [around_x(labels) for labels in each])
     spread = lax.all_to_all(spread, "y", 0, 0, tiled=True)
     return jnp.log(spread.reshape(classes, rows).T.astype(F32))
 

time: 249 us -> 264 us (1.060)
  blocking collectives: 81.5 us -> 58.1 us
  waiting for transfers between devices: 71.2 us -> 89.9 us
  starting transfers between devices: 45.4 us -> 55.7 us
  local copies, waits for them, and re-layouts: 11.9 us -> 18.8 us
  Pallas kernels: 18.1 us -> 21.4 us
    all_to_all x1 -> x0, blocking collectives: 34.9 us -> none  [on_device(): prior = lax.all_to_all(prior, 'y', 0, 0, tiled=True)]
    all_gather x1 -> x3, waiting for transfers between devices: 0.02 us -> 25.5 us  [the longest x2 25.5 us: on_device(): gathered.append(lax.all_gather(piece, ('y', 'c'), axis=0, tiled=False))]
    all_to_all x1 -> x2, waiting for transfers between devices: 15 us -> 31.2 us  [the longest x1 23.6 us: on_device(): prior = lax.all_to_all(prior, 'y', 0, 0, tiled=True)]
    ppermute x2 -> x3, waiting for transfers between devices: 27.3 us -> 15.7 us  [around_x(): before = lax.ppermute(mine, 'x', forward)]
    all_to_all x1, blocking collectives: 10.3 us -> 17.9 us  [on_device(): lax.all_to_all(jnp.broadcast_to(part, (NZ * NC, rows)), ('z', 'c'), 0, 0,...]
    ppermute x2 -> x3, waiting for transfers between devices: 7.1 us -> 1.21 us  [around_x(): oppa = lax.ppermute(before[:half], 'x', forward)]
    ppermute x2 -> x3, starting transfers between devices: 5.89 us -> 11.7 us  [around_x(): before = lax.ppermute(mine, 'x', forward)]
    ppermute x2 -> x3, waiting for transfers between devices: 11 us -> 5.63 us  [around_x(): oppb = lax.ppermute(after[half:], 'x', backward)]
  transfers between devices with their start and end apart: 11 -> 18, of which waited for: 8 -> 9; matrix products, arithmetic and copies ran while one was open for 1% -> 3% of each run, Pallas kernels for 0% -> 4%
where the time goes in v3:
time: 264 us; the launch traced here: 263 us
  waiting for transfers between devices  89.9 us (34%)
  blocking collectives  58.1 us (22%)
  starting transfers between devices  55.7 us (21%)
  Pallas kernels  21.4 us (8%)
  local copies, waits for them, and re-layouts  18.8 us (7%)
  between operations  14.2 us (5%)
  other arithmetic  3.23 us (1%)
    all_gather x2, waiting for transfers between devices, on_device(): gathered.append(lax.all_gather(piece, ('y', 'c'), axis=0, tiled=False))  25.5 us
    all_to_all x1, blocking collectives, on_device(): spread = lax.all_to_all(spread, 'y', 0, 0, tiled=True)  25.1 us
    all_to_all x1, waiting for transfers between devices, on_device(): prior = lax.all_to_all(prior, 'y', 0, 0, tiled=True)  23.6 us
    pallas_call x3, Pallas kernels, sweep(): pl.pallas_call(functools.partial(sweep_kernel, first, (len(weights), len(...  21.4 us
    all_to_all x1, blocking collectives, on_device(): lax.all_to_all(jnp.broadcast_to(part, (NZ * NC, rows)), ('z', 'c'), 0, 0,...  17.9 us
    ppermute x3, waiting for transfers between devices, around_x(): before = lax.ppermute(mine, 'x', forward)  15.7 us
    all_to_all x1, blocking collectives, on_device(): lax.all_to_all(scored.reshape(TILES, 2 * SUB, TILE), ('x', 'y'), 0, 0, ti...  15 us
    ppermute x3, starting transfers between devices, around_x(): oppa = lax.ppermute(before[:half], 'x', forward)  13.9 us
  transfers between devices with their start and end apart: 18, of which 9 were waited for; matrix products, arithmetic and copies ran while one was open for 3% of the time, Pallas kernels for 4%

profile of v3, /device:TPU:6, one launch (start us, length us, event | category | flops | bytes accessed | tf_op | source)
XLA Modules:
  0.0 262.6 jit_solution(15426208023867378020)
XLA Ops:
  6.5 0.9 copy.61
  7.4 0.1 broadcast_in_dim.24
  7.5 0.2 convert_reduce_fusion
  7.7 0.1 copy.62
  7.8 0.7 multiply_add_fusion
  8.6 1.1 constant_dynamic-slice_fusion
  9.7 0.3 convolution_convert_fusion
  10.0 0.9 reshape.81
  10.9 10.2 %all-to-all-start.1 = ((bf16[32,4,1280]{2,1,0:T(4,128)(2,1)}), bf16[32,4,1280]{2,1,0:T(4,128)(2,1)S(1)}, u32[]{:S(2)}, u32[]{:S(2)}) async-start(bf16[32,4,1280]{2,1,0:T(4,128)(2,1)} %reshape.81), calls=%async_computation.1 | async-start | bytes 655360 | tf_op jit(solution)/shard_map/all_to_all | solution.py:155
  21.9 0.3 fusion
  22.2 10.6 %all-to-all-done.1 = bf16[32,4,1280]{2,1,0:T(4,128)(2,1)S(1)} async-done(((bf16[32,4,1280]{2,1,0:T(4,128)(2,1)}), bf16[32,4,1280]{2,1,0:T(4,128)(2,1)S(1)}, u32[]{:S(2)}, u32[]{:S(2)}) %all-to-all-start.1) | async-done | bytes 327712 | tf_op jit(solution)/shard_map/all_to_all | solution.py:155
  32.8 0.2 multiply_reduce_fusion
  33.1 0.1 rsqrt.20
  33.2 0.7 fusion.17
  34.0 15.0 %all_to_all.32 = bf16[32,4,512]{2,1,0:T(4,128)(2,1)S(1)} all-to-all(bf16[32,4,512]{2,1,0:T(4,128)(2,1)S(1)} %reshape.82), channel_id=1, replica_groups=mesh['x'=4,'y'=8,'z'=8,'c'=2] {'x','y'}, dimensions={0} | all-to-all | bytes 262144 | tf_op jit(solution)/shard_map/all_to_all | solution.py:179
  49.0 0.1 reshape.83
  49.1 0.3 fusion.36
  49.4 0.1 fusion.25
  49.6 0.7 all_gather_reshape.9
  50.3 0.3 fusion.3
  50.6 17.9 %all_to_all.33 = f32[16,1,512]{2,1,0:T(1,128)S(1)} all-to-all(f32[16,1,512]{2,1,0:T(1,128)S(1)} %broadcast_in_dim.28), channel_id=1, replica_groups=mesh['x'=4,'y'=8,'z'=8,'c'=2] {'z','c'}, dimensions={0} | all-to-all | bytes 65536 | tf_op jit(solution)/shard_map/all_to_all | solution.py:161
  68.6 0.3 fusion.20
  68.9 1.2 copy.66
  70.1 3.5 %all-to-all-start.4 = ((bf16[8,96,512]{2,1,0:T(8,128)(2,1)}), bf16[8,96,512]{2,1,0:T(8,128)(2,1)S(1)}, u32[]{:S(2)}, u32[]{:S(2)}) async-start(bf16[8,96,512]{2,1,0:T(8,128)(2,1)} %bitcast.8), calls=%async_computation.4 | async-start | bytes 1572864 | tf_op jit(solution)/shard_map/all_to_all | solution.py:167
  73.7 23.6 %all-to-all-done.4.refs_1_.refs_2_ = bf16[8,96,512]{2,1,0:T(8,128)(2,1)S(1)} async-done(((bf16[8,96,512]{2,1,0:T(8,128)(2,1)}), bf16[8,96,512]{2,1,0:T(8,128)(2,1)S(1)}, u32[]{:S(2)}, u32[]{:S(2)}) %all-to-all-start.4) | async-done | bytes 786464 | tf_op jit(solution)/shard_map/all_to_all | solution.py:167
  97.3 1.5 dynamic-slice_bitcast_fusion
  98.8 0.2 copy.67
  99.0 0.8 all_gather_reshape.10
  99.9 0.2 copy.68
  100.2 0.8 all_gather_reshape.11
  101.0 4.0 %collective-permute-start.1 = (bf16[8,96,512]{2,1,0:T(8,128)(2,1)S(1)}, bf16[8,96,512]{2,1,0:T(8,128)(2,1)S(1)}, u32[]{:S(2)}, u32[]{:S(2)}) collective-permute-start(bf16[8,96,512]{2,1,0:T(8,128)(2,1)S(1)} %all-to-all-done.4.refs_1_.refs_2_), channel_id=1, source_target_pairs={{0,128},{128,256},{256,384},{384,0},{1,129},{129,257},{257,385},{3... | collective-permute-start | bytes 2359304 | tf_op jit(solution)/shard_map/ppermute | solution.py:127
  105.0 1.9 collective-permute-start
  106.9 15.5 %collective-permute-done.1.refs_6_ = bf16[8,96,512]{2,1,0:T(8,128)(2,1)S(1)} collective-permute-done((bf16[8,96,512]{2,1,0:T(8,128)(2,1)S(1)}, bf16[8,96,512]{2,1,0:T(8,128)(2,1)S(1)}, u32[]{:S(2)}, u32[]{:S(2)}) %collective-permute-start.1) | collective-permute-done | bytes 786464 | tf_op jit(solution)/shard_map/ppermute | solution.py:127
  122.4 5.2 %collective-permute-start.2 = (bf16[4,96,512]{2,1,0:T(8,128)(2,1)S(1)}, bf16[4,96,512]{2,1,0:T(8,128)(2,1)S(1)}, u32[]{:S(2)}, u32[]{:S(2)}) collective-permute-start(bf16[4,96,512]{2,1,0:T(8,128)(2,1)S(1)} %slice.24), channel_id=1, source_target_pairs={{0,128},{128,256},{256,384},{384,0},{1,129},{129,257},{257,385},{3... | collective-permute-start | bytes 1179656 | tf_op jit(solution)/shard_map/ppermute | solution.py:130
  127.6 0.8 slice.25
  128.4 1.9 collective-permute-start.3
  130.3 0.6 broadcast_in_dim.25
  130.9 3.3 %all-to-all-start = ((s32[8,1,32]{2,1,0:T(1,128)}), s32[8,1,32]{2,1,0:T(1,128)S(1)}, u32[]{:S(2)}, u32[]{:S(2)}) async-start(s32[8,1,32]{2,1,0:T(1,128)} %broadcast_in_dim.25), calls=%async_computation | async-start | bytes 8192 | tf_op jit(solution)/shard_map/all_to_all | solution.py:168
  134.2 7.6 %all-to-all-done = s32[8,1,32]{2,1,0:T(1,128)S(1)} async-done(((s32[8,1,32]{2,1,0:T(1,128)}), s32[8,1,32]{2,1,0:T(1,128)S(1)}, u32[]{:S(2)}, u32[]{:S(2)}) %all-to-all-start) | async-done | bytes 1056 | tf_op jit(solution)/shard_map/all_to_all | solution.py:168
  141.7 0.5 broadcast.65
  142.3 0.7 reduce.6
  143.1 2.2 copy-done
  145.3 5.9 %shard_map.55.refs_3_ = bf16[8,96,256]{2,1,0:T(8,128)(2,1)S(1)} custom-call(s32[256]{0:T(256)S(1)} %fusion.33.index_ref, bf16[16,128,1024]{2,1,0:T(8,128)(2,1)S(1)} %copy-done, bf16[8,96,512]{2,1,0:T(8,128)(2,1)S(1)} %all-to-all-done.4.refs_1_.refs_2_, bf16[8,96,512]{2,1,0:T(8,128)(2,1)S(1)} %all-to-all-done.4.refs_1_.refs_2_, ...), custom_call_target="tpu_custom_call" | custom-call | flops 1610612736 | bytes 7340032 | tf_op jit(solution)/shard_map/pallas_call | solution.py:98
  151.2 5.1 %collective-permute-start.5 = (bf16[8,96,256]{2,1,0:T(8,128)(2,1)S(1)}, bf16[8,96,256]{2,1,0:T(8,128)(2,1)}, u32[]{:S(2)}, u32[]{:S(2)}) collective-permute-start(bf16[8,96,256]{2,1,0:T(8,128)(2,1)S(1)} %shard_map.55.refs_3_), channel_id=1, source_target_pairs={{0,128},{128,256},{256,384},{384,0},{1,129},{129,257},{257,385},{3... | collective-permute-start | bytes 1179656 | tf_op jit(solution)/shard_map/ppermute | solution.py:127
  156.3 1.9 collective-permute-start.4
  158.2 25.5 %all-gather.8.cloned.1.call-done.refs_0_.refs_1_ = bf16[16,128,1024]{2,1,0:T(8,128)(2,1)} async-done(((bf16[1,128,1024]{2,1,0:T(8,128)(2,1)}), bf16[16,128,1024]{2,1,0:T(8,128)(2,1)}) %all-gather.8.cloned.1.call-update) | async-done | bytes 4194320 | tf_op jit(solution)/shard_map/all_gather | solution.py:195
  183.7 2.2 copy-done.2
  185.9 5.9 %shard_map.56.refs_8_ = bf16[8,96,256]{2,1,0:T(8,128)(2,1)S(1)} custom-call(s32[256]{0:T(256)S(1)} %fusion.33.index_ref, bf16[16,128,1024]{2,1,0:T(8,128)(2,1)S(1)} %copy-done.2, bf16[8,96,512]{2,1,0:T(8,128)(2,1)S(1)} %all-to-all-done.4.refs_1_.refs_2_, bf16[8,96,512]{2,1,0:T(8,128)(2,1)S(1)} %all-to-all-done.4.refs_1_.refs_2_, ...), custom_call_target="tpu_custom_call" | custom-call | flops 1610612736 | bytes 7340032 | tf_op jit(solution)/shard_map/pallas_call | solution.py:98
  191.8 2.6 %collective-permute-start.9 = (bf16[8,96,256]{2,1,0:T(8,128)(2,1)S(1)}, bf16[8,96,256]{2,1,0:T(8,128)(2,1)S(1)}, u32[]{:S(2)}, u32[]{:S(2)}) collective-permute-start(bf16[8,96,256]{2,1,0:T(8,128)(2,1)S(1)} %shard_map.56.refs_8_), channel_id=1, source_target_pairs={{0,128},{128,256},{256,384},{384,0},{1,129},{129,257},{257,385},{3... | collective-permute-start | bytes 1179656 | tf_op jit(solution)/shard_map/ppermute | solution.py:127
  194.5 3.2 %collective-permute-start.8 = (bf16[8,96,256]{2,1,0:T(8,128)(2,1)S(1)}, bf16[8,96,256]{2,1,0:T(8,128)(2,1)S(1)}, u32[]{:S(2)}, u32[]{:S(2)}) collective-permute-start(bf16[8,96,256]{2,1,0:T(8,128)(2,1)S(1)} %shard_map.56.refs_8_), channel_id=1, source_target_pairs={{0,384},{128,0},{256,128},{384,256},{1,385},{129,1},{257,129},{385... | collective-permute-start | bytes 1179656 | tf_op jit(solution)/shard_map/ppermute | solution.py:128
  197.7 0.9 slice.26
  198.6 3.9 %collective-permute-start.6 = (bf16[4,96,256]{2,1,0:T(8,128)(2,1)S(1)}, bf16[4,96,256]{2,1,0:T(8,128)(2,1)S(1)}, u32[]{:S(2)}, u32[]{:S(2)}) collective-permute-start(bf16[4,96,256]{2,1,0:T(8,128)(2,1)S(1)} %slice.26), channel_id=1, source_target_pairs={{0,128},{128,256},{256,384},{384,0},{1,129},{129,257},{257,385},{3... | collective-permute-start | bytes 589832 | tf_op jit(solution)/shard_map/ppermute | solution.py:130
  202.5 0.9 slice.27
  203.4 2.0 collective-permute-start.7
  205.4 0.2 collective-permute-done.9.refs_12_
  205.7 4.9 %collective-permute-start.10 = (bf16[4,96,256]{2,1,0:T(8,128)(2,1)S(1)}, bf16[4,96,256]{2,1,0:T(8,128)(2,1)S(1)}, u32[]{:S(2)}, u32[]{:S(2)}) collective-permute-start(bf16[4,96,256]{2,1,0:T(8,128)(2,1)S(1)} %slice.28), channel_id=1, source_target_pairs={{0,128},{128,256},{256,384},{384,0},{1,129},{129,257},{257,385},{3... | collective-permute-start | bytes 589832 | tf_op jit(solution)/shard_map/ppermute | solution.py:130
  210.6 1.9 collective-permute-start.11
  212.5 0.3 collective-permute-done.7.refs_6_
  212.8 1.2 collective-permute-done.10.refs_10_
  214.0 5.4 %collective-permute-done.11.refs_11_ = bf16[4,96,256]{2,1,0:T(8,128)(2,1)S(1)} collective-permute-done((bf16[4,96,256]{2,1,0:T(8,128)(2,1)S(1)}, bf16[4,96,256]{2,1,0:T(8,128)(2,1)S(1)}, u32[]{:S(2)}, u32[]{:S(2)}) %collective-permute-start.11) | collective-permute-done | bytes 196640 | tf_op jit(solution)/shard_map/ppermute | solution.py:131
  219.4 9.7 %shard_map.57 = bf16[8,96,512]{2,1,0:T(8,128)(2,1)S(1)} custom-call(s32[256]{0:T(256)S(1)} %fusion.33.index_ref, bf16[16,128,1024]{2,1,0:T(8,128)(2,1)S(1)} %copy-done.1, bf16[16,128,1024]{2,1,0:T(8,128)(2,1)S(1)} %copy-done.3, bf16[8,96,512]{2,1,0:T(8,128)(2,1)S(1)} %all-to-all-done.4.refs_1_.refs_2_, bf16[8,96,256]{2,1,0:T(8,128)(2,1)S(1)} %shard_map.55.refs_3_, ...), custom_call_target="tpu_custom_call" | custom-call | flops 3221225472 | bytes 11534336 | tf_op jit(solution)/shard_map/pallas_call | solution.py:98
  229.1 25.1 %all_to_all.34 = bf16[8,96,512]{2,1,0:T(8,128)(2,1)S(1)} all-to-all(bf16[8,96,512]{2,1,0:T(8,128)(2,1)S(1)} %shard_map.57), channel_id=1, replica_groups=mesh['x'=4,'y'=8,'z'=8,'c'=2] {'y'}, dimensions={0} | all-to-all | bytes 1572864 | tf_op jit(solution)/shard_map/all_to_all | solution.py:206
  254.2 0.2 convert_log_fusion
  254.4 1.6 copy.69
  (43 shorter events, 0.8 us)
Async XLA Ops:
  6.5 15.3 %copy-start.5 = (bf16[512,1280]{1,0:T(8,128)(2,1)S(1)}, bf16[512,1280]{1,0:T(8,128)(2,1)}, u32[]{:S(2)}) copy-start(bf16[512,1280]{1,0:T(8,128)(2,1)} %param.5) | copy-start | bytes 3932164
  10.9 21.9 %all-to-all-start.1 = ((bf16[32,4,1280]{2,1,0:T(4,128)(2,1)}), bf16[32,4,1280]{2,1,0:T(4,128)(2,1)S(1)}, u32[]{:S(2)}, u32[]{:S(2)}) async-start(bf16[32,4,1280]{2,1,0:T(4,128)(2,1)} %reshape.81), calls=%async_computation.1 | async-start | bytes 655360 | tf_op jit(solution)/shard_map/all_to_all | solution.py:155
  21.2 76.1 %all-gather.4.cloned.1.call-start = ((), (), s32[]{:S(2)}) async-start(), calls=%async_computation.6 | async-start | bytes 1114112 | tf_op jit(solution)/shard_map/all_gather | solution.py:188
  33.9 16.3 %copy-start.4 = (bf16[512,768]{1,0:T(8,128)(2,1)S(1)}, bf16[512,768]{1,0:T(8,128)(2,1)}, u32[]{:S(2)}) copy-start(bf16[512,768]{1,0:T(8,128)(2,1)} %param.7) | copy-start | bytes 2359300
  33.9 16.3 %copy-start.6 = (f32[768]{0:T(1024)S(1)}, f32[768]{0:T(1024)}, u32[]{:S(2)}) copy-start(f32[768]{0:T(1024)} %param.6) | copy-start | bytes 9220
  70.1 27.2 %all-to-all-start.4 = ((bf16[8,96,512]{2,1,0:T(8,128)(2,1)}), bf16[8,96,512]{2,1,0:T(8,128)(2,1)S(1)}, u32[]{:S(2)}, u32[]{:S(2)}) async-start(bf16[8,96,512]{2,1,0:T(8,128)(2,1)} %bitcast.8), calls=%async_computation.4 | async-start | bytes 1572864 | tf_op jit(solution)/shard_map/all_to_all | solution.py:167
  73.6 69.4 %all-gather.6.cloned.1.call-start = ((), (), s32[]{:S(2)}) async-start(), calls=%async_computation.7 | async-start | bytes 4456448 | tf_op jit(solution)/shard_map/all_gather | solution.py:195
  99.9 83.8 %all-gather.8.cloned.1.call-start = ((), (), s32[]{:S(2)}) async-start(), calls=%async_computation.8 | async-start | bytes 4456448 | tf_op jit(solution)/shard_map/all_gather | solution.py:195
  101.0 21.4 %collective-permute-start.1 = (bf16[8,96,512]{2,1,0:T(8,128)(2,1)S(1)}, bf16[8,96,512]{2,1,0:T(8,128)(2,1)S(1)}, u32[]{:S(2)}, u32[]{:S(2)}) collective-permute-start(bf16[8,96,512]{2,1,0:T(8,128)(2,1)S(1)} %all-to-all-done.4.refs_1_.refs_2_), channel_id=1, source_target_pairs={{0,128},{128,256},{256,384},{384,0},{1,129},{129,257},{257,385},{3... | collective-permute-start | bytes 2359304 | tf_op jit(solution)/shard_map/ppermute | solution.py:127
  105.0 22.6 %collective-permute-start = (bf16[8,96,512]{2,1,0:T(8,128)(2,1)S(1)}, bf16[8,96,512]{2,1,0:T(8,128)(2,1)S(1)}, u32[]{:S(2)}, u32[]{:S(2)}) collective-permute-start(bf16[8,96,512]{2,1,0:T(8,128)(2,1)S(1)} %all-to-all-done.4.refs_1_.refs_2_), channel_id=1, source_target_pairs={{0,384},{128,0},{256,128},{384,256},{1,385},{129,1},{257,129},{385... | collective-permute-start | bytes 2359304 | tf_op jit(solution)/shard_map/ppermute | solution.py:128
  122.4 20.6 %collective-permute-start.2 = (bf16[4,96,512]{2,1,0:T(8,128)(2,1)S(1)}, bf16[4,96,512]{2,1,0:T(8,128)(2,1)S(1)}, u32[]{:S(2)}, u32[]{:S(2)}) collective-permute-start(bf16[4,96,512]{2,1,0:T(8,128)(2,1)S(1)} %slice.24), channel_id=1, source_target_pairs={{0,128},{128,256},{256,384},{384,0},{1,129},{129,257},{257,385},{3... | collective-permute-start | bytes 1179656 | tf_op jit(solution)/shard_map/ppermute | solution.py:130
  128.4 14.7 %collective-permute-start.3 = (bf16[4,96,512]{2,1,0:T(8,128)(2,1)}, bf16[4,96,512]{2,1,0:T(8,128)(2,1)S(1)}, u32[]{:S(2)}, u32[]{:S(2)}) collective-permute-start(bf16[4,96,512]{2,1,0:T(8,128)(2,1)} %slice.25), channel_id=1, source_target_pairs={{0,384},{128,0},{256,128},{384,256},{1,385},{129,1},{257,129},{385... | collective-permute-start | bytes 1179656 | tf_op jit(solution)/shard_map/ppermute | solution.py:131
  130.9 10.9 %all-to-all-start = ((s32[8,1,32]{2,1,0:T(1,128)}), s32[8,1,32]{2,1,0:T(1,128)S(1)}, u32[]{:S(2)}, u32[]{:S(2)}) async-start(s32[8,1,32]{2,1,0:T(1,128)} %broadcast_in_dim.25), calls=%async_computation | async-start | bytes 8192 | tf_op jit(solution)/shard_map/all_to_all | solution.py:168
  143.1 2.2 copy-start
  151.2 46.5 %collective-permute-start.5 = (bf16[8,96,256]{2,1,0:T(8,128)(2,1)S(1)}, bf16[8,96,256]{2,1,0:T(8,128)(2,1)}, u32[]{:S(2)}, u32[]{:S(2)}) collective-permute-start(bf16[8,96,256]{2,1,0:T(8,128)(2,1)S(1)} %shard_map.55.refs_3_), channel_id=1, source_target_pairs={{0,128},{128,256},{256,384},{384,0},{1,129},{129,257},{257,385},{3... | collective-permute-start | bytes 1179656 | tf_op jit(solution)/shard_map/ppermute | solution.py:127
  156.3 46.2 %collective-permute-start.4 = (bf16[8,96,256]{2,1,0:T(8,128)(2,1)S(1)}, bf16[8,96,256]{2,1,0:T(8,128)(2,1)}, u32[]{:S(2)}, u32[]{:S(2)}) collective-permute-start(bf16[8,96,256]{2,1,0:T(8,128)(2,1)S(1)} %shard_map.55.refs_3_), channel_id=1, source_target_pairs={{0,384},{128,0},{256,128},{384,256},{1,385},{129,1},{257,129},{385... | collective-permute-start | bytes 1179656 | tf_op jit(solution)/shard_map/ppermute | solution.py:128
  183.7 2.2 copy-start.2
  185.9 33.4 %copy-start.1 = (bf16[16,128,1024]{2,1,0:T(8,128)(2,1)S(1)}, bf16[16,128,1024]{2,1,0:T(8,128)(2,1)}, u32[]{:S(2)}) copy-start(bf16[16,128,1024]{2,1,0:T(8,128)(2,1)} %all-gather.6.cloned.1.call-done.refs_0_) | copy-start | bytes 12582916
  185.9 33.4 %copy-start.3 = (bf16[16,128,1024]{2,1,0:T(8,128)(2,1)S(1)}, bf16[16,128,1024]{2,1,0:T(8,128)(2,1)}, u32[]{:S(2)}) copy-start(bf16[16,128,1024]{2,1,0:T(8,128)(2,1)} %all-gather.8.cloned.1.call-done.refs_0_.refs_1_) | copy-start | bytes 12582916
  191.8 13.8 %collective-permute-start.9 = (bf16[8,96,256]{2,1,0:T(8,128)(2,1)S(1)}, bf16[8,96,256]{2,1,0:T(8,128)(2,1)S(1)}, u32[]{:S(2)}, u32[]{:S(2)}) collective-permute-start(bf16[8,96,256]{2,1,0:T(8,128)(2,1)S(1)} %shard_map.56.refs_8_), channel_id=1, source_target_pairs={{0,128},{128,256},{256,384},{384,0},{1,129},{129,257},{257,385},{3... | collective-permute-start | bytes 1179656 | tf_op jit(solution)/shard_map/ppermute | solution.py:127
  194.5 16.1 %collective-permute-start.8 = (bf16[8,96,256]{2,1,0:T(8,128)(2,1)S(1)}, bf16[8,96,256]{2,1,0:T(8,128)(2,1)S(1)}, u32[]{:S(2)}, u32[]{:S(2)}) collective-permute-start(bf16[8,96,256]{2,1,0:T(8,128)(2,1)S(1)} %shard_map.56.refs_8_), channel_id=1, source_target_pairs={{0,384},{128,0},{256,128},{384,256},{1,385},{129,1},{257,129},{385... | collective-permute-start | bytes 1179656 | tf_op jit(solution)/shard_map/ppermute | solution.py:128
  198.6 13.9 %collective-permute-start.6 = (bf16[4,96,256]{2,1,0:T(8,128)(2,1)S(1)}, bf16[4,96,256]{2,1,0:T(8,128)(2,1)S(1)}, u32[]{:S(2)}, u32[]{:S(2)}) collective-permute-start(bf16[4,96,256]{2,1,0:T(8,128)(2,1)S(1)} %slice.26), channel_id=1, source_target_pairs={{0,128},{128,256},{256,384},{384,0},{1,129},{129,257},{257,385},{3... | collective-permute-start | bytes 589832 | tf_op jit(solution)/shard_map/ppermute | solution.py:130
  203.4 9.3 %collective-permute-start.7 = (bf16[4,96,256]{2,1,0:T(8,128)(2,1)S(1)}, bf16[4,96,256]{2,1,0:T(8,128)(2,1)S(1)}, u32[]{:S(2)}, u32[]{:S(2)}) collective-permute-start(bf16[4,96,256]{2,1,0:T(8,128)(2,1)S(1)} %slice.27), channel_id=1, source_target_pairs={{0,384},{128,0},{256,128},{384,256},{1,385},{129,1},{257,129},{385... | collective-permute-start | bytes 589832 | tf_op jit(solution)/shard_map/ppermute | solution.py:131
  205.7 8.3 %collective-permute-start.10 = (bf16[4,96,256]{2,1,0:T(8,128)(2,1)S(1)}, bf16[4,96,256]{2,1,0:T(8,128)(2,1)S(1)}, u32[]{:S(2)}, u32[]{:S(2)}) collective-permute-start(bf16[4,96,256]{2,1,0:T(8,128)(2,1)S(1)} %slice.28), channel_id=1, source_target_pairs={{0,128},{128,256},{256,384},{384,0},{1,129},{129,257},{257,385},{3... | collective-permute-start | bytes 589832 | tf_op jit(solution)/shard_map/ppermute | solution.py:130
  210.6 8.8 %collective-permute-start.11 = (bf16[4,96,256]{2,1,0:T(8,128)(2,1)S(1)}, bf16[4,96,256]{2,1,0:T(8,128)(2,1)S(1)}, u32[]{:S(2)}, u32[]{:S(2)}) collective-permute-start(bf16[4,96,256]{2,1,0:T(8,128)(2,1)S(1)} %slice.29), channel_id=1, source_target_pairs={{0,384},{128,0},{256,128},{384,256},{1,385},{129,1},{257,129},{385... | collective-permute-start | bytes 589832 | tf_op jit(solution)/shard_map/ppermute | solution.py:131
Sparse Core Ops, SparseCore 0:
  50.4 41.8 all-gather.3
  100.0 37.8 all-gather.5
  140.1 43.6 all-gather.7

commit v4 on v3

--- a/solution.py
+++ b/solution.py
@@ -22,7 +22,6 @@
 PER = NBLK * NT
 SLOTS = TILES * 2
 SUB = 2
-PARTS = 2
 BF = jnp.bfloat16
 F32 = jnp.float32
 
@@ -112,7 +111,7 @@
             ],
         ),
         out_shape=jax.ShapeDtypeStruct((ny, classes, rows), BF),
-        compiler_params=pltpu.CompilerParams(vmem_limit_bytes=40 << 20),
+        compiler_params=pltpu.CompilerParams(vmem_limit_bytes=48 << 20),
         cost_estimate=pl.CostEstimate(
             flops=2 * ny * rows * NT * TILE * classes * 4,
             bytes_accessed=sum(w.size for w in weights) * 2 + 4 * prior.size * 2,
@@ -132,10 +131,20 @@
     return mine, after, oppa, oppb, before
 
 
+def split_terms(value):
+    terms = []
+    for scale in (0.99, 1.0, 1.0):
+        term = (value * scale).astype(BF)
+        value = value - term.astype(F32)
+        terms.append(term)
+    return terms
+
+
 def on_device(features, class_bias, logits, tile_lists, valid_counts):
     width = features.shape[1]
     rows, classes = logits.shape
-    z, core, x = lax.axis_index("z"), lax.axis_index("c"), lax.axis_index("x")
+    x, y = lax.axis_index("x"), lax.axis_index("y")
+    z, core = lax.axis_index("z"), lax.axis_index("c")
 
     owners = tile_lists.reshape(PER)
     order = jnp.arange(PER, dtype=jnp.int32)
@@ -154,19 +163,6 @@
     ).astype(BF)
     arrived = lax.all_to_all(
         outgoing.reshape(TILES, 2 * SUB, width), ("x", "y"), 0, 0, tiled=True
-    )
-
-    adjusted = logits.astype(F32) + class_bias[None, :]
-    part = jnp.sum(jnp.exp(adjusted), axis=1)
-    parts = lax.all_to_all(
-        jnp.broadcast_to(part, (NZ * NC, rows)), ("z", "c"), 0, 0, tiled=True
-    )
-    totals = jnp.sum(parts, axis=0)
-    prior = (jnp.exp(adjusted) / totals[:, None]).astype(BF)
-    prior = prior.T.reshape(NY, classes // NY, rows)
-    prior = lax.all_to_all(prior, "y", 0, 0, tiled=True)
-    lists = lax.all_to_all(
-        jnp.broadcast_to(owners, (NY, PER)), "y", 0, 0, tiled=True
     )
 
     memory = unitnorm_rows(features)
@@ -185,24 +181,46 @@
     scaled = (ALPHA * chosen / denominator).astype(BF)
     scaled = scaled.transpose(0, 2, 1, 3).reshape(NBLK, SUB, NT * TILE)
 
-    own = lax.all_gather(scaled, ("z", "c"), axis=0, tiled=False)
-    own, prior = lax.optimization_barrier((own, prior))
-    count = NBLK // PARTS // NC
-    gathered = []
-    for part in range(PARTS):
-        piece = lax.dynamic_slice_in_dim(own, (part * NC + core) * count, count, axis=1)
-        piece = piece.transpose(1, 0, 2, 3).reshape(count * QB, NT * TILE)
-        gathered.append(lax.all_gather(piece, ("y", "c"), axis=0, tiled=False))
-
-    named = lists.reshape(NY * PER)
+    part = jnp.sum(jnp.exp(logits.astype(F32) + class_bias[None, :]), axis=1)
+    high, middle, low = split_terms(part)
+    terms = jnp.concatenate([high, middle, low, jnp.zeros_like(low)])
+    piece = jnp.concatenate([scaled, terms.reshape(1, SUB, NT * TILE)])
+    own = lax.all_gather(piece, ("z", "c"), axis=0, tiled=False)
+
+    raw, _ = lax.optimization_barrier((logits, piece))
+    raw = raw.T.reshape(NY, classes // NY, rows)
+    raw = lax.all_to_all(raw, "y", 0, 0, tiled=True)
+    own, _ = lax.optimization_barrier((own, raw))
+    raw = around_x(raw)
+
+    half = NBLK // NC
+    piece = lax.dynamic_slice_in_dim(own, core * half, half, axis=1)
+    piece = piece.transpose(1, 0, 2, 3).reshape(half * QB, NT * TILE)
+    weights = lax.all_gather(piece, ("y", "c"), axis=0, tiled=False)
+
+    terms = jnp.sum(own[:, NBLK].astype(F32), axis=0).reshape(4, rows)
+    totals = terms[0] + terms[1] + terms[2]
+    known = jnp.concatenate([totals, owners.astype(F32), jnp.zeros((128 - PER,), F32)])
+    known = lax.all_to_all(
+        jnp.broadcast_to(known, (TILES,) + known.shape), ("x", "y"), 0, 0, tiled=True
+    )
+    known = known.reshape(NX, NY, -1)
+    known = lax.dynamic_slice_in_dim(jnp.concatenate([known, known]), x, NX, axis=0)
+    totals = known[:, :, :rows]
+
+    bias = lax.dynamic_slice_in_dim(class_bias.reshape(NY, classes // NY), y, 1, axis=0)
+    bias = bias.reshape(1, classes // NY, 1)
+    half = NY // 2
+    sums = totals[0], totals[1], totals[2, :half], totals[2, half:], totals[3]
+    priors = tuple(
+        (jnp.exp(r.astype(F32) + bias) / t[:, None, :]).astype(BF) for r, t in zip(raw, sums)
+    )
+
+    named = known[0, :, rows : rows + PER].astype(jnp.int32).reshape(NY * PER)
     index = (named // NY - x) % NX * NY + named % NY
 
-    priors = around_x(prior)
-    each = [
-        sweep(index, [w], part * NBLK // PARTS, prior, part, [priors])
-        for part, w in enumerate(gathered)
-    ]
-    spread = sweep(index, gathered, 0, prior, 0, [around_x(labels) for labels in each])
+    labels = sweep(index, [weights], 0, priors[0], 0, [priors])
+    spread = sweep(index, [weights], 0, priors[0], 0, [around_x(labels)])
     spread = lax.all_to_all(spread, "y", 0, 0, tiled=True)
     return jnp.log(spread.reshape(classes, rows).T.astype(F32))
 

time: 264 us -> 251 us (0.951)
  blocking collectives: 58.1 us -> 25.8 us
  waiting for transfers between devices: 89.9 us -> 112 us
  local copies, waits for them, and re-layouts: 18.8 us -> 13.5 us
  other arithmetic: 3.23 us -> 7.13 us
    all_to_all x2 -> x0, blocking collectives: 33 us -> none  [the longest x1 17.9 us: on_device(): lax.all_to_all(jnp.broadcast_to(part, (NZ * NC, rows)), ('z', 'c'), 0, 0,...]
    all_to_all x2 -> x3, starting transfers between devices: 6.83 us -> 20.1 us  [the longest x1 9.95 us: on_device(): lax.all_to_all(jnp.broadcast_to(known, (TILES,) + known.shape), ('x', 'y'...]
    all_gather x3 -> x2, waiting for transfers between devices: 25.5 us -> 32.8 us  [the longest x1 16.6 us: on_device(): weights = lax.all_gather(piece, ('y', 'c'), axis=0, tiled=False)]
    ppermute x3 -> x2, waiting for transfers between devices: 1.21 us -> 8.18 us  [around_x(): oppa = lax.ppermute(before[:half], 'x', forward)]
    ppermute x3 -> x2, starting transfers between devices: 11.7 us -> 4.88 us  [around_x(): before = lax.ppermute(mine, 'x', forward)]
    ppermute x3 -> x2, starting transfers between devices: 13.9 us -> 7.22 us  [around_x(): oppa = lax.ppermute(before[:half], 'x', forward)]
    ppermute x3 -> x2, waiting for transfers between devices: 5.63 us -> 10.4 us  [around_x(): oppb = lax.ppermute(after[half:], 'x', backward)]
    ppermute x3 -> x2, waiting for transfers between devices: 15.7 us -> 20 us  [around_x(): before = lax.ppermute(mine, 'x', forward)]
  transfers between devices with their start and end apart: 18 -> 14, of which waited for: 9 -> 12; matrix products, arithmetic and copies ran while one was open for 3% -> 4% of each run, Pallas kernels for 4% -> 0%
where the time goes in v4:
time: 251 us; the launch traced here: 250 us
  waiting for transfers between devices  112 us (45%)
  starting transfers between devices  53.6 us (21%)
  blocking collectives  25.8 us (10%)
  Pallas kernels  22.2 us (9%)
  between operations  14.4 us (6%)
  local copies, waits for them, and re-layouts  13.5 us (5%)
  other arithmetic  7.13 us (3%)
    all_to_all x1, blocking collectives, on_device(): spread = lax.all_to_all(spread, 'y', 0, 0, tiled=True)  25.8 us
    pallas_call x2, Pallas kernels, sweep(): pl.pallas_call(functools.partial(sweep_kernel, first, (len(weights), len(...  22.2 us
    all_to_all x1, waiting for transfers between devices, on_device(): raw = lax.all_to_all(raw, 'y', 0, 0, tiled=True)  21.1 us
    ppermute x2, waiting for transfers between devices, around_x(): before = lax.ppermute(mine, 'x', forward)  20 us
    all_gather x1, waiting for transfers between devices, on_device(): weights = lax.all_gather(piece, ('y', 'c'), axis=0, tiled=False)  16.6 us
    all_gather x1, waiting for transfers between devices, on_device(): own = lax.all_gather(piece, ('z', 'c'), axis=0, tiled=False)  16.2 us
    ppermute x2, waiting for transfers between devices, around_x(): oppb = lax.ppermute(after[half:], 'x', backward)  10.4 us
    all_to_all x1, waiting for transfers between devices, on_device(): lax.all_to_all(outgoing.reshape(TILES, 2 * SUB, width), ('x', 'y'), 0, 0,...  10.3 us
  transfers between devices with their start and end apart: 14, of which 12 were waited for; matrix products, arithmetic and copies ran while one was open for 4% of the time, Pallas kernels for 0%

profile of v4, /device:TPU:6, one launch (start us, length us, event | category | flops | bytes accessed | tf_op | source)
XLA Modules:
  0.0 249.6 jit_solution(12027010836281861998)
XLA Ops:
  6.5 1.2 constant_dynamic-slice_fusion.1
  7.8 0.8 copy.65
  8.5 0.1 eq.31
  8.6 0.2 convert_reduce_fusion.1
  8.8 0.1 reduce_sum.69
  8.9 0.1 copy.66
  9.0 0.7 multiply_add_fusion
  9.7 0.1 fusion.29
  9.7 0.3 convolution_convert_fusion
  10.0 0.9 reshape.97
  11.0 10.2 %all-to-all-start = ((bf16[32,4,1280]{2,1,0:T(4,128)(2,1)}), bf16[32,4,1280]{2,1,0:T(4,128)(2,1)S(1)}, u32[]{:S(2)}, u32[]{:S(2)}) async-start(bf16[32,4,1280]{2,1,0:T(4,128)(2,1)} %reshape.97), calls=%async_computation | async-start | bytes 655360 | tf_op jit(solution)/shard_map/all_to_all | solution.py:164
  21.9 0.3 exponential_reduce_fusion
  22.2 0.3 fusion
  22.6 10.3 %all-to-all-done = bf16[32,4,1280]{2,1,0:T(4,128)(2,1)S(1)} async-done(((bf16[32,4,1280]{2,1,0:T(4,128)(2,1)}), bf16[32,4,1280]{2,1,0:T(4,128)(2,1)S(1)}, u32[]{:S(2)}, u32[]{:S(2)}) %all-to-all-start) | async-done | bytes 327712 | tf_op jit(solution)/shard_map/all_to_all | solution.py:164
  32.9 0.2 multiply_reduce_fusion
  33.1 0.1 rsqrt.20
  33.3 0.7 fusion.16
  34.0 0.7 reshape.98
  34.7 6.6 %all-to-all-start.1 = ((bf16[32,4,512]{2,1,0:T(4,128)(2,1)}), bf16[32,4,512]{2,1,0:T(4,128)(2,1)S(1)}, u32[]{:S(2)}, u32[]{:S(2)}) async-start(bf16[32,4,512]{2,1,0:T(4,128)(2,1)} %reshape.98), calls=%async_computation.1 | async-start | bytes 262144 | tf_op jit(solution)/shard_map/all_to_all | solution.py:175
  41.4 8.5 %all-to-all-done.1 = bf16[32,4,512]{2,1,0:T(4,128)(2,1)S(1)} async-done(((bf16[32,4,512]{2,1,0:T(4,128)(2,1)}), bf16[32,4,512]{2,1,0:T(4,128)(2,1)S(1)}, u32[]{:S(2)}, u32[]{:S(2)}) %all-to-all-start.1) | async-done | bytes 131104 | tf_op jit(solution)/shard_map/all_to_all | solution.py:175
  49.8 0.1 reshape.99
  49.9 0.3 fusion.37
  50.2 0.1 fusion.24
  50.4 0.7 copy.70
  51.1 1.2 copy.71
  52.2 3.5 %all-to-all-start.2 = ((bf16[8,96,512]{2,1,0:T(8,128)(2,1)}), bf16[8,96,512]{2,1,0:T(8,128)(2,1)S(1)}, u32[]{:S(2)}, u32[]{:S(2)}) async-start(bf16[8,96,512]{2,1,0:T(8,128)(2,1)} %bitcast.9), calls=%async_computation.2 | async-start | bytes 1572864 | tf_op jit(solution)/shard_map/all_to_all | solution.py:192
  55.8 0.0 all-gather.4.cloned.1.call-start
  55.9 21.1 %all-to-all-done.2 = bf16[8,96,512]{2,1,0:T(8,128)(2,1)S(1)} async-done(((bf16[8,96,512]{2,1,0:T(8,128)(2,1)}), bf16[8,96,512]{2,1,0:T(8,128)(2,1)S(1)}, u32[]{:S(2)}, u32[]{:S(2)}) %all-to-all-start.2) | async-done | bytes 786464 | tf_op jit(solution)/shard_map/all_to_all | solution.py:192
  77.0 16.2 %all-gather.6.cloned.1.call-done = bf16[272,2,1024]{2,1,0:T(2,128)(2,1)} async-done(((bf16[17,2,1024]{2,1,0:T(2,128)(2,1)}), bf16[272,2,1024]{2,1,0:T(2,128)(2,1)}) %all-gather.6.cloned.1.call-update) | async-done | bytes 1114128 | tf_op jit(solution)/shard_map/all_gather | solution.py:188
  93.2 1.4 dynamic-slice_bitcast_fusion
  94.7 0.4 copy.72
  95.0 1.0 all_gather_reshape.3
  96.1 2.4 collective-permute-start.1
  98.5 3.4 %collective-permute-start = (bf16[8,96,512]{2,1,0:T(8,128)(2,1)S(1)}, bf16[8,96,512]{2,1,0:T(8,128)(2,1)S(1)}, u32[]{:S(2)}, u32[]{:S(2)}) collective-permute-start(bf16[8,96,512]{2,1,0:T(8,128)(2,1)S(1)} %all-to-all-done.2), channel_id=1, source_target_pairs={{0,384},{128,0},{256,128},{384,256},{1,385},{129,1},{257,129},{385... | collective-permute-start | bytes 2359304 | tf_op jit(solution)/shard_map/ppermute | solution.py:127
  102.0 0.9 convert_reduce_fusion
  102.9 0.1 pad_maximum_fusion.1
  103.0 0.7 broadcast_in_dim.28
  103.7 9.9 %all-to-all-start.3 = ((f32[32,1,640]{2,1,0:T(1,128)}), f32[32,1,640]{2,1,0:T(1,128)S(1)}, u32[]{:S(2)}, u32[]{:S(2)}) async-start(f32[32,1,640]{2,1,0:T(1,128)} %broadcast_in_dim.28), calls=%async_computation.3 | async-start | bytes 163840 | tf_op jit(solution)/shard_map/all_to_all | solution.py:204
  113.6 0.1 reshape.105
  113.7 4.2 %collective-permute-done.1 = bf16[8,96,512]{2,1,0:T(8,128)(2,1)S(1)} collective-permute-done((bf16[8,96,512]{2,1,0:T(8,128)(2,1)S(1)}, bf16[8,96,512]{2,1,0:T(8,128)(2,1)S(1)}, u32[]{:S(2)}, u32[]{:S(2)}) %collective-permute-start.1) | collective-permute-done | bytes 786464 | tf_op jit(solution)/shard_map/ppermute | solution.py:126
  118.0 3.5 %collective-permute-start.2 = (bf16[4,96,512]{2,1,0:T(8,128)(2,1)S(1)}, bf16[4,96,512]{2,1,0:T(8,128)(2,1)}, u32[]{:S(2)}, u32[]{:S(2)}) collective-permute-start(bf16[4,96,512]{2,1,0:T(8,128)(2,1)S(1)} %slice.68), channel_id=1, source_target_pairs={{0,128},{128,256},{256,384},{384,0},{1,129},{129,257},{257,385},{3... | collective-permute-start | bytes 1179656 | tf_op jit(solution)/shard_map/ppermute | solution.py:129
  121.5 0.3 collective-permute-done
  121.9 0.8 slice.70
  122.7 2.1 collective-permute-start.3
  124.9 0.1 convert_element_type.127
  125.0 0.5 copy-done.4
  125.5 2.4 divide_convert_fusion
  127.9 0.8 slice_bitcast_fusion.3
  128.7 1.7 collective-permute-done.2
  130.4 5.7 %collective-permute-done.3 = bf16[4,96,512]{2,1,0:T(8,128)(2,1)} collective-permute-done((bf16[4,96,512]{2,1,0:T(8,128)(2,1)}, bf16[4,96,512]{2,1,0:T(8,128)(2,1)}, u32[]{:S(2)}, u32[]{:S(2)}) %collective-permute-start.3) | collective-permute-done | bytes 393248 | tf_op jit(solution)/shard_map/ppermute | solution.py:130
  136.2 1.5 divide_convert_fusion.3
  137.7 16.6 %all-gather.4.cloned.1.call-done.refs_0_ = bf16[16,256,1024]{2,1,0:T(8,128)(2,1)} async-done(((bf16[1,256,1024]{2,1,0:T(8,128)(2,1)}), bf16[16,256,1024]{2,1,0:T(8,128)(2,1)}) %all-gather.4.cloned.1.call-update) | async-done | bytes 8388624 | tf_op jit(solution)/shard_map/all_gather | solution.py:199
  154.3 11.1 %shard_map.55.refs_2_ = bf16[8,96,512]{2,1,0:T(8,128)(2,1)S(1)} custom-call(s32[256]{0:T(256)S(1)} %fusion.33.index_ref, bf16[16,256,1024]{2,1,0:T(8,128)(2,1)} %all-gather.4.cloned.1.call-done.refs_0_, bf16[8,96,512]{2,1,0:T(8,128)(2,1)S(1)} %get-tuple-element.19.refs_1_.refs_2_, bf16[8,96,512]{2,1,0:T(8,128)(2,1)S(1)} %get-tuple-element.19.refs_1_.refs_2_, ...), custom_call_target="tpu_custom_call" | custom-call | flops 3221225472 | bytes 11534336 | tf_op jit(solution)/shard_map/pallas_call | solution.py:97
  165.4 2.5 collective-permute-start.5
  167.8 3.4 %collective-permute-start.4 = (bf16[8,96,512]{2,1,0:T(8,128)(2,1)S(1)}, bf16[8,96,512]{2,1,0:T(8,128)(2,1)S(1)}, u32[]{:S(2)}, u32[]{:S(2)}) collective-permute-start(bf16[8,96,512]{2,1,0:T(8,128)(2,1)S(1)} %shard_map.55.refs_2_), channel_id=1, source_target_pairs={{0,384},{128,0},{256,128},{384,256},{1,385},{129,1},{257,129},{385... | collective-permute-start | bytes 2359304 | tf_op jit(solution)/shard_map/ppermute | solution.py:127
  171.2 15.7 %collective-permute-done.5.refs_6_ = bf16[8,96,512]{2,1,0:T(8,128)(2,1)S(1)} collective-permute-done((bf16[8,96,512]{2,1,0:T(8,128)(2,1)S(1)}, bf16[8,96,512]{2,1,0:T(8,128)(2,1)S(1)}, u32[]{:S(2)}, u32[]{:S(2)}) %collective-permute-start.5) | collective-permute-done | bytes 786464 | tf_op jit(solution)/shard_map/ppermute | solution.py:126
  187.0 3.7 %collective-permute-start.6 = (bf16[4,96,512]{2,1,0:T(8,128)(2,1)S(1)}, bf16[4,96,512]{2,1,0:T(8,128)(2,1)S(1)}, u32[]{:S(2)}, u32[]{:S(2)}) collective-permute-start(bf16[4,96,512]{2,1,0:T(8,128)(2,1)S(1)} %slice.73), channel_id=1, source_target_pairs={{0,128},{128,256},{256,384},{384,0},{1,129},{129,257},{257,385},{3... | collective-permute-start | bytes 1179656 | tf_op jit(solution)/shard_map/ppermute | solution.py:129
  190.7 2.2 collective-permute-start.7
  192.9 6.4 %collective-permute-done.6.refs_4_ = bf16[4,96,512]{2,1,0:T(8,128)(2,1)S(1)} collective-permute-done((bf16[4,96,512]{2,1,0:T(8,128)(2,1)S(1)}, bf16[4,96,512]{2,1,0:T(8,128)(2,1)S(1)}, u32[]{:S(2)}, u32[]{:S(2)}) %collective-permute-start.6) | collective-permute-done | bytes 393248 | tf_op jit(solution)/shard_map/ppermute | solution.py:129
  199.3 4.7 %collective-permute-done.7.refs_5_ = bf16[4,96,512]{2,1,0:T(8,128)(2,1)S(1)} collective-permute-done((bf16[4,96,512]{2,1,0:T(8,128)(2,1)S(1)}, bf16[4,96,512]{2,1,0:T(8,128)(2,1)S(1)}, u32[]{:S(2)}, u32[]{:S(2)}) %collective-permute-start.7) | collective-permute-done | bytes 393248 | tf_op jit(solution)/shard_map/ppermute | solution.py:130
  204.0 11.1 %shard_map.56 = bf16[8,96,512]{2,1,0:T(8,128)(2,1)S(1)} custom-call(s32[256]{0:T(256)S(1)} %fusion.33.index_ref, bf16[16,256,1024]{2,1,0:T(8,128)(2,1)} %all-gather.4.cloned.1.call-done.refs_0_, bf16[8,96,512]{2,1,0:T(8,128)(2,1)S(1)} %get-tuple-element.19.refs_1_.refs_2_, bf16[8,96,512]{2,1,0:T(8,128)(2,1)S(1)} %shard_map.55.refs_2_, ...), custom_call_target="tpu_custom_call" | custom-call | flops 3221225472 | bytes 11534336 | tf_op jit(solution)/shard_map/pallas_call | solution.py:97
  215.1 25.8 %all_to_all.26 = bf16[8,96,512]{2,1,0:T(8,128)(2,1)S(1)} all-to-all(bf16[8,96,512]{2,1,0:T(8,128)(2,1)S(1)} %shard_map.56), channel_id=1, replica_groups=mesh['x'=4,'y'=8,'z'=8,'c'=2] {'y'}, dimensions={0} | all-to-all | bytes 1572864 | tf_op jit(solution)/shard_map/all_to_all | solution.py:224
  240.9 0.2 convert_log_fusion
  241.1 1.6 copy.73
  (41 shorter events, 0.4 us)
Async XLA Ops:
  6.5 15.7 %copy-start.3 = (bf16[512,1280]{1,0:T(8,128)(2,1)S(1)}, bf16[512,1280]{1,0:T(8,128)(2,1)}, u32[]{:S(2)}) copy-start(bf16[512,1280]{1,0:T(8,128)(2,1)} %param.5) | copy-start | bytes 3932164
  6.5 15.3 %copy-start.5 = (f32[768]{0:T(1024)S(1)}, f32[768]{0:T(1024)}, u32[]{:S(2)}) copy-start(f32[768]{0:T(1024)} %param.6) | copy-start | bytes 9220
  6.5 15.3 %copy-start = (bf16[512,768]{1,0:T(8,128)(2,1)S(1)}, bf16[512,768]{1,0:T(8,128)(2,1)}, u32[]{:S(2)}) copy-start(bf16[512,768]{1,0:T(8,128)(2,1)} %param.7) | copy-start | bytes 2359300
  11.0 21.9 %all-to-all-start = ((bf16[32,4,1280]{2,1,0:T(4,128)(2,1)}), bf16[32,4,1280]{2,1,0:T(4,128)(2,1)S(1)}, u32[]{:S(2)}, u32[]{:S(2)}) async-start(bf16[32,4,1280]{2,1,0:T(4,128)(2,1)} %reshape.97), calls=%async_computation | async-start | bytes 655360 | tf_op jit(solution)/shard_map/all_to_all | solution.py:164
  34.7 15.1 %all-to-all-start.1 = ((bf16[32,4,512]{2,1,0:T(4,128)(2,1)}), bf16[32,4,512]{2,1,0:T(4,128)(2,1)S(1)}, u32[]{:S(2)}, u32[]{:S(2)}) async-start(bf16[32,4,512]{2,1,0:T(4,128)(2,1)} %reshape.98), calls=%async_computation.1 | async-start | bytes 262144 | tf_op jit(solution)/shard_map/all_to_all | solution.py:175
  41.3 52.0 %all-gather.6.cloned.1.call-start = ((), (), s32[]{:S(2)}) async-start(), calls=%async_computation.6 | async-start | bytes 1183744 | tf_op jit(solution)/shard_map/all_gather | solution.py:188
  52.2 24.8 %all-to-all-start.2 = ((bf16[8,96,512]{2,1,0:T(8,128)(2,1)}), bf16[8,96,512]{2,1,0:T(8,128)(2,1)S(1)}, u32[]{:S(2)}, u32[]{:S(2)}) async-start(bf16[8,96,512]{2,1,0:T(8,128)(2,1)} %bitcast.9), calls=%async_computation.2 | async-start | bytes 1572864 | tf_op jit(solution)/shard_map/all_to_all | solution.py:192
  55.8 98.4 %all-gather.4.cloned.1.call-start = ((), (), s32[]{:S(2)}) async-start(), calls=%async_computation.5 | async-start | bytes 8912896 | tf_op jit(solution)/shard_map/all_gather | solution.py:199
  96.1 21.9 %collective-permute-start.1 = (bf16[8,96,512]{2,1,0:T(8,128)(2,1)S(1)}, bf16[8,96,512]{2,1,0:T(8,128)(2,1)S(1)}, u32[]{:S(2)}, u32[]{:S(2)}) collective-permute-start(bf16[8,96,512]{2,1,0:T(8,128)(2,1)S(1)} %all-to-all-done.2), channel_id=1, source_target_pairs={{0,128},{128,256},{256,384},{384,0},{1,129},{129,257},{257,385},{3... | collective-permute-start | bytes 2359304 | tf_op jit(solution)/shard_map/ppermute | solution.py:126
  98.5 23.3 %collective-permute-start = (bf16[8,96,512]{2,1,0:T(8,128)(2,1)S(1)}, bf16[8,96,512]{2,1,0:T(8,128)(2,1)S(1)}, u32[]{:S(2)}, u32[]{:S(2)}) collective-permute-start(bf16[8,96,512]{2,1,0:T(8,128)(2,1)S(1)} %all-to-all-done.2), channel_id=1, source_target_pairs={{0,384},{128,0},{256,128},{384,256},{1,385},{129,1},{257,129},{385... | collective-permute-start | bytes 2359304 | tf_op jit(solution)/shard_map/ppermute | solution.py:127
  103.7 21.2 %all-to-all-start.3 = ((f32[32,1,640]{2,1,0:T(1,128)}), f32[32,1,640]{2,1,0:T(1,128)S(1)}, u32[]{:S(2)}, u32[]{:S(2)}) async-start(f32[32,1,640]{2,1,0:T(1,128)} %broadcast_in_dim.28), calls=%async_computation.3 | async-start | bytes 163840 | tf_op jit(solution)/shard_map/all_to_all | solution.py:204
  118.0 7.1 %copy-start.1 = (bf16[8,96,512]{2,1,0:T(8,128)(2,1)}, bf16[8,96,512]{2,1,0:T(8,128)(2,1)S(1)}, u32[]{:S(2)}) copy-start(bf16[8,96,512]{2,1,0:T(8,128)(2,1)S(1)} %collective-permute-done.1) | copy-start | bytes 2359300
  118.0 12.5 %collective-permute-start.2 = (bf16[4,96,512]{2,1,0:T(8,128)(2,1)S(1)}, bf16[4,96,512]{2,1,0:T(8,128)(2,1)}, u32[]{:S(2)}, u32[]{:S(2)}) collective-permute-start(bf16[4,96,512]{2,1,0:T(8,128)(2,1)S(1)} %slice.68), channel_id=1, source_target_pairs={{0,128},{128,256},{256,384},{384,0},{1,129},{129,257},{257,385},{3... | collective-permute-start | bytes 1179656 | tf_op jit(solution)/shard_map/ppermute | solution.py:129
  121.9 3.1 %copy-start.2 = (bf16[8,96,512]{2,1,0:T(8,128)(2,1)}, bf16[8,96,512]{2,1,0:T(8,128)(2,1)S(1)}, u32[]{:S(2)}) copy-start(bf16[8,96,512]{2,1,0:T(8,128)(2,1)S(1)} %collective-permute-done) | copy-start | bytes 2359300
  122.7 13.5 %collective-permute-start.3 = (bf16[4,96,512]{2,1,0:T(8,128)(2,1)}, bf16[4,96,512]{2,1,0:T(8,128)(2,1)}, u32[]{:S(2)}, u32[]{:S(2)}) collective-permute-start(bf16[4,96,512]{2,1,0:T(8,128)(2,1)} %slice.70), channel_id=1, source_target_pairs={{0,384},{128,0},{256,128},{384,256},{1,385},{129,1},{257,129},{385... | collective-permute-start | bytes 1179656 | tf_op jit(solution)/shard_map/ppermute | solution.py:130
  124.9 0.6 copy-start.4
  165.4 21.6 %collective-permute-start.5 = (bf16[8,96,512]{2,1,0:T(8,128)(2,1)S(1)}, bf16[8,96,512]{2,1,0:T(8,128)(2,1)S(1)}, u32[]{:S(2)}, u32[]{:S(2)}) collective-permute-start(bf16[8,96,512]{2,1,0:T(8,128)(2,1)S(1)} %shard_map.55.refs_2_), channel_id=1, source_target_pairs={{0,128},{128,256},{256,384},{384,0},{1,129},{129,257},{257,385},{3... | collective-permute-start | bytes 2359304 | tf_op jit(solution)/shard_map/ppermute | solution.py:126
  167.8 22.8 %collective-permute-start.4 = (bf16[8,96,512]{2,1,0:T(8,128)(2,1)S(1)}, bf16[8,96,512]{2,1,0:T(8,128)(2,1)S(1)}, u32[]{:S(2)}, u32[]{:S(2)}) collective-permute-start(bf16[8,96,512]{2,1,0:T(8,128)(2,1)S(1)} %shard_map.55.refs_2_), channel_id=1, source_target_pairs={{0,384},{128,0},{256,128},{384,256},{1,385},{129,1},{257,129},{385... | collective-permute-start | bytes 2359304 | tf_op jit(solution)/shard_map/ppermute | solution.py:127
  187.0 12.3 %collective-permute-start.6 = (bf16[4,96,512]{2,1,0:T(8,128)(2,1)S(1)}, bf16[4,96,512]{2,1,0:T(8,128)(2,1)S(1)}, u32[]{:S(2)}, u32[]{:S(2)}) collective-permute-start(bf16[4,96,512]{2,1,0:T(8,128)(2,1)S(1)} %slice.73), channel_id=1, source_target_pairs={{0,128},{128,256},{256,384},{384,0},{1,129},{129,257},{257,385},{3... | collective-permute-start | bytes 1179656 | tf_op jit(solution)/shard_map/ppermute | solution.py:129
  190.7 13.3 %collective-permute-start.7 = (bf16[4,96,512]{2,1,0:T(8,128)(2,1)S(1)}, bf16[4,96,512]{2,1,0:T(8,128)(2,1)S(1)}, u32[]{:S(2)}, u32[]{:S(2)}) collective-permute-start(bf16[4,96,512]{2,1,0:T(8,128)(2,1)S(1)} %slice.74), channel_id=1, source_target_pairs={{0,384},{128,0},{256,128},{384,256},{1,385},{129,1},{257,129},{385... | collective-permute-start | bytes 1179656 | tf_op jit(solution)/shard_map/ppermute | solution.py:130
Sparse Core Ops, SparseCore 0:
  51.2 41.9 all-gather.5
  96.2 57.9 all-gather.3

commit v5 on v1

--- a/solution.py
+++ b/solution.py
@@ -32,7 +32,7 @@
     return (wide * scale / math.sqrt(wide.shape[-1])).astype(BF)
 
 
-def sweep_kernel(index_ref, w_ref, prior_ref, own, after, oppa, oppb, before, out_ref, held, sems):
+def sweep_kernel(index_ref, mine_ref, other_ref, prior_ref, own, after, oppa, oppb, before, out_ref, held, sems):
     y = pl.program_id(0)
 
     @pl.when(y == 0)
@@ -54,19 +54,19 @@
         for copy in copies:
             copy.wait()
 
+    first_core = index_ref[NY * PER] == 0
     classes = out_ref.shape[1]
     lanes = lax.broadcasted_iota(jnp.int32, (classes, 128), 1) // QB
     for group in range(NBLK // 4):
         total = None
         for k in range(NT):
-            weights = jnp.concatenate(
-                [
-                    w_ref[c, pl.ds((4 * group + b) * ROWS_C, ROWS_C), pl.ds(k * TILE, TILE)]
-                    for b in range(4)
-                    for c in range(NC)
-                ],
-                axis=0,
-            )
+            rows = []
+            for b in range(4):
+                at = pl.ds((4 * group + b) * ROWS_C, ROWS_C), pl.ds(k * TILE, TILE)
+                mine, other = mine_ref[0, *at], other_ref[0, *at]
+                rows.append(jnp.where(first_core, mine, other))
+                rows.append(jnp.where(first_core, other, mine))
+            weights = jnp.concatenate(rows, axis=0)
             labels = jnp.concatenate(
                 [held[index_ref[y * PER + (4 * group + b) * NT + k]] for b in range(4)], axis=0
             )
@@ -82,32 +82,30 @@
         out_ref[0, :, at] = (picked + (1.0 - ALPHA) * prior).astype(BF)
 
 
-def sweep(index, weights, prior, pieces):
+def sweep(index, mine, other, prior, pieces):
     ny, classes, rows = prior.shape
+    by_y = lambda array: pl.BlockSpec((1,) + array.shape[1:], lambda y, _: (y, 0, 0))
     return pl.pallas_call(
         sweep_kernel,
         grid_spec=pltpu.PrefetchScalarGridSpec(
             num_scalar_prefetch=1,
             grid=(ny,),
-            in_specs=[
-                pl.BlockSpec((NC,) + weights.shape[1:], lambda y, _: (y, 0, 0)),
-                pl.BlockSpec((1, classes, rows), lambda y, _: (y, 0, 0)),
-            ]
+            in_specs=[by_y(mine), by_y(other), by_y(prior)]
             + [pl.BlockSpec(memory_space=pl.ANY)] * len(pieces),
-            out_specs=pl.BlockSpec((1, classes, rows), lambda y, _: (y, 0, 0)),
+            out_specs=by_y(prior),
             scratch_shapes=[
                 pltpu.VMEM((TILES, classes, rows), BF),
                 pltpu.SemaphoreType.DMA((len(pieces),)),
             ],
         ),
         out_shape=jax.ShapeDtypeStruct(prior.shape, BF),
-        compiler_params=pltpu.CompilerParams(vmem_limit_bytes=24 << 20),
+        compiler_params=pltpu.CompilerParams(vmem_limit_bytes=40 << 20),
         cost_estimate=pl.CostEstimate(
             flops=2 * ny * rows * NT * TILE * classes * 4,
-            bytes_accessed=weights.size * 2 + 4 * prior.size * 2,
+            bytes_accessed=2 * mine.size * 2 + 4 * prior.size * 2,
             transcendentals=0,
         ),
-    )(index, weights, prior, *pieces)
+    )(index, mine, other, prior, *pieces)
 
 
 def around_x(mine):
@@ -121,10 +119,23 @@
     return mine, after, oppa, oppb, before
 
 
+def split_terms(value):
+    terms = []
+    for scale in (0.99, 1.0, 1.0):
+        term = (value * scale).astype(BF)
+        value = value - term.astype(F32)
+        terms.append(term)
+    return terms
+
+
 def on_device(features, class_bias, logits, tile_lists, valid_counts):
     width = features.shape[1]
     rows, classes = logits.shape
-    z, core, x = lax.axis_index("z"), lax.axis_index("c"), lax.axis_index("x")
+    x, y = lax.axis_index("x"), lax.axis_index("y")
+    z, core = lax.axis_index("z"), lax.axis_index("c")
+
+    raw = logits.T.reshape(NY, classes // NY, rows)
+    raw = lax.all_gather(raw, "y", axis=0, tiled=False)
 
     owners = tile_lists.reshape(PER)
     order = jnp.arange(PER, dtype=jnp.int32)
@@ -144,16 +155,6 @@
     arrived = lax.all_to_all(
         outgoing.reshape(TILES, 2 * SUB, width), ("x", "y"), 0, 0, tiled=True
     )
-
-    adjusted = logits.astype(F32) + class_bias[None, :]
-    part = jnp.sum(jnp.exp(adjusted), axis=1)
-    parts = lax.all_to_all(
-        jnp.broadcast_to(part, (NZ * NC, rows)), ("z", "c"), 0, 0, tiled=True
-    )
-    totals = jnp.sum(parts, axis=0)
-    prior = (jnp.exp(adjusted) / totals[:, None]).astype(BF)
-    prior = prior.T.reshape(NY, classes // NY, rows)
-    prior = lax.all_to_all(prior, "y", 0, 0, tiled=True)
 
     memory = unitnorm_rows(features)
     queries = unitnorm_rows(arrived.reshape(SLOTS * SUB, width))
@@ -171,20 +172,49 @@
     scaled = (ALPHA * chosen / denominator).astype(BF)
     scaled = scaled.transpose(0, 2, 1, 3).reshape(NBLK, SUB, NT * TILE)
 
+    part = jnp.sum(jnp.exp(logits.astype(F32) + class_bias[None, :]), axis=1)
+    high, middle, low = split_terms(part)
+    terms = jnp.concatenate([high, middle, low, jnp.zeros_like(low)])
+    piece = jnp.concatenate([scaled, terms.reshape(1, SUB, NT * TILE)])
     over_z = lax.all_to_all(
-        jnp.broadcast_to(scaled, (NZ,) + scaled.shape), "z", 0, 0, tiled=True
-    )
-    over_z = over_z.transpose(1, 0, 2, 3).reshape(NBLK * ROWS_C, NT * TILE)
-    names = jnp.zeros((16, NT * TILE), BF).at[0, :PER].set(owners.astype(BF))
-    piece = jnp.concatenate([over_z, names], axis=0)
-    weights = lax.all_gather(piece, ("y", "c"), axis=0, tiled=False)
-
-    named = weights[::NC, NBLK * ROWS_C, :PER].astype(jnp.int32)
-    index = ((named // NY - x) % NX) * NY + named % NY
-    index = index.reshape(NY * PER)
-
-    labels = sweep(index, weights, prior, around_x(prior))
-    spread = sweep(index, weights, prior, around_x(labels))
+        jnp.broadcast_to(piece, (NZ,) + piece.shape), "z", 0, 0, tiled=True
+    )
+
+    raw, over_z = lax.optimization_barrier((raw, over_z))
+    piece = over_z[:, :NBLK].transpose(1, 0, 2, 3).reshape(NBLK * ROWS_C, NT * TILE)
+    weights = lax.all_gather(piece, "y", axis=0, tiled=False)
+
+    raw = lax.dynamic_index_in_dim(raw, y, axis=1, keepdims=False)
+    raw = around_x(raw)
+
+    terms = jnp.sum(over_z[:, NBLK].astype(F32), axis=0).reshape(4, rows)
+    totals = terms[0] + terms[1] + terms[2]
+    totals = totals + lax.ppermute(totals, "c", [(0, 1), (1, 0)])
+    known = jnp.concatenate([totals, owners.astype(F32), jnp.zeros((128 - PER,), F32)])
+    known, _ = lax.optimization_barrier((known, (raw[1], raw[4])))
+    known = lax.all_to_all(
+        jnp.broadcast_to(known, (TILES,) + known.shape), ("x", "y"), 0, 0, tiled=True
+    )
+    weights, _ = lax.optimization_barrier((weights, (known, raw)))
+    swapped = lax.ppermute(weights, "c", [(0, 1), (1, 0)])
+    known = known.reshape(NX, NY, -1)
+    known = lax.dynamic_slice_in_dim(jnp.concatenate([known, known]), x, NX, axis=0)
+    totals = known[:, :, :rows]
+
+    bias = lax.dynamic_slice_in_dim(class_bias.reshape(NY, classes // NY), y, 1, axis=0)
+    bias = bias.reshape(1, classes // NY, 1)
+    half = NY // 2
+    sums = totals[0], totals[1], totals[2, :half], totals[2, half:], totals[3]
+    priors = tuple(
+        (jnp.exp(r.astype(F32) + bias) / t[:, None, :]).astype(BF) for r, t in zip(raw, sums)
+    )
+
+    named = known[0, :, rows : rows + PER].astype(jnp.int32).reshape(NY * PER)
+    index = (named // NY - x) % NX * NY + named % NY
+    index = jnp.concatenate([index, core.reshape(1)])
+
+    labels = sweep(index, weights, swapped, priors[0], priors)
+    spread = sweep(index, weights, swapped, priors[0], around_x(labels))
     spread = lax.all_to_all(spread, "y", 0, 0, tiled=True)
     return jnp.log(spread.reshape(classes, rows).T.astype(F32))
 

time: 249 us -> 273 us (1.096)
  waiting for transfers between devices: 71.2 us -> 116 us
  blocking collectives: 81.5 us -> 51.4 us
  starting transfers between devices: 45.4 us -> 53.5 us
    all_gather x1 -> x2, waiting for transfers between devices: 0.02 us -> 33.3 us  [the longest x1 19.3 us: on_device(): weights = lax.all_gather(piece, 'y', axis=0, tiled=False)]
    all_to_all x3 -> x1, blocking collectives: 60 us -> 28.7 us  [on_device(): lax.all_to_all(jnp.broadcast_to(piece, (NZ,) + piece.shape), 'z', 0, 0, t...]
    ppermute x0 -> x2, waiting for transfers between devices: none -> 4.62 us  [the longest x1 4.62 us: on_device(): totals = totals + lax.ppermute(totals, 'c', [(0, 1), (1, 0)])]
    ppermute x0 -> x2, starting transfers between devices: none -> 4.32 us  [the longest x1 2.41 us: on_device(): totals = totals + lax.ppermute(totals, 'c', [(0, 1), (1, 0)])]
    all_to_all x1 -> x2, starting transfers between devices: 10.3 us -> 14.2 us  [the longest x1 7.63 us: on_device(): lax.all_to_all(jnp.broadcast_to(known, (TILES,) + known.shape), ('x', 'y'...]
    ppermute x2, waiting for transfers between devices: 7.1 us -> 10.7 us  [around_x(): oppa = lax.ppermute(before[:half], 'x', forward)]
    all_to_all x1 -> x2, waiting for transfers between devices: 15 us -> 17.5 us  [the longest x1 9.36 us: on_device(): lax.all_to_all(scored.reshape(TILES, 2 * SUB, TILE), ('x', 'y'), 0, 0, ti...]
  transfers between devices with their start and end apart: 11 -> 15, of which waited for: 8 -> 12; matrix products, arithmetic and copies ran while one was open for 1% -> 4% of each run, Pallas kernels for 0% -> 0%
where the time goes in v5:
time: 273 us; the launch traced here: 272 us
  waiting for transfers between devices  116 us (42%)
  starting transfers between devices  53.5 us (20%)
  blocking collectives  51.4 us (19%)
  Pallas kernels  20.7 us (8%)
  between operations  14.5 us (5%)
  local copies, waits for them, and re-layouts  10.7 us (4%)
  other arithmetic  4.35 us (2%)
    ppermute x2, waiting for transfers between devices, around_x(): before = lax.ppermute(mine, 'x', forward)  29.7 us
    all_to_all x1, blocking collectives, on_device(): lax.all_to_all(jnp.broadcast_to(piece, (NZ,) + piece.shape), 'z', 0, 0, t...  28.7 us
    all_to_all x1, blocking collectives, on_device(): spread = lax.all_to_all(spread, 'y', 0, 0, tiled=True)  22.8 us
    pallas_call x2, Pallas kernels, sweep(): pl.pallas_call(sweep_kernel, grid_spec=pltpu.PrefetchScalarGridSpec(num_s...  20.7 us
    all_gather x1, waiting for transfers between devices, on_device(): weights = lax.all_gather(piece, 'y', axis=0, tiled=False)  19.3 us
    all_gather x1, waiting for transfers between devices, on_device(): raw = lax.all_gather(raw, 'y', axis=0, tiled=False)  14 us
    ppermute x2, waiting for transfers between devices, around_x(): oppa = lax.ppermute(before[:half], 'x', forward)  10.7 us
    all_to_all x1, waiting for transfers between devices, on_device(): lax.all_to_all(outgoing.reshape(TILES, 2 * SUB, width), ('x', 'y'), 0, 0,...  10.3 us
  transfers between devices with their start and end apart: 15, of which 12 were waited for; matrix products, arithmetic and copies ran while one was open for 4% of the time, Pallas kernels for 0%

profile of v5, /device:TPU:6, one launch (start us, length us, event | category | flops | bytes accessed | tf_op | source)
XLA Modules:
  0.0 272.5 jit_solution(3809778303699602381)
XLA Ops:
  6.5 2.4 copy.63
  8.9 0.0 all-gather.3.cloned.1.call-update
  9.0 0.1 constant_dynamic-slice_fusion.1
  9.1 0.1 copy.64
  9.2 0.1 eq.31
  9.3 0.2 convert_reduce_fusion.1
  9.5 0.1 reduce_sum.69
  9.6 0.1 copy.65
  9.6 0.1 fusion.29
  9.7 0.3 convolution_convert_fusion
  10.0 0.9 reshape.97
  10.9 10.2 %all-to-all-start = ((bf16[32,4,1280]{2,1,0:T(4,128)(2,1)}), bf16[32,4,1280]{2,1,0:T(4,128)(2,1)S(1)}, u32[]{:S(2)}, u32[]{:S(2)}) async-start(bf16[32,4,1280]{2,1,0:T(4,128)(2,1)} %reshape.97), calls=%async_computation | async-start | bytes 655360 | tf_op jit(solution)/shard_map/all_to_all | solution.py:155
  21.9 0.3 exponential_reduce_fusion
  22.2 0.3 fusion
  22.6 10.3 %all-to-all-done = bf16[32,4,1280]{2,1,0:T(4,128)(2,1)S(1)} async-done(((bf16[32,4,1280]{2,1,0:T(4,128)(2,1)}), bf16[32,4,1280]{2,1,0:T(4,128)(2,1)S(1)}, u32[]{:S(2)}, u32[]{:S(2)}) %all-to-all-start) | async-done | bytes 327712 | tf_op jit(solution)/shard_map/all_to_all | solution.py:155
  32.9 0.2 multiply_reduce_fusion
  33.1 0.1 rsqrt.20
  33.3 0.7 fusion.16
  34.0 0.7 reshape.98
  34.7 6.6 %all-to-all-start.1 = ((bf16[32,4,512]{2,1,0:T(4,128)(2,1)}), bf16[32,4,512]{2,1,0:T(4,128)(2,1)S(1)}, u32[]{:S(2)}, u32[]{:S(2)}) async-start(bf16[32,4,512]{2,1,0:T(4,128)(2,1)} %reshape.98), calls=%async_computation.1 | async-start | bytes 262144 | tf_op jit(solution)/shard_map/all_to_all | solution.py:166
  41.3 0.0 all-gather.5.cloned.1.call-start
  41.4 9.4 %all-to-all-done.1 = bf16[32,4,512]{2,1,0:T(4,128)(2,1)S(1)} async-done(((bf16[32,4,512]{2,1,0:T(4,128)(2,1)}), bf16[32,4,512]{2,1,0:T(4,128)(2,1)S(1)}, u32[]{:S(2)}, u32[]{:S(2)}) %all-to-all-start.1) | async-done | bytes 131104 | tf_op jit(solution)/shard_map/all_to_all | solution.py:166
  50.7 0.1 reshape.99
  50.8 0.3 fusion.37
  51.1 0.1 fusion.24
  51.2 0.1 copy.69
  51.3 0.3 broadcast_in_dim.30
  51.6 28.7 %all_to_all.26 = bf16[8,17,2,1024]{3,2,1,0:T(2,128)(2,1)S(1)} all-to-all(bf16[8,17,2,1024]{3,2,1,0:T(2,128)(2,1)S(1)} %broadcast_in_dim.30), channel_id=1, replica_groups=mesh['x'=4,'y'=8,'z'=8,'c'=2] {'z'}, dimensions={0} | all-to-all | bytes 1114112 | tf_op jit(solution)/shard_map/all_to_all | solution.py:179
  80.3 14.0 %all-gather.3.cloned.1.call-done = bf16[8,8,96,512]{3,2,1,0:T(8,128)(2,1)} async-done(((bf16[1,8,96,512]{3,2,1,0:T(8,128)(2,1)}), bf16[8,8,96,512]{3,2,1,0:T(8,128)(2,1)}) %all-gather.3.cloned.1.call-update) | async-done | bytes 6291472 | tf_op jit(solution)/shard_map/all_gather | solution.py:138
  94.3 0.4 slice_bitcast_fusion
  94.6 0.5 copy.70
  95.1 1.0 all_gather_reshape.7
  96.1 1.2 dynamic-slice_bitcast_fusion
  97.3 2.4 collective-permute-start.2
  99.7 3.5 %collective-permute-start.1 = (bf16[8,96,512]{2,1,0:T(8,128)(2,1)S(1)}, bf16[8,96,512]{2,1,0:T(8,128)(2,1)S(1)}, u32[]{:S(2)}, u32[]{:S(2)}) collective-permute-start(bf16[8,96,512]{2,1,0:T(8,128)(2,1)S(1)} %dynamic-slice_bitcast_fusion), channel_id=1, source_target_pairs={{0,384},{128,0},{256,128},{384,256},{1,385},{129,1},{257,129},{385... | collective-permute-start | bytes 2359304 | tf_op jit(solution)/shard_map/ppermute | solution.py:115
  103.2 15.5 %collective-permute-done.2 = bf16[8,96,512]{2,1,0:T(8,128)(2,1)S(1)} collective-permute-done((bf16[8,96,512]{2,1,0:T(8,128)(2,1)S(1)}, bf16[8,96,512]{2,1,0:T(8,128)(2,1)S(1)}, u32[]{:S(2)}, u32[]{:S(2)}) %collective-permute-start.2) | collective-permute-done | bytes 786464 | tf_op jit(solution)/shard_map/ppermute | solution.py:114
  118.8 3.6 %collective-permute-start.3 = (bf16[4,96,512]{2,1,0:T(8,128)(2,1)S(1)}, bf16[4,96,512]{2,1,0:T(8,128)(2,1)S(1)}, u32[]{:S(2)}, u32[]{:S(2)}) collective-permute-start(bf16[4,96,512]{2,1,0:T(8,128)(2,1)S(1)} %slice.70), channel_id=1, source_target_pairs={{0,128},{128,256},{256,384},{384,0},{1,129},{129,257},{257,385},{3... | collective-permute-start | bytes 1179656 | tf_op jit(solution)/shard_map/ppermute | solution.py:117
  122.4 2.3 collective-permute-start.4
  124.7 6.3 %collective-permute-done.3 = bf16[4,96,512]{2,1,0:T(8,128)(2,1)S(1)} collective-permute-done((bf16[4,96,512]{2,1,0:T(8,128)(2,1)S(1)}, bf16[4,96,512]{2,1,0:T(8,128)(2,1)S(1)}, u32[]{:S(2)}, u32[]{:S(2)}) %collective-permute-start.3) | collective-permute-done | bytes 393248 | tf_op jit(solution)/shard_map/ppermute | solution.py:117
  131.0 4.5 %collective-permute-done.4 = bf16[4,96,512]{2,1,0:T(8,128)(2,1)S(1)} collective-permute-done((bf16[4,96,512]{2,1,0:T(8,128)(2,1)S(1)}, bf16[4,96,512]{2,1,0:T(8,128)(2,1)S(1)}, u32[]{:S(2)}, u32[]{:S(2)}) %collective-permute-start.4) | collective-permute-done | bytes 393248 | tf_op jit(solution)/shard_map/ppermute | solution.py:118
  135.5 19.3 %all-gather.5.cloned.1.call-done.mine_ref = bf16[8,256,1024]{2,1,0:T(8,128)(2,1)} async-done(((bf16[1,256,1024]{2,1,0:T(8,128)(2,1)}), bf16[8,256,1024]{2,1,0:T(8,128)(2,1)}) %all-gather.5.cloned.1.call-update) | async-done | bytes 4194320 | tf_op jit(solution)/shard_map/all_gather | solution.py:185
  154.8 1.9 collective-permute-start.5
  156.8 2.4 collective-permute-start
  159.2 4.6 %collective-permute-done = f32[512]{0:T(512)S(1)} collective-permute-done((f32[512]{0:T(512)S(1)}, f32[512]{0:T(512)S(1)}, u32[]{:S(2)}, u32[]{:S(2)}) %collective-permute-start) | collective-permute-done | bytes 2080 | tf_op jit(solution)/shard_map/ppermute | solution.py:192
  163.8 0.1 pad_maximum_fusion.2
  163.9 0.7 broadcast_in_dim.32
  164.6 7.6 %all-to-all-start.3 = ((f32[32,1,640]{2,1,0:T(1,128)}), f32[32,1,640]{2,1,0:T(1,128)S(1)}, u32[]{:S(2)}, u32[]{:S(2)}) async-start(f32[32,1,640]{2,1,0:T(1,128)} %broadcast_in_dim.32), calls=%async_computation.3 | async-start | bytes 163840 | tf_op jit(solution)/shard_map/all_to_all | solution.py:195
  172.2 0.1 reshape.105
  172.3 8.1 %all-to-all-done.3 = f32[32,1,640]{2,1,0:T(1,128)S(1)} async-done(((f32[32,1,640]{2,1,0:T(1,128)}), f32[32,1,640]{2,1,0:T(1,128)S(1)}, u32[]{:S(2)}, u32[]{:S(2)}) %all-to-all-start.3) | async-done | bytes 81952 | tf_op jit(solution)/shard_map/all_to_all | solution.py:195
  180.5 0.1 convert_element_type.127
  180.6 2.3 divide_convert_fusion
  182.9 0.4 divide_convert_fusion.3
  183.3 10.3 %shard_map.55.own = bf16[8,96,512]{2,1,0:T(8,128)(2,1)S(1)} custom-call(s32[257]{0:T(512)S(1)} %pad_add_fusion.index_ref, bf16[8,256,1024]{2,1,0:T(8,128)(2,1)S(1)} %copy-done, bf16[8,256,1024]{2,1,0:T(8,128)(2,1)} %collective-permute-done.5.other_ref, bf16[8,96,512]{2,1,0:T(8,128)(2,1)S(1)} %get-tuple-element.23.prior_ref.own, ...), custom_call_target="tpu_custom_call" | custom-call | flops 3221225472 | bytes 11534336 | tf_op jit(solution)/shard_map/pallas_call | solution.py:88
  193.6 4.0 %collective-permute-start.7 = (bf16[8,96,512]{2,1,0:T(8,128)(2,1)S(1)}, bf16[8,96,512]{2,1,0:T(8,128)(2,1)S(1)}, u32[]{:S(2)}, u32[]{:S(2)}) collective-permute-start(bf16[8,96,512]{2,1,0:T(8,128)(2,1)S(1)} %shard_map.55.own), channel_id=1, source_target_pairs={{0,128},{128,256},{256,384},{384,0},{1,129},{129,257},{257,385},{3... | collective-permute-start | bytes 2359304 | tf_op jit(solution)/shard_map/ppermute | solution.py:114
  197.6 1.9 collective-permute-start.6
  199.5 14.2 %collective-permute-done.7.before = bf16[8,96,512]{2,1,0:T(8,128)(2,1)S(1)} collective-permute-done((bf16[8,96,512]{2,1,0:T(8,128)(2,1)S(1)}, bf16[8,96,512]{2,1,0:T(8,128)(2,1)S(1)}, u32[]{:S(2)}, u32[]{:S(2)}) %collective-permute-start.7) | collective-permute-done | bytes 786464 | tf_op jit(solution)/shard_map/ppermute | solution.py:114
  213.8 5.2 %collective-permute-start.8 = (bf16[4,96,512]{2,1,0:T(8,128)(2,1)S(1)}, bf16[4,96,512]{2,1,0:T(8,128)(2,1)S(1)}, u32[]{:S(2)}, u32[]{:S(2)}) collective-permute-start(bf16[4,96,512]{2,1,0:T(8,128)(2,1)S(1)} %slice.77), channel_id=1, source_target_pairs={{0,128},{128,256},{256,384},{384,0},{1,129},{129,257},{257,385},{3... | collective-permute-start | bytes 1179656 | tf_op jit(solution)/shard_map/ppermute | solution.py:117
  219.0 1.9 collective-permute-start.9
  220.9 4.4 %collective-permute-done.8.oppa = bf16[4,96,512]{2,1,0:T(8,128)(2,1)S(1)} collective-permute-done((bf16[4,96,512]{2,1,0:T(8,128)(2,1)S(1)}, bf16[4,96,512]{2,1,0:T(8,128)(2,1)S(1)}, u32[]{:S(2)}, u32[]{:S(2)}) %collective-permute-start.8) | collective-permute-done | bytes 393248 | tf_op jit(solution)/shard_map/ppermute | solution.py:117
  225.3 5.4 %collective-permute-done.9.oppb = bf16[4,96,512]{2,1,0:T(8,128)(2,1)S(1)} collective-permute-done((bf16[4,96,512]{2,1,0:T(8,128)(2,1)S(1)}, bf16[4,96,512]{2,1,0:T(8,128)(2,1)S(1)}, u32[]{:S(2)}, u32[]{:S(2)}) %collective-permute-start.9) | collective-permute-done | bytes 393248 | tf_op jit(solution)/shard_map/ppermute | solution.py:118
  230.7 10.3 %shard_map.56 = bf16[8,96,512]{2,1,0:T(8,128)(2,1)S(1)} custom-call(s32[257]{0:T(512)S(1)} %pad_add_fusion.index_ref, bf16[8,256,1024]{2,1,0:T(8,128)(2,1)S(1)} %copy-done, bf16[8,256,1024]{2,1,0:T(8,128)(2,1)} %collective-permute-done.5.other_ref, bf16[8,96,512]{2,1,0:T(8,128)(2,1)S(1)} %get-tuple-element.23.prior_ref.own, ...), custom_call_target="tpu_custom_call" | custom-call | flops 3221225472 | bytes 11534336 | tf_op jit(solution)/shard_map/pallas_call | solution.py:88
  241.0 22.8 %all_to_all.27 = bf16[8,96,512]{2,1,0:T(8,128)(2,1)S(1)} all-to-all(bf16[8,96,512]{2,1,0:T(8,128)(2,1)S(1)} %shard_map.56), channel_id=1, replica_groups=mesh['x'=4,'y'=8,'z'=8,'c'=2] {'y'}, dimensions={0} | all-to-all | bytes 1572864 | tf_op jit(solution)/shard_map/all_to_all | solution.py:218
  263.8 0.2 convert_log_fusion
  264.0 1.6 copy.71
  (45 shorter events, 0.5 us)
Async XLA Ops:
  6.5 2.4 copy-start.2
  6.5 2.6 copy-start.4
  6.5 87.7 %all-gather.3.cloned.1.call-start = ((), (), s32[]{:S(2)}) async-start(), calls=%async_computation.5 | async-start | bytes 7077888 | tf_op jit(solution)/shard_map/all_gather | solution.py:138
  8.9 12.9 %copy-start.1 = (bf16[512,768]{1,0:T(8,128)(2,1)S(1)}, bf16[512,768]{1,0:T(8,128)(2,1)}, u32[]{:S(2)}) copy-start(bf16[512,768]{1,0:T(8,128)(2,1)} %param.7) | copy-start | bytes 2359300
  8.9 12.9 %copy-start.3 = (f32[768]{0:T(1024)S(1)}, f32[768]{0:T(1024)}, u32[]{:S(2)}) copy-start(f32[768]{0:T(1024)} %param.6) | copy-start | bytes 9220
  10.9 21.9 %all-to-all-start = ((bf16[32,4,1280]{2,1,0:T(4,128)(2,1)}), bf16[32,4,1280]{2,1,0:T(4,128)(2,1)S(1)}, u32[]{:S(2)}, u32[]{:S(2)}) async-start(bf16[32,4,1280]{2,1,0:T(4,128)(2,1)} %reshape.97), calls=%async_computation | async-start | bytes 655360 | tf_op jit(solution)/shard_map/all_to_all | solution.py:155
  34.7 16.0 %all-to-all-start.1 = ((bf16[32,4,512]{2,1,0:T(4,128)(2,1)}), bf16[32,4,512]{2,1,0:T(4,128)(2,1)S(1)}, u32[]{:S(2)}, u32[]{:S(2)}) async-start(bf16[32,4,512]{2,1,0:T(4,128)(2,1)} %reshape.98), calls=%async_computation.1 | async-start | bytes 262144 | tf_op jit(solution)/shard_map/all_to_all | solution.py:166
  41.3 113.5 %all-gather.5.cloned.1.call-start = ((), (), s32[]{:S(2)}) async-start(), calls=%async_computation.6 | async-start | bytes 4718592 | tf_op jit(solution)/shard_map/all_gather | solution.py:185
  97.3 21.4 %collective-permute-start.2 = (bf16[8,96,512]{2,1,0:T(8,128)(2,1)S(1)}, bf16[8,96,512]{2,1,0:T(8,128)(2,1)S(1)}, u32[]{:S(2)}, u32[]{:S(2)}) collective-permute-start(bf16[8,96,512]{2,1,0:T(8,128)(2,1)S(1)} %dynamic-slice_bitcast_fusion), channel_id=1, source_target_pairs={{0,128},{128,256},{256,384},{384,0},{1,129},{129,257},{257,385},{3... | collective-permute-start | bytes 2359304 | tf_op jit(solution)/shard_map/ppermute | solution.py:114
  99.7 22.6 %collective-permute-start.1 = (bf16[8,96,512]{2,1,0:T(8,128)(2,1)S(1)}, bf16[8,96,512]{2,1,0:T(8,128)(2,1)S(1)}, u32[]{:S(2)}, u32[]{:S(2)}) collective-permute-start(bf16[8,96,512]{2,1,0:T(8,128)(2,1)S(1)} %dynamic-slice_bitcast_fusion), channel_id=1, source_target_pairs={{0,384},{128,0},{256,128},{384,256},{1,385},{129,1},{257,129},{385... | collective-permute-start | bytes 2359304 | tf_op jit(solution)/shard_map/ppermute | solution.py:115
  118.8 12.2 %collective-permute-start.3 = (bf16[4,96,512]{2,1,0:T(8,128)(2,1)S(1)}, bf16[4,96,512]{2,1,0:T(8,128)(2,1)S(1)}, u32[]{:S(2)}, u32[]{:S(2)}) collective-permute-start(bf16[4,96,512]{2,1,0:T(8,128)(2,1)S(1)} %slice.70), channel_id=1, source_target_pairs={{0,128},{128,256},{256,384},{384,0},{1,129},{129,257},{257,385},{3... | collective-permute-start | bytes 1179656 | tf_op jit(solution)/shard_map/ppermute | solution.py:117
  122.4 13.1 %collective-permute-start.4 = (bf16[4,96,512]{2,1,0:T(8,128)(2,1)S(1)}, bf16[4,96,512]{2,1,0:T(8,128)(2,1)S(1)}, u32[]{:S(2)}, u32[]{:S(2)}) collective-permute-start(bf16[4,96,512]{2,1,0:T(8,128)(2,1)S(1)} %slice.71), channel_id=1, source_target_pairs={{0,384},{128,0},{256,128},{384,256},{1,385},{129,1},{257,129},{385... | collective-permute-start | bytes 1179656 | tf_op jit(solution)/shard_map/ppermute | solution.py:118
  154.8 28.5 %collective-permute-start.5 = (bf16[8,256,1024]{2,1,0:T(8,128)(2,1)}, bf16[8,256,1024]{2,1,0:T(8,128)(2,1)}, u32[]{:S(2)}, u32[]{:S(2)}) collective-permute-start(bf16[8,256,1024]{2,1,0:T(8,128)(2,1)} %all-gather.5.cloned.1.call-done.mine_ref), channel_id=1, source_target_pairs={{0,1},{1,0},{2,3},{3,2},{4,5},{5,4},{6,7},{7,6},{8,9},{9,8},{10,11... | collective-permute-start | bytes 12582920 | tf_op jit(solution)/shard_map/ppermute | solution.py:199
  156.8 7.0 %collective-permute-start = (f32[512]{0:T(512)S(1)}, f32[512]{0:T(512)S(1)}, u32[]{:S(2)}, u32[]{:S(2)}) collective-permute-start(f32[512]{0:T(512)S(1)} %bitcast.66), channel_id=1, source_target_pairs={{0,1},{1,0},{2,3},{3,2},{4,5},{5,4},{6,7},{7,6},{8,9},{9,8},{10,11... | collective-permute-start | bytes 6152 | tf_op jit(solution)/shard_map/ppermute | solution.py:192
  164.6 15.8 %all-to-all-start.3 = ((f32[32,1,640]{2,1,0:T(1,128)}), f32[32,1,640]{2,1,0:T(1,128)S(1)}, u32[]{:S(2)}, u32[]{:S(2)}) async-start(f32[32,1,640]{2,1,0:T(1,128)} %broadcast_in_dim.32), calls=%async_computation.3 | async-start | bytes 163840 | tf_op jit(solution)/shard_map/all_to_all | solution.py:195
  180.6 2.6 copy-start
  193.6 20.1 %collective-permute-start.7 = (bf16[8,96,512]{2,1,0:T(8,128)(2,1)S(1)}, bf16[8,96,512]{2,1,0:T(8,128)(2,1)S(1)}, u32[]{:S(2)}, u32[]{:S(2)}) collective-permute-start(bf16[8,96,512]{2,1,0:T(8,128)(2,1)S(1)} %shard_map.55.own), channel_id=1, source_target_pairs={{0,128},{128,256},{256,384},{384,0},{1,129},{129,257},{257,385},{3... | collective-permute-start | bytes 2359304 | tf_op jit(solution)/shard_map/ppermute | solution.py:114
  197.6 21.4 %collective-permute-start.6 = (bf16[8,96,512]{2,1,0:T(8,128)(2,1)S(1)}, bf16[8,96,512]{2,1,0:T(8,128)(2,1)S(1)}, u32[]{:S(2)}, u32[]{:S(2)}) collective-permute-start(bf16[8,96,512]{2,1,0:T(8,128)(2,1)S(1)} %shard_map.55.own), channel_id=1, source_target_pairs={{0,384},{128,0},{256,128},{384,256},{1,385},{129,1},{257,129},{385... | collective-permute-start | bytes 2359304 | tf_op jit(solution)/shard_map/ppermute | solution.py:115
  213.8 11.6 %collective-permute-start.8 = (bf16[4,96,512]{2,1,0:T(8,128)(2,1)S(1)}, bf16[4,96,512]{2,1,0:T(8,128)(2,1)S(1)}, u32[]{:S(2)}, u32[]{:S(2)}) collective-permute-start(bf16[4,96,512]{2,1,0:T(8,128)(2,1)S(1)} %slice.77), channel_id=1, source_target_pairs={{0,128},{128,256},{256,384},{384,0},{1,129},{129,257},{257,385},{3... | collective-permute-start | bytes 1179656 | tf_op jit(solution)/shard_map/ppermute | solution.py:117
  219.0 11.7 %collective-permute-start.9 = (bf16[4,96,512]{2,1,0:T(8,128)(2,1)S(1)}, bf16[4,96,512]{2,1,0:T(8,128)(2,1)S(1)}, u32[]{:S(2)}, u32[]{:S(2)}) collective-permute-start(bf16[4,96,512]{2,1,0:T(8,128)(2,1)S(1)} %slice.78), channel_id=1, source_target_pairs={{0,384},{128,0},{256,128},{384,256},{1,385},{129,1},{257,129},{385... | collective-permute-start | bytes 1179656 | tf_op jit(solution)/shard_map/ppermute | solution.py:118
Sparse Core Ops, SparseCore 0:
  9.4 84.7 all-gather.2
  96.3 58.4 all-gather.4

commit v6 on v5

--- a/solution.py
+++ b/solution.py
@@ -32,7 +32,7 @@
     return (wide * scale / math.sqrt(wide.shape[-1])).astype(BF)
 
 
-def sweep_kernel(index_ref, mine_ref, other_ref, prior_ref, own, after, oppa, oppb, before, out_ref, held, sems):
+def sweep_kernel(index_ref, w_ref, prior_ref, own, after, oppa, oppb, before, out_ref, held, sems):
     y = pl.program_id(0)
 
     @pl.when(y == 0)
@@ -54,19 +54,19 @@
         for copy in copies:
             copy.wait()
 
-    first_core = index_ref[NY * PER] == 0
     classes = out_ref.shape[1]
     lanes = lax.broadcasted_iota(jnp.int32, (classes, 128), 1) // QB
     for group in range(NBLK // 4):
         total = None
         for k in range(NT):
-            rows = []
-            for b in range(4):
-                at = pl.ds((4 * group + b) * ROWS_C, ROWS_C), pl.ds(k * TILE, TILE)
-                mine, other = mine_ref[0, *at], other_ref[0, *at]
-                rows.append(jnp.where(first_core, mine, other))
-                rows.append(jnp.where(first_core, other, mine))
-            weights = jnp.concatenate(rows, axis=0)
+            weights = jnp.concatenate(
+                [
+                    w_ref[c, pl.ds((4 * group + b) * ROWS_C, ROWS_C), pl.ds(k * TILE, TILE)]
+                    for b in range(4)
+                    for c in range(NC)
+                ],
+                axis=0,
+            )
             labels = jnp.concatenate(
                 [held[index_ref[y * PER + (4 * group + b) * NT + k]] for b in range(4)], axis=0
             )
@@ -82,37 +82,38 @@
         out_ref[0, :, at] = (picked + (1.0 - ALPHA) * prior).astype(BF)
 
 
-def sweep(index, mine, other, prior, pieces):
+def sweep(index, weights, prior, pieces):
     ny, classes, rows = prior.shape
-    by_y = lambda array: pl.BlockSpec((1,) + array.shape[1:], lambda y, _: (y, 0, 0))
     return pl.pallas_call(
         sweep_kernel,
         grid_spec=pltpu.PrefetchScalarGridSpec(
             num_scalar_prefetch=1,
             grid=(ny,),
-            in_specs=[by_y(mine), by_y(other), by_y(prior)]
+            in_specs=[
+                pl.BlockSpec((NC,) + weights.shape[1:], lambda y, _: (y, 0, 0)),
+                pl.BlockSpec((1, classes, rows), lambda y, _: (y, 0, 0)),
+            ]
             + [pl.BlockSpec(memory_space=pl.ANY)] * len(pieces),
-            out_specs=by_y(prior),
+            out_specs=pl.BlockSpec((1, classes, rows), lambda y, _: (y, 0, 0)),
             scratch_shapes=[
                 pltpu.VMEM((TILES, classes, rows), BF),
                 pltpu.SemaphoreType.DMA((len(pieces),)),
             ],
         ),
         out_shape=jax.ShapeDtypeStruct(prior.shape, BF),
-        compiler_params=pltpu.CompilerParams(vmem_limit_bytes=40 << 20),
+        compiler_params=pltpu.CompilerParams(vmem_limit_bytes=48 << 20),
         cost_estimate=pl.CostEstimate(
             flops=2 * ny * rows * NT * TILE * classes * 4,
-            bytes_accessed=2 * mine.size * 2 + 4 * prior.size * 2,
+            bytes_accessed=weights.size * 2 + 4 * prior.size * 2,
             transcendentals=0,
         ),
-    )(index, mine, other, prior, *pieces)
-
-
-def around_x(mine):
+    )(index, weights, prior, *pieces)
+
+
+def around_x(mine, beside=lambda *near: near):
     forward = [(i, (i + 1) % NX) for i in range(NX)]
     backward = [(i, (i - 1) % NX) for i in range(NX)]
-    before = lax.ppermute(mine, "x", forward)
-    after = lax.ppermute(mine, "x", backward)
+    before, after = beside(lax.ppermute(mine, "x", forward), lax.ppermute(mine, "x", backward))
     half = NY // 2
     oppa = lax.ppermute(before[:half], "x", forward)
     oppb = lax.ppermute(after[half:], "x", backward)
@@ -133,9 +134,6 @@
     rows, classes = logits.shape
     x, y = lax.axis_index("x"), lax.axis_index("y")
     z, core = lax.axis_index("z"), lax.axis_index("c")
-
-    raw = logits.T.reshape(NY, classes // NY, rows)
-    raw = lax.all_gather(raw, "y", axis=0, tiled=False)
 
     owners = tile_lists.reshape(PER)
     order = jnp.arange(PER, dtype=jnp.int32)
@@ -180,23 +178,22 @@
         jnp.broadcast_to(piece, (NZ,) + piece.shape), "z", 0, 0, tiled=True
     )
 
-    raw, over_z = lax.optimization_barrier((raw, over_z))
     piece = over_z[:, :NBLK].transpose(1, 0, 2, 3).reshape(NBLK * ROWS_C, NT * TILE)
-    weights = lax.all_gather(piece, "y", axis=0, tiled=False)
-
-    raw = lax.dynamic_index_in_dim(raw, y, axis=1, keepdims=False)
-    raw = around_x(raw)
+    weights = lax.all_gather(piece, ("y", "c"), axis=0, tiled=False)
 
     terms = jnp.sum(over_z[:, NBLK].astype(F32), axis=0).reshape(4, rows)
     totals = terms[0] + terms[1] + terms[2]
+    raw, _ = lax.optimization_barrier((logits, over_z))
+    raw = lax.all_to_all(
+        raw.T.reshape(NY, classes // NY, rows), "y", 0, 0, tiled=True
+    )
     totals = totals + lax.ppermute(totals, "c", [(0, 1), (1, 0)])
     known = jnp.concatenate([totals, owners.astype(F32), jnp.zeros((128 - PER,), F32)])
-    known, _ = lax.optimization_barrier((known, (raw[1], raw[4])))
+    known, _ = lax.optimization_barrier((known, raw))
     known = lax.all_to_all(
         jnp.broadcast_to(known, (TILES,) + known.shape), ("x", "y"), 0, 0, tiled=True
     )
-    weights, _ = lax.optimization_barrier((weights, (known, raw)))
-    swapped = lax.ppermute(weights, "c", [(0, 1), (1, 0)])
+    raw = around_x(raw, lambda *near: lax.optimization_barrier((*near, known))[:2])
     known = known.reshape(NX, NY, -1)
     known = lax.dynamic_slice_in_dim(jnp.concatenate([known, known]), x, NX, axis=0)
     totals = known[:, :, :rows]
@@ -211,10 +208,9 @@
 
     named = known[0, :, rows : rows + PER].astype(jnp.int32).reshape(NY * PER)
     index = (named // NY - x) % NX * NY + named % NY
-    index = jnp.concatenate([index, core.reshape(1)])
-
-    labels = sweep(index, weights, swapped, priors[0], priors)
-    spread = sweep(index, weights, swapped, priors[0], around_x(labels))
+
+    labels = sweep(index, weights, priors[0], priors)
+    spread = sweep(index, weights, priors[0], around_x(labels))
     spread = lax.all_to_all(spread, "y", 0, 0, tiled=True)
     return jnp.log(spread.reshape(classes, rows).T.astype(F32))
 

time: 273 us -> 237 us (0.87)
  waiting for transfers between devices: 116 us -> 80.3 us
    all_gather x2 -> x1, waiting for transfers between devices: 33.3 us -> 0.02 us  [on_device(): weights = lax.all_gather(piece, ('y', 'c'), axis=0, tiled=False)]
    all_to_all x0 -> x1, waiting for transfers between devices: none -> 24.4 us  [on_device(): lax.all_to_all(raw.T.reshape(NY, classes // NY, rows), 'y', 0, 0, tiled=T...]
    ppermute x5 -> x4, waiting for transfers between devices: 29.7 us -> 19.8 us  [the longest x2 16.7 us: around_x(): lax.ppermute(mine, 'x', forward)]
    ppermute x2, waiting for transfers between devices: 10.7 us -> 5.19 us  [around_x(): oppa = lax.ppermute(before[:half], 'x', forward)]
    all_to_all x1, waiting for transfers between devices: 8.11 us -> 2.7 us  [on_device(): lax.all_to_all(jnp.broadcast_to(known, (TILES,) + known.shape), ('x', 'y'...]
    all_to_all x0 -> x1, starting transfers between devices: none -> 3.55 us  [on_device(): lax.all_to_all(raw.T.reshape(NY, classes // NY, rows), 'y', 0, 0, tiled=T...]
    ppermute x1, waiting for transfers between devices: 4.62 us -> 1.11 us  [on_device(): totals = totals + lax.ppermute(totals, 'c', [(0, 1), (1, 0)])]
    ppermute x2, starting transfers between devices: 8.75 us -> 5.71 us  [around_x(): oppa = lax.ppermute(before[:half], 'x', forward)]
  transfers between devices with their start and end apart: 15 -> 14, of which waited for: 12 -> 12; matrix products, arithmetic and copies ran while one was open for 4% -> 2% of each run, Pallas kernels for 0% -> 0%
where the time goes in v6:
time: 237 us; the launch traced here: 235 us
  waiting for transfers between devices  80.3 us (34%)
  starting transfers between devices  52.4 us (22%)
  blocking collectives  49.6 us (21%)
  Pallas kernels  22.2 us (9%)
  between operations  14.4 us (6%)
  local copies, waits for them, and re-layouts  10.1 us (4%)
  other arithmetic  5.11 us (2%)
    all_to_all x1, blocking collectives, on_device(): lax.all_to_all(jnp.broadcast_to(piece, (NZ,) + piece.shape), 'z', 0, 0, t...  26.1 us
    all_to_all x1, waiting for transfers between devices, on_device(): lax.all_to_all(raw.T.reshape(NY, classes // NY, rows), 'y', 0, 0, tiled=T...  24.4 us
    all_to_all x1, blocking collectives, on_device(): spread = lax.all_to_all(spread, 'y', 0, 0, tiled=True)  23.4 us
    pallas_call x2, Pallas kernels, sweep(): pl.pallas_call(sweep_kernel, grid_spec=pltpu.PrefetchScalarGridSpec(num_s...  22.2 us
    ppermute x2, waiting for transfers between devices, around_x(): lax.ppermute(mine, 'x', forward)  16.7 us
    all_to_all x1, waiting for transfers between devices, on_device(): lax.all_to_all(outgoing.reshape(TILES, 2 * SUB, width), ('x', 'y'), 0, 0,...  10.3 us
    all_to_all x1, starting transfers between devices, on_device(): lax.all_to_all(outgoing.reshape(TILES, 2 * SUB, width), ('x', 'y'), 0, 0,...  10.2 us
    all_to_all x1, waiting for transfers between devices, on_device(): lax.all_to_all(scored.reshape(TILES, 2 * SUB, TILE), ('x', 'y'), 0, 0, ti...  8.46 us
  transfers between devices with their start and end apart: 14, of which 12 were waited for; matrix products, arithmetic and copies ran while one was open for 2% of the time, Pallas kernels for 0%

profile of v6, /device:TPU:6, one launch (start us, length us, event | category | flops | bytes accessed | tf_op | source)
XLA Modules:
  0.0 235.5 jit_solution(10058132496354408008)
XLA Ops:
  6.5 1.2 constant_dynamic-slice_fusion.1
  7.8 0.8 copy.63
  8.5 0.1 eq.31
  8.6 0.2 convert_reduce_fusion.1
  8.8 0.1 reduce_sum.69
  8.9 0.1 copy.64
  9.0 0.7 multiply_add_fusion
  9.7 0.1 fusion.29
  9.7 0.3 convolution_convert_fusion
  10.0 0.9 reshape.97
  11.0 10.2 %all-to-all-start = ((bf16[32,4,1280]{2,1,0:T(4,128)(2,1)}), bf16[32,4,1280]{2,1,0:T(4,128)(2,1)S(1)}, u32[]{:S(2)}, u32[]{:S(2)}) async-start(bf16[32,4,1280]{2,1,0:T(4,128)(2,1)} %reshape.97), calls=%async_computation | async-start | bytes 655360 | tf_op jit(solution)/shard_map/all_to_all | solution.py:153
  21.9 0.3 exponential_reduce_fusion
  22.2 0.3 fusion
  22.6 10.3 %all-to-all-done = bf16[32,4,1280]{2,1,0:T(4,128)(2,1)S(1)} async-done(((bf16[32,4,1280]{2,1,0:T(4,128)(2,1)}), bf16[32,4,1280]{2,1,0:T(4,128)(2,1)S(1)}, u32[]{:S(2)}, u32[]{:S(2)}) %all-to-all-start) | async-done | bytes 327712 | tf_op jit(solution)/shard_map/all_to_all | solution.py:153
  32.9 0.2 multiply_reduce_fusion
  33.1 0.1 rsqrt.20
  33.3 0.7 fusion.16
  34.0 0.7 reshape.98
  34.7 6.6 %all-to-all-start.1 = ((bf16[32,4,512]{2,1,0:T(4,128)(2,1)}), bf16[32,4,512]{2,1,0:T(4,128)(2,1)S(1)}, u32[]{:S(2)}, u32[]{:S(2)}) async-start(bf16[32,4,512]{2,1,0:T(4,128)(2,1)} %reshape.98), calls=%async_computation.1 | async-start | bytes 262144 | tf_op jit(solution)/shard_map/all_to_all | solution.py:164
  41.3 0.0 all-gather.2.cloned.1.call-start
  41.4 8.5 %all-to-all-done.1 = bf16[32,4,512]{2,1,0:T(4,128)(2,1)S(1)} async-done(((bf16[32,4,512]{2,1,0:T(4,128)(2,1)}), bf16[32,4,512]{2,1,0:T(4,128)(2,1)S(1)}, u32[]{:S(2)}, u32[]{:S(2)}) %all-to-all-start.1) | async-done | bytes 131104 | tf_op jit(solution)/shard_map/all_to_all | solution.py:164
  49.8 0.1 reshape.99
  49.9 0.3 fusion.37
  50.2 0.1 fusion.24
  50.3 0.1 copy.68
  50.4 0.3 broadcast_in_dim.30
  50.7 26.1 %all_to_all.31 = bf16[8,17,2,1024]{3,2,1,0:T(2,128)(2,1)S(1)} all-to-all(bf16[8,17,2,1024]{3,2,1,0:T(2,128)(2,1)S(1)} %broadcast_in_dim.30), channel_id=1, replica_groups=mesh['x'=4,'y'=8,'z'=8,'c'=2] {'z'}, dimensions={0} | all-to-all | bytes 1114112 | tf_op jit(solution)/shard_map/all_to_all | solution.py:177
  76.9 0.4 slice_bitcast_fusion
  77.2 0.5 copy.70
  77.7 1.0 all_gather_reshape.3
  78.7 1.2 copy.69
  79.9 3.5 %all-to-all-start.3 = ((bf16[8,96,512]{2,1,0:T(8,128)(2,1)}), bf16[8,96,512]{2,1,0:T(8,128)(2,1)S(1)}, u32[]{:S(2)}, u32[]{:S(2)}) async-start(bf16[8,96,512]{2,1,0:T(8,128)(2,1)} %bitcast.9), calls=%async_computation.3 | async-start | bytes 1572864 | tf_op jit(solution)/shard_map/all_to_all | solution.py:187
  83.5 1.9 collective-permute-start
  85.5 1.1 collective-permute-done
  86.6 0.1 pad_maximum_fusion.2
  86.7 24.4 %all-to-all-done.3 = bf16[8,96,512]{2,1,0:T(8,128)(2,1)S(1)} async-done(((bf16[8,96,512]{2,1,0:T(8,128)(2,1)}), bf16[8,96,512]{2,1,0:T(8,128)(2,1)S(1)}, u32[]{:S(2)}, u32[]{:S(2)}) %all-to-all-start.3) | async-done | bytes 786464 | tf_op jit(solution)/shard_map/all_to_all | solution.py:187
  111.1 0.7 broadcast_in_dim.32
  111.8 6.8 %all-to-all-start.4 = ((f32[32,1,640]{2,1,0:T(1,128)}), f32[32,1,640]{2,1,0:T(1,128)S(1)}, u32[]{:S(2)}, u32[]{:S(2)}) async-start(f32[32,1,640]{2,1,0:T(1,128)} %broadcast_in_dim.32), calls=%async_computation.4 | async-start | bytes 163840 | tf_op jit(solution)/shard_map/all_to_all | solution.py:193
  118.6 0.1 reshape.105
  118.6 2.1 collective-permute-start.1
  120.7 3.7 %collective-permute-start.2 = (bf16[8,96,512]{2,1,0:T(8,128)(2,1)S(1)}, bf16[8,96,512]{2,1,0:T(8,128)(2,1)S(1)}, u32[]{:S(2)}, u32[]{:S(2)}) collective-permute-start(bf16[8,96,512]{2,1,0:T(8,128)(2,1)S(1)} %all-to-all-done.3), channel_id=1, source_target_pairs={{0,384},{128,0},{256,128},{384,256},{1,385},{129,1},{257,129},{385... | collective-permute-start | bytes 2359304 | tf_op jit(solution)/shard_map/ppermute | solution.py:116
  124.5 2.7 %all-to-all-done.4 = f32[32,1,640]{2,1,0:T(1,128)S(1)} async-done(((f32[32,1,640]{2,1,0:T(1,128)}), f32[32,1,640]{2,1,0:T(1,128)S(1)}, u32[]{:S(2)}, u32[]{:S(2)}) %all-to-all-start.4) | async-done | bytes 81952 | tf_op jit(solution)/shard_map/all_to_all | solution.py:193
  127.2 0.1 convert_element_type.127
  127.4 6.2 %collective-permute-done.1 = bf16[8,96,512]{2,1,0:T(8,128)(2,1)S(1)} collective-permute-done((bf16[8,96,512]{2,1,0:T(8,128)(2,1)S(1)}, bf16[8,96,512]{2,1,0:T(8,128)(2,1)S(1)}, u32[]{:S(2)}, u32[]{:S(2)}) %collective-permute-start.1) | collective-permute-done | bytes 786464 | tf_op jit(solution)/shard_map/ppermute | solution.py:116
  133.5 3.1 %collective-permute-done.2 = bf16[8,96,512]{2,1,0:T(8,128)(2,1)S(1)} collective-permute-done((bf16[8,96,512]{2,1,0:T(8,128)(2,1)S(1)}, bf16[8,96,512]{2,1,0:T(8,128)(2,1)S(1)}, u32[]{:S(2)}, u32[]{:S(2)}) %collective-permute-start.2) | collective-permute-done | bytes 786464 | tf_op jit(solution)/shard_map/ppermute | solution.py:116
  136.7 2.2 collective-permute-start.3
  138.9 3.7 %collective-permute-start.4 = (bf16[4,96,512]{2,1,0:T(8,128)(2,1)S(1)}, bf16[4,96,512]{2,1,0:T(8,128)(2,1)S(1)}, u32[]{:S(2)}, u32[]{:S(2)}) collective-permute-start(bf16[4,96,512]{2,1,0:T(8,128)(2,1)S(1)} %slice.61), channel_id=1, source_target_pairs={{0,384},{128,0},{256,128},{384,256},{1,385},{129,1},{257,129},{385... | collective-permute-start | bytes 1179656 | tf_op jit(solution)/shard_map/ppermute | solution.py:119
  142.6 2.3 divide_convert_fusion
  144.9 1.4 collective-permute-done.3
  146.4 3.4 %collective-permute-done.4 = bf16[4,96,512]{2,1,0:T(8,128)(2,1)S(1)} collective-permute-done((bf16[4,96,512]{2,1,0:T(8,128)(2,1)S(1)}, bf16[4,96,512]{2,1,0:T(8,128)(2,1)S(1)}, u32[]{:S(2)}, u32[]{:S(2)}) %collective-permute-start.4) | collective-permute-done | bytes 393248 | tf_op jit(solution)/shard_map/ppermute | solution.py:119
  149.8 0.4 divide_convert_fusion.3
  150.1 0.0 all-gather.2.cloned.1.call-done.w_ref
  150.2 11.1 %shard_map.55.own = bf16[8,96,512]{2,1,0:T(8,128)(2,1)S(1)} custom-call(s32[256]{0:T(256)S(1)} %fusion.33.index_ref, bf16[16,256,1024]{2,1,0:T(8,128)(2,1)} %all-gather.2.cloned.1.call-done.w_ref, bf16[8,96,512]{2,1,0:T(8,128)(2,1)S(1)} %get-tuple-element.23.prior_ref.own, bf16[8,96,512]{2,1,0:T(8,128)(2,1)S(1)} %get-tuple-element.23.prior_ref.own, ...), custom_call_target="tpu_custom_call" | custom-call | flops 3221225472 | bytes 11534336 | tf_op jit(solution)/shard_map/pallas_call | solution.py:87
  161.3 2.3 collective-permute-start.6
  163.6 3.6 %collective-permute-start.5 = (bf16[8,96,512]{2,1,0:T(8,128)(2,1)S(1)}, bf16[8,96,512]{2,1,0:T(8,128)(2,1)S(1)}, u32[]{:S(2)}, u32[]{:S(2)}) collective-permute-start(bf16[8,96,512]{2,1,0:T(8,128)(2,1)S(1)} %shard_map.55.own), channel_id=1, source_target_pairs={{0,384},{128,0},{256,128},{384,256},{1,385},{129,1},{257,129},{385... | collective-permute-start | bytes 2359304 | tf_op jit(solution)/shard_map/ppermute | solution.py:116
  167.2 10.6 %collective-permute-done.6.before = bf16[8,96,512]{2,1,0:T(8,128)(2,1)S(1)} collective-permute-done((bf16[8,96,512]{2,1,0:T(8,128)(2,1)S(1)}, bf16[8,96,512]{2,1,0:T(8,128)(2,1)S(1)}, u32[]{:S(2)}, u32[]{:S(2)}) %collective-permute-start.6) | collective-permute-done | bytes 786464 | tf_op jit(solution)/shard_map/ppermute | solution.py:116
  177.7 3.5 %collective-permute-start.7 = (bf16[4,96,512]{2,1,0:T(8,128)(2,1)S(1)}, bf16[4,96,512]{2,1,0:T(8,128)(2,1)S(1)}, u32[]{:S(2)}, u32[]{:S(2)}) collective-permute-start(bf16[4,96,512]{2,1,0:T(8,128)(2,1)S(1)} %slice.77), channel_id=1, source_target_pairs={{0,128},{128,256},{256,384},{384,0},{1,129},{129,257},{257,385},{3... | collective-permute-start | bytes 1179656 | tf_op jit(solution)/shard_map/ppermute | solution.py:118
  181.3 2.3 collective-permute-start.8
  183.6 3.8 %collective-permute-done.7.oppa = bf16[4,96,512]{2,1,0:T(8,128)(2,1)S(1)} collective-permute-done((bf16[4,96,512]{2,1,0:T(8,128)(2,1)S(1)}, bf16[4,96,512]{2,1,0:T(8,128)(2,1)S(1)}, u32[]{:S(2)}, u32[]{:S(2)}) %collective-permute-start.7) | collective-permute-done | bytes 393248 | tf_op jit(solution)/shard_map/ppermute | solution.py:118
  187.4 4.8 %collective-permute-done.8.oppb = bf16[4,96,512]{2,1,0:T(8,128)(2,1)S(1)} collective-permute-done((bf16[4,96,512]{2,1,0:T(8,128)(2,1)S(1)}, bf16[4,96,512]{2,1,0:T(8,128)(2,1)S(1)}, u32[]{:S(2)}, u32[]{:S(2)}) %collective-permute-start.8) | collective-permute-done | bytes 393248 | tf_op jit(solution)/shard_map/ppermute | solution.py:119
  192.2 11.1 %shard_map.56 = bf16[8,96,512]{2,1,0:T(8,128)(2,1)S(1)} custom-call(s32[256]{0:T(256)S(1)} %fusion.33.index_ref, bf16[16,256,1024]{2,1,0:T(8,128)(2,1)} %all-gather.2.cloned.1.call-done.w_ref, bf16[8,96,512]{2,1,0:T(8,128)(2,1)S(1)} %get-tuple-element.23.prior_ref.own, bf16[8,96,512]{2,1,0:T(8,128)(2,1)S(1)} %shard_map.55.own, ...), custom_call_target="tpu_custom_call" | custom-call | flops 3221225472 | bytes 11534336 | tf_op jit(solution)/shard_map/pallas_call | solution.py:87
  203.3 23.4 %all_to_all.32 = bf16[8,96,512]{2,1,0:T(8,128)(2,1)S(1)} all-to-all(bf16[8,96,512]{2,1,0:T(8,128)(2,1)S(1)} %shard_map.56), channel_id=1, replica_groups=mesh['x'=4,'y'=8,'z'=8,'c'=2] {'y'}, dimensions={0} | all-to-all | bytes 1572864 | tf_op jit(solution)/shard_map/all_to_all | solution.py:214
  226.8 0.2 convert_log_fusion
  227.0 1.6 copy.71
  (40 shorter events, 0.4 us)
Async XLA Ops:
  6.5 15.7 %copy-start.3 = (bf16[512,1280]{1,0:T(8,128)(2,1)S(1)}, bf16[512,1280]{1,0:T(8,128)(2,1)}, u32[]{:S(2)}) copy-start(bf16[512,1280]{1,0:T(8,128)(2,1)} %param.5) | copy-start | bytes 3932164
  6.5 15.3 %copy-start.4 = (f32[768]{0:T(1024)S(1)}, f32[768]{0:T(1024)}, u32[]{:S(2)}) copy-start(f32[768]{0:T(1024)} %param.6) | copy-start | bytes 9220
  6.5 15.3 %copy-start = (bf16[512,768]{1,0:T(8,128)(2,1)S(1)}, bf16[512,768]{1,0:T(8,128)(2,1)}, u32[]{:S(2)}) copy-start(bf16[512,768]{1,0:T(8,128)(2,1)} %param.7) | copy-start | bytes 2359300
  11.0 21.9 %all-to-all-start = ((bf16[32,4,1280]{2,1,0:T(4,128)(2,1)}), bf16[32,4,1280]{2,1,0:T(4,128)(2,1)S(1)}, u32[]{:S(2)}, u32[]{:S(2)}) async-start(bf16[32,4,1280]{2,1,0:T(4,128)(2,1)} %reshape.97), calls=%async_computation | async-start | bytes 655360 | tf_op jit(solution)/shard_map/all_to_all | solution.py:153
  34.7 15.1 %all-to-all-start.1 = ((bf16[32,4,512]{2,1,0:T(4,128)(2,1)}), bf16[32,4,512]{2,1,0:T(4,128)(2,1)S(1)}, u32[]{:S(2)}, u32[]{:S(2)}) async-start(bf16[32,4,512]{2,1,0:T(4,128)(2,1)} %reshape.98), calls=%async_computation.1 | async-start | bytes 262144 | tf_op jit(solution)/shard_map/all_to_all | solution.py:164
  41.3 108.9 %all-gather.2.cloned.1.call-start = ((), (), s32[]{:S(2)}) async-start(), calls=%async_computation.6 | async-start | bytes 8912896 | tf_op jit(solution)/shard_map/all_gather | solution.py:182
  79.9 31.2 %all-to-all-start.3 = ((bf16[8,96,512]{2,1,0:T(8,128)(2,1)}), bf16[8,96,512]{2,1,0:T(8,128)(2,1)S(1)}, u32[]{:S(2)}, u32[]{:S(2)}) async-start(bf16[8,96,512]{2,1,0:T(8,128)(2,1)} %bitcast.9), calls=%async_computation.3 | async-start | bytes 1572864 | tf_op jit(solution)/shard_map/all_to_all | solution.py:187
  83.5 3.1 %collective-permute-start = (f32[512]{0:T(512)S(1)}, f32[512]{0:T(512)S(1)}, u32[]{:S(2)}, u32[]{:S(2)}) collective-permute-start(f32[512]{0:T(512)S(1)} %bitcast.60), channel_id=1, source_target_pairs={{0,1},{1,0},{2,3},{3,2},{4,5},{5,4},{6,7},{7,6},{8,9},{9,8},{10,11... | collective-permute-start | bytes 6152 | tf_op jit(solution)/shard_map/ppermute | solution.py:190
  111.8 15.4 %all-to-all-start.4 = ((f32[32,1,640]{2,1,0:T(1,128)}), f32[32,1,640]{2,1,0:T(1,128)S(1)}, u32[]{:S(2)}, u32[]{:S(2)}) async-start(f32[32,1,640]{2,1,0:T(1,128)} %broadcast_in_dim.32), calls=%async_computation.4 | async-start | bytes 163840 | tf_op jit(solution)/shard_map/all_to_all | solution.py:193
  118.6 14.9 %collective-permute-start.1 = (bf16[8,96,512]{2,1,0:T(8,128)(2,1)S(1)}, bf16[8,96,512]{2,1,0:T(8,128)(2,1)S(1)}, u32[]{:S(2)}, u32[]{:S(2)}) collective-permute-start(bf16[8,96,512]{2,1,0:T(8,128)(2,1)S(1)} %all-to-all-done.3), channel_id=1, source_target_pairs={{0,128},{128,256},{256,384},{384,0},{1,129},{129,257},{257,385},{3... | collective-permute-start | bytes 2359304 | tf_op jit(solution)/shard_map/ppermute | solution.py:116
  120.7 15.9 %collective-permute-start.2 = (bf16[8,96,512]{2,1,0:T(8,128)(2,1)S(1)}, bf16[8,96,512]{2,1,0:T(8,128)(2,1)S(1)}, u32[]{:S(2)}, u32[]{:S(2)}) collective-permute-start(bf16[8,96,512]{2,1,0:T(8,128)(2,1)S(1)} %all-to-all-done.3), channel_id=1, source_target_pairs={{0,384},{128,0},{256,128},{384,256},{1,385},{129,1},{257,129},{385... | collective-permute-start | bytes 2359304 | tf_op jit(solution)/shard_map/ppermute | solution.py:116
  133.5 9.0 %copy-start.1 = (bf16[8,96,512]{2,1,0:T(8,128)(2,1)}, bf16[8,96,512]{2,1,0:T(8,128)(2,1)S(1)}, u32[]{:S(2)}) copy-start(bf16[8,96,512]{2,1,0:T(8,128)(2,1)S(1)} %collective-permute-done.1) | copy-start | bytes 2359300
  136.7 5.9 %copy-start.2 = (bf16[8,96,512]{2,1,0:T(8,128)(2,1)}, bf16[8,96,512]{2,1,0:T(8,128)(2,1)S(1)}, u32[]{:S(2)}) copy-start(bf16[8,96,512]{2,1,0:T(8,128)(2,1)S(1)} %collective-permute-done.2) | copy-start | bytes 2359300
  136.7 9.7 %collective-permute-start.3 = (bf16[4,96,512]{2,1,0:T(8,128)(2,1)S(1)}, bf16[4,96,512]{2,1,0:T(8,128)(2,1)S(1)}, u32[]{:S(2)}, u32[]{:S(2)}) collective-permute-start(bf16[4,96,512]{2,1,0:T(8,128)(2,1)S(1)} %slice.59), channel_id=1, source_target_pairs={{0,128},{128,256},{256,384},{384,0},{1,129},{129,257},{257,385},{3... | collective-permute-start | bytes 1179656 | tf_op jit(solution)/shard_map/ppermute | solution.py:118
  138.9 10.9 %collective-permute-start.4 = (bf16[4,96,512]{2,1,0:T(8,128)(2,1)S(1)}, bf16[4,96,512]{2,1,0:T(8,128)(2,1)S(1)}, u32[]{:S(2)}, u32[]{:S(2)}) collective-permute-start(bf16[4,96,512]{2,1,0:T(8,128)(2,1)S(1)} %slice.61), channel_id=1, source_target_pairs={{0,384},{128,0},{256,128},{384,256},{1,385},{129,1},{257,129},{385... | collective-permute-start | bytes 1179656 | tf_op jit(solution)/shard_map/ppermute | solution.py:119
  161.3 16.4 %collective-permute-start.6 = (bf16[8,96,512]{2,1,0:T(8,128)(2,1)S(1)}, bf16[8,96,512]{2,1,0:T(8,128)(2,1)S(1)}, u32[]{:S(2)}, u32[]{:S(2)}) collective-permute-start(bf16[8,96,512]{2,1,0:T(8,128)(2,1)S(1)} %shard_map.55.own), channel_id=1, source_target_pairs={{0,128},{128,256},{256,384},{384,0},{1,129},{129,257},{257,385},{3... | collective-permute-start | bytes 2359304 | tf_op jit(solution)/shard_map/ppermute | solution.py:116
  163.6 17.7 %collective-permute-start.5 = (bf16[8,96,512]{2,1,0:T(8,128)(2,1)S(1)}, bf16[8,96,512]{2,1,0:T(8,128)(2,1)S(1)}, u32[]{:S(2)}, u32[]{:S(2)}) collective-permute-start(bf16[8,96,512]{2,1,0:T(8,128)(2,1)S(1)} %shard_map.55.own), channel_id=1, source_target_pairs={{0,384},{128,0},{256,128},{384,256},{1,385},{129,1},{257,129},{385... | collective-permute-start | bytes 2359304 | tf_op jit(solution)/shard_map/ppermute | solution.py:116
  177.7 9.7 %collective-permute-start.7 = (bf16[4,96,512]{2,1,0:T(8,128)(2,1)S(1)}, bf16[4,96,512]{2,1,0:T(8,128)(2,1)S(1)}, u32[]{:S(2)}, u32[]{:S(2)}) collective-permute-start(bf16[4,96,512]{2,1,0:T(8,128)(2,1)S(1)} %slice.77), channel_id=1, source_target_pairs={{0,128},{128,256},{256,384},{384,0},{1,129},{129,257},{257,385},{3... | collective-permute-start | bytes 1179656 | tf_op jit(solution)/shard_map/ppermute | solution.py:118
  181.3 10.9 %collective-permute-start.8 = (bf16[4,96,512]{2,1,0:T(8,128)(2,1)S(1)}, bf16[4,96,512]{2,1,0:T(8,128)(2,1)S(1)}, u32[]{:S(2)}, u32[]{:S(2)}) collective-permute-start(bf16[4,96,512]{2,1,0:T(8,128)(2,1)S(1)} %slice.78), channel_id=1, source_target_pairs={{0,384},{128,0},{256,128},{384,256},{1,385},{129,1},{257,129},{385... | collective-permute-start | bytes 1179656 | tf_op jit(solution)/shard_map/ppermute | solution.py:119
Sparse Core Ops, SparseCore 0:
  78.9 63.8 all-gather.1

commit v7 on v6

--- a/solution.py
+++ b/solution.py
@@ -32,10 +32,27 @@
     return (wide * scale / math.sqrt(wide.shape[-1])).astype(BF)
 
 
-def sweep_kernel(index_ref, w_ref, prior_ref, own, after, oppa, oppb, before, out_ref, held, sems):
-    y = pl.program_id(0)
-
-    @pl.when(y == 0)
+GROUPS = (((0, 0), (1, 1), (2, 7)), ((0, 2), (1, 6)), ((0, 3), (1, 5), (2, 4)))
+
+
+def sweep_kernel(index_ref, prior_ref, *refs):
+    weights, (own, after, oppa, oppb, before), refs = refs[:6], refs[6:11], refs[11:]
+    out_ref, held, kept, sems, weight_sems = refs
+    step = pl.program_id(0)
+    y = lax.rem(index_ref[NY * PER + 1] - step + NY, NY)
+    size = NBLK * ROWS_C
+    brought = {
+        (side, back): pltpu.make_async_copy(
+            weights[3 * side + group].at[pl.ds(place * size, size)],
+            kept.at[side, back],
+            weight_sems.at[side, back],
+        )
+        for side in range(NC)
+        for group, places in enumerate(GROUPS)
+        for place, back in places
+    }
+
+    @pl.when(step == 0)
     def _():
         half = NY // 2
         places = (
@@ -51,27 +68,39 @@
         ]
         for copy in copies:
             copy.start()
+        for back in range(NY):
+            for side in range(NC):
+                brought[side, back].start()
         for copy in copies:
             copy.wait()
 
+    for back in range(NY):
+
+        @pl.when(step == back)
+        def _():
+            for side in range(NC):
+                brought[side, back].wait()
+
+    first_core = index_ref[NY * PER] == 0
     classes = out_ref.shape[1]
     lanes = lax.broadcasted_iota(jnp.int32, (classes, 128), 1) // QB
     for group in range(NBLK // 4):
         total = None
         for k in range(NT):
-            weights = jnp.concatenate(
-                [
-                    w_ref[c, pl.ds((4 * group + b) * ROWS_C, ROWS_C), pl.ds(k * TILE, TILE)]
-                    for b in range(4)
-                    for c in range(NC)
-                ],
-                axis=0,
-            )
+            rows = []
+            for b in range(4):
+                at = pl.ds((4 * group + b) * ROWS_C, ROWS_C), pl.ds(k * TILE, TILE)
+                mine, other = kept[0, step, *at], kept[1, step, *at]
+                rows.append(jnp.where(first_core, mine, other))
+                rows.append(jnp.where(first_core, other, mine))
             labels = jnp.concatenate(
                 [held[index_ref[y * PER + (4 * group + b) * NT + k]] for b in range(4)], axis=0
             )
             sums = lax.dot_general(
-                labels, weights, (((1,), (1,)), ((), ())), preferred_element_type=F32
+                labels,
+                jnp.concatenate(rows, axis=0),
+                (((1,), (1,)), ((), ())),
+                preferred_element_type=F32,
             )
             total = sums if total is None else total + sums
         picked = total[:classes]
@@ -84,30 +113,53 @@
 
 def sweep(index, weights, prior, pieces):
     ny, classes, rows = prior.shape
+
+    def by_y(step, index):
+        return lax.rem(index[NY * PER + 1] - step + NY, NY), 0, 0
+
     return pl.pallas_call(
         sweep_kernel,
         grid_spec=pltpu.PrefetchScalarGridSpec(
             num_scalar_prefetch=1,
             grid=(ny,),
-            in_specs=[
-                pl.BlockSpec((NC,) + weights.shape[1:], lambda y, _: (y, 0, 0)),
-                pl.BlockSpec((1, classes, rows), lambda y, _: (y, 0, 0)),
-            ]
-            + [pl.BlockSpec(memory_space=pl.ANY)] * len(pieces),
-            out_specs=pl.BlockSpec((1, classes, rows), lambda y, _: (y, 0, 0)),
+            in_specs=[pl.BlockSpec((1, classes, rows), by_y)]
+            + [pl.BlockSpec(memory_space=pl.ANY)] * (len(weights) + len(pieces)),
+            out_specs=pl.BlockSpec((1, classes, rows), by_y),
             scratch_shapes=[
                 pltpu.VMEM((TILES, classes, rows), BF),
+                pltpu.VMEM((NC, NY, NBLK * ROWS_C, NT * TILE), BF),
                 pltpu.SemaphoreType.DMA((len(pieces),)),
+                pltpu.SemaphoreType.DMA((NC, NY)),
             ],
         ),
         out_shape=jax.ShapeDtypeStruct(prior.shape, BF),
-        compiler_params=pltpu.CompilerParams(vmem_limit_bytes=48 << 20),
+        compiler_params=pltpu.CompilerParams(vmem_limit_bytes=32 << 20),
         cost_estimate=pl.CostEstimate(
             flops=2 * ny * rows * NT * TILE * classes * 4,
-            bytes_accessed=weights.size * 2 + 4 * prior.size * 2,
+            bytes_accessed=ny * rows * NT * TILE * 2 + 4 * prior.size * 2,
             transcendentals=0,
         ),
-    )(index, weights, prior, *pieces)
+    )(index, prior, *weights, *pieces)
+
+
+def around_y(mine):
+    forward = [(i, (i + 1) % NY) for i in range(NY)]
+    backward = [(i, (i - 1) % NY) for i in range(NY)]
+    before, after = [mine], [mine]
+    for _ in range(3):
+        before.append(lax.ppermute(before[-1], "y", forward))
+        after.append(lax.ppermute(after[-1], "y", backward))
+    half = mine.shape[0] // 2
+    far = (
+        lax.ppermute(before[3][:half], "y", forward),
+        lax.ppermute(after[3][half:], "y", backward),
+    )
+    groups = (
+        jnp.concatenate([mine, before[1], after[1]]),
+        jnp.concatenate([before[2], after[2]]),
+        jnp.concatenate([before[3], after[3], *far]),
+    )
+    return groups + tuple(lax.ppermute(g, "c", [(0, 1), (1, 0)]) for g in groups)
 
 
 def around_x(mine, beside=lambda *near: near):
@@ -179,7 +231,7 @@
     )
 
     piece = over_z[:, :NBLK].transpose(1, 0, 2, 3).reshape(NBLK * ROWS_C, NT * TILE)
-    weights = lax.all_gather(piece, ("y", "c"), axis=0, tiled=False)
+    weights = around_y(piece)
 
     terms = jnp.sum(over_z[:, NBLK].astype(F32), axis=0).reshape(4, rows)
     totals = terms[0] + terms[1] + terms[2]
@@ -209,6 +261,8 @@
     named = known[0, :, rows : rows + PER].astype(jnp.int32).reshape(NY * PER)
     index = (named // NY - x) % NX * NY + named % NY
 
+    index = jnp.concatenate([index, core.reshape(1), y.reshape(1)])
+
     labels = sweep(index, weights, priors[0], priors)
     spread = sweep(index, weights, priors[0], around_x(labels))
     spread = lax.all_to_all(spread, "y", 0, 0, tiled=True)

time: 237 us -> 280 us (1.18)
  starting transfers between devices: 52.4 us -> 92.1 us
  between operations: 14.4 us -> 1.25 us
  local copies, waits for them, and re-layouts: 10.1 us -> 19.4 us
  blocking collectives: 49.6 us -> 54.3 us
  waiting for transfers between devices: 80.3 us -> 84.1 us
    ppermute x0 -> x11, starting transfers between devices: none -> 33.9 us  [the longest x3 13.5 us: around_y(): after.append(lax.ppermute(after[-1], 'y', backward))]
    all_to_all x1, waiting for transfers between devices: 24.4 us -> 0.01 us  [on_device(): lax.all_to_all(raw.T.reshape(NY, classes // NY, rows), 'y', 0, 0, tiled=T...]
    ppermute x0 -> x11, waiting for transfers between devices: none -> 23.4 us  [the longest x3 23.1 us: around_y(): before.append(lax.ppermute(before[-1], 'y', forward))]
    ppermute x2, waiting for transfers between devices: 16.7 us -> 24 us  [around_x(): lax.ppermute(mine, 'x', forward)]
    unnamed x13 -> x15, local copies, waits for them, and re-layouts: 0.79 us -> 6.25 us
    all_to_all x1, blocking collectives: 23.4 us -> 28.2 us  [on_device(): spread = lax.all_to_all(spread, 'y', 0, 0, tiled=True)]
    ppermute x2, starting transfers between devices: 5.71 us -> 8.85 us  [around_x(): oppa = lax.ppermute(before[:half], 'x', forward)]
    ppermute x2, waiting for transfers between devices: 3.12 us -> 0.01 us  [around_x(): lax.ppermute(mine, 'x', backward)]
  transfers between devices with their start and end apart: 14 -> 24, of which waited for: 12 -> 13; matrix products, arithmetic and copies ran while one was open for 2% -> 6% of each run, Pallas kernels for 0% -> 0%
where the time goes in v7:
time: 280 us; the launch traced here: 278 us
  starting transfers between devices  92.1 us (33%)
  waiting for transfers between devices  84.1 us (30%)
  blocking collectives  54.3 us (19%)
  Pallas kernels  20.9 us (7%)
  local copies, waits for them, and re-layouts  19.4 us (7%)
  other arithmetic  4.97 us (2%)
    all_to_all x1, blocking collectives, on_device(): spread = lax.all_to_all(spread, 'y', 0, 0, tiled=True)  28.2 us
    all_to_all x1, blocking collectives, on_device(): lax.all_to_all(jnp.broadcast_to(piece, (NZ,) + piece.shape), 'z', 0, 0, t...  26 us
    ppermute x2, waiting for transfers between devices, around_x(): lax.ppermute(mine, 'x', forward)  24 us
    ppermute x3, waiting for transfers between devices, around_y(): before.append(lax.ppermute(before[-1], 'y', forward))  23.1 us
    pallas_call x2, Pallas kernels, sweep(): pl.pallas_call(sweep_kernel, grid_spec=pltpu.PrefetchScalarGridSpec(num_s...  20.9 us
    ppermute x3, starting transfers between devices, around_y(): after.append(lax.ppermute(after[-1], 'y', backward))  13.5 us
    all_to_all x1, waiting for transfers between devices, on_device(): lax.all_to_all(outgoing.reshape(TILES, 2 * SUB, width), ('x', 'y'), 0, 0,...  10.3 us
    all_to_all x1, starting transfers between devices, on_device(): lax.all_to_all(outgoing.reshape(TILES, 2 * SUB, width), ('x', 'y'), 0, 0,...  10.2 us
  transfers between devices with their start and end apart: 24, of which 13 were waited for; matrix products, arithmetic and copies ran while one was open for 6% of the time, Pallas kernels for 0%

profile of v7, /device:TPU:6, one launch (start us, length us, event | category | flops | bytes accessed | tf_op | source)
XLA Modules:
  0.0 278.1 jit_solution(146078439242464851)
XLA Ops:
  0.0 0.9 copy.53
  1.4 0.7 multiply_add_fusion
  2.1 1.1 constant_dynamic-slice_fusion.1
  3.5 0.9 reshape.106
  4.4 10.2 %all-to-all-start = ((bf16[32,4,1280]{2,1,0:T(4,128)(2,1)}), bf16[32,4,1280]{2,1,0:T(4,128)(2,1)S(1)}, u32[]{:S(2)}, u32[]{:S(2)}) async-start(bf16[32,4,1280]{2,1,0:T(4,128)(2,1)} %reshape.106), calls=%async_computation | async-start | bytes 655360 | tf_op jit(solution)/shard_map/all_to_all | solution.py:205
  15.4 0.3 exponential_reduce_fusion
  15.7 0.3 fusion
  16.0 10.3 %all-to-all-done = bf16[32,4,1280]{2,1,0:T(4,128)(2,1)S(1)} async-done(((bf16[32,4,1280]{2,1,0:T(4,128)(2,1)}), bf16[32,4,1280]{2,1,0:T(4,128)(2,1)S(1)}, u32[]{:S(2)}, u32[]{:S(2)}) %all-to-all-start) | async-done | bytes 327712 | tf_op jit(solution)/shard_map/all_to_all | solution.py:205
  26.8 0.7 fusion.16
  27.5 0.7 reshape.107
  28.2 6.6 %all-to-all-start.1 = ((bf16[32,4,512]{2,1,0:T(4,128)(2,1)}), bf16[32,4,512]{2,1,0:T(4,128)(2,1)S(1)}, u32[]{:S(2)}, u32[]{:S(2)}) async-start(bf16[32,4,512]{2,1,0:T(4,128)(2,1)} %reshape.107), calls=%async_computation.1 | async-start | bytes 262144 | tf_op jit(solution)/shard_map/all_to_all | solution.py:216
  34.8 8.5 %all-to-all-done.1 = bf16[32,4,512]{2,1,0:T(4,128)(2,1)S(1)} async-done(((bf16[32,4,512]{2,1,0:T(4,128)(2,1)}), bf16[32,4,512]{2,1,0:T(4,128)(2,1)S(1)}, u32[]{:S(2)}, u32[]{:S(2)}) %all-to-all-start.1) | async-done | bytes 131104 | tf_op jit(solution)/shard_map/all_to_all | solution.py:216
  44.1 26.0 %all_to_all.31 = bf16[8,17,2,1024]{3,2,1,0:T(2,128)(2,1)S(1)} all-to-all(bf16[8,17,2,1024]{3,2,1,0:T(2,128)(2,1)S(1)} %broadcast_in_dim.30), channel_id=1, replica_groups=mesh['x'=4,'y'=8,'z'=8,'c'=2] {'z'}, dimensions={0} | all-to-all | bytes 1114112 | tf_op jit(solution)/shard_map/all_to_all | solution.py:229
  70.2 1.2 copy.59
  71.3 3.5 %all-to-all-start.3 = ((bf16[8,96,512]{2,1,0:T(8,128)(2,1)}), bf16[8,96,512]{2,1,0:T(8,128)(2,1)S(1)}, u32[]{:S(2)}, u32[]{:S(2)}) async-start(bf16[8,96,512]{2,1,0:T(8,128)(2,1)} %bitcast.9), calls=%async_computation.3 | async-start | bytes 1572864 | tf_op jit(solution)/shard_map/all_to_all | solution.py:239
  74.9 0.4 slice_bitcast_fusion
  75.3 0.5 copy.60
  76.0 3.8 %collective-permute-start.1 = (bf16[256,1024]{1,0:T(8,128)(2,1)S(1)}, bf16[256,1024]{1,0:T(8,128)(2,1)}, u32[]{:S(2)}, u32[]{:S(2)}) collective-permute-start(bf16[256,1024]{1,0:T(8,128)(2,1)S(1)} %reshape.117), channel_id=1, source_target_pairs={{0,16},{16,32},{32,48},{48,64},{64,80},{80,96},{96,112},{112,0},{1... | collective-permute-start | bytes 1572872 | tf_op jit(solution)/shard_map/ppermute | solution.py:150
  79.8 3.2 %collective-permute-start.2 = (bf16[256,1024]{1,0:T(8,128)(2,1)S(1)}, bf16[256,1024]{1,0:T(8,128)(2,1)S(1)}, u32[]{:S(2)}, u32[]{:S(2)}) collective-permute-start(bf16[256,1024]{1,0:T(8,128)(2,1)S(1)} %reshape.117), channel_id=1, source_target_pairs={{0,112},{16,0},{32,16},{48,32},{64,48},{80,64},{96,80},{112,96},{1... | collective-permute-start | bytes 1572872 | tf_op jit(solution)/shard_map/ppermute | solution.py:151
  83.1 19.1 %collective-permute-done.1 = bf16[256,1024]{1,0:T(8,128)(2,1)} collective-permute-done((bf16[256,1024]{1,0:T(8,128)(2,1)S(1)}, bf16[256,1024]{1,0:T(8,128)(2,1)}, u32[]{:S(2)}, u32[]{:S(2)}) %collective-permute-start.1) | collective-permute-done | bytes 524320 | tf_op jit(solution)/shard_map/ppermute | solution.py:150
  102.3 1.9 collective-permute-start.3
  104.3 5.1 %collective-permute-start.4 = (bf16[256,1024]{1,0:T(8,128)(2,1)S(1)}, bf16[256,1024]{1,0:T(8,128)(2,1)}, u32[]{:S(2)}, u32[]{:S(2)}) collective-permute-start(bf16[256,1024]{1,0:T(8,128)(2,1)S(1)} %collective-permute-done.2), channel_id=1, source_target_pairs={{0,112},{16,0},{32,16},{48,32},{64,48},{80,64},{96,80},{112,96},{1... | collective-permute-start | bytes 1572872 | tf_op jit(solution)/shard_map/ppermute | solution.py:151
  109.4 1.9 collective-permute-start
  111.4 1.1 collective-permute-done
  112.6 4.0 %collective-permute-done.3 = bf16[256,1024]{1,0:T(8,128)(2,1)} collective-permute-done((bf16[256,1024]{1,0:T(8,128)(2,1)}, bf16[256,1024]{1,0:T(8,128)(2,1)}, u32[]{:S(2)}, u32[]{:S(2)}) %collective-permute-start.3) | collective-permute-done | bytes 524320 | tf_op jit(solution)/shard_map/ppermute | solution.py:150
  116.6 1.9 collective-permute-start.5
  118.5 1.1 constant_dynamic-update-slice_fusion.1
  119.6 1.9 collective-permute-start.9
  121.5 5.1 %collective-permute-start.6 = (bf16[256,1024]{1,0:T(8,128)(2,1)}, bf16[256,1024]{1,0:T(8,128)(2,1)}, u32[]{:S(2)}, u32[]{:S(2)}) collective-permute-start(bf16[256,1024]{1,0:T(8,128)(2,1)} %collective-permute-done.4), channel_id=1, source_target_pairs={{0,112},{16,0},{32,16},{48,32},{64,48},{80,64},{96,80},{112,96},{1... | collective-permute-start | bytes 1572872 | tf_op jit(solution)/shard_map/ppermute | solution.py:151
  126.7 0.7 broadcast_in_dim.32
  127.4 9.6 %all-to-all-start.4 = ((f32[32,1,640]{2,1,0:T(1,128)}), f32[32,1,640]{2,1,0:T(1,128)S(1)}, u32[]{:S(2)}, u32[]{:S(2)}) async-start(f32[32,1,640]{2,1,0:T(1,128)} %broadcast_in_dim.32), calls=%async_computation.4 | async-start | bytes 163840 | tf_op jit(solution)/shard_map/all_to_all | solution.py:245
  137.0 1.1 constant_dynamic-update-slice_fusion.4
  138.0 1.1 constant_dynamic-update-slice_fusion.3.refs_1_
  139.1 1.9 collective-permute-start.10
  141.1 2.7 collective-permute-start.13
  143.8 1.4 all-to-all-done.4
  145.2 1.7 slice.81
  146.9 3.9 %collective-permute-start.7 = (bf16[128,1024]{1,0:T(8,128)(2,1)}, bf16[128,1024]{1,0:T(8,128)(2,1)}, u32[]{:S(2)}, u32[]{:S(2)}) collective-permute-start(bf16[128,1024]{1,0:T(8,128)(2,1)} %slice.81), channel_id=1, source_target_pairs={{0,16},{16,32},{32,48},{48,64},{64,80},{80,96},{96,112},{112,0},{1... | collective-permute-start | bytes 786440 | tf_op jit(solution)/shard_map/ppermute | solution.py:154
  150.9 1.0 slice.82
  151.8 3.2 %collective-permute-start.8 = (bf16[128,1024]{1,0:T(8,128)(2,1)S(1)}, bf16[128,1024]{1,0:T(8,128)(2,1)S(1)}, u32[]{:S(2)}, u32[]{:S(2)}) collective-permute-start(bf16[128,1024]{1,0:T(8,128)(2,1)S(1)} %slice.82), channel_id=1, source_target_pairs={{0,112},{16,0},{32,16},{48,32},{64,48},{80,64},{96,80},{112,96},{1... | collective-permute-start | bytes 786440 | tf_op jit(solution)/shard_map/ppermute | solution.py:155
  155.0 1.1 constant_dynamic-update-slice_fusion.8
  156.1 1.1 constant_dynamic-update-slice_fusion.7
  157.4 4.3 %collective-permute-start.12 = (bf16[8,96,512]{2,1,0:T(8,128)(2,1)S(1)}, bf16[8,96,512]{2,1,0:T(8,128)(2,1)S(1)}, u32[]{:S(2)}, u32[]{:S(2)}) collective-permute-start(bf16[8,96,512]{2,1,0:T(8,128)(2,1)S(1)} %all-to-all-done.3), channel_id=1, source_target_pairs={{0,128},{128,256},{256,384},{384,0},{1,129},{129,257},{257,385},{3... | collective-permute-start | bytes 2359304 | tf_op jit(solution)/shard_map/ppermute | solution.py:168
  161.7 1.0 constant_dynamic-update-slice_fusion.6
  162.7 1.9 collective-permute-start.11
  164.8 12.2 %collective-permute-done.12 = bf16[8,96,512]{2,1,0:T(8,128)(2,1)S(1)} collective-permute-done((bf16[8,96,512]{2,1,0:T(8,128)(2,1)S(1)}, bf16[8,96,512]{2,1,0:T(8,128)(2,1)S(1)}, u32[]{:S(2)}, u32[]{:S(2)}) %collective-permute-start.12) | collective-permute-done | bytes 786464 | tf_op jit(solution)/shard_map/ppermute | solution.py:168
  176.9 1.0 slice.69
  178.0 5.6 %collective-permute-start.14 = (bf16[4,96,512]{2,1,0:T(8,128)(2,1)S(1)}, bf16[4,96,512]{2,1,0:T(8,128)(2,1)S(1)}, u32[]{:S(2)}, u32[]{:S(2)}) collective-permute-start(bf16[4,96,512]{2,1,0:T(8,128)(2,1)S(1)} %slice.67), channel_id=1, source_target_pairs={{0,128},{128,256},{256,384},{384,0},{1,129},{129,257},{257,385},{3... | collective-permute-start | bytes 1179656 | tf_op jit(solution)/shard_map/ppermute | solution.py:170
  183.6 1.9 collective-permute-start.15
  185.5 2.1 divide_convert_fusion
  187.6 1.9 collective-permute-done.14
  189.5 5.3 %collective-permute-done.15 = bf16[4,96,512]{2,1,0:T(8,128)(2,1)S(1)} collective-permute-done((bf16[4,96,512]{2,1,0:T(8,128)(2,1)S(1)}, bf16[4,96,512]{2,1,0:T(8,128)(2,1)S(1)}, u32[]{:S(2)}, u32[]{:S(2)}) %collective-permute-start.15) | collective-permute-done | bytes 393248 | tf_op jit(solution)/shard_map/ppermute | solution.py:171
  194.8 0.4 divide_convert_fusion.3
  195.2 10.4 %shard_map.55.refs_6_ = bf16[8,96,512]{2,1,0:T(8,128)(2,1)S(1)} custom-call(s32[258]{0:T(512)S(1)} %pad_add_fusion.index_ref, bf16[8,96,512]{2,1,0:T(8,128)(2,1)S(1)} %get-tuple-element.23.prior_ref.refs_6_, bf16[768,1024]{1,0:T(8,128)(2,1)S(1)} %constant_dynamic-update-slice_fusion.refs_0_, ...), custom_call_target="tpu_custom_call" | custom-call | flops 3221225472 | bytes 11534336 | tf_op jit(solution)/shard_map/pallas_call | solution.py:120
  205.7 1.9 collective-permute-start.17
  207.6 3.9 %collective-permute-start.16 = (bf16[8,96,512]{2,1,0:T(8,128)(2,1)S(1)}, bf16[8,96,512]{2,1,0:T(8,128)(2,1)S(1)}, u32[]{:S(2)}, u32[]{:S(2)}) collective-permute-start(bf16[8,96,512]{2,1,0:T(8,128)(2,1)S(1)} %shard_map.55.refs_6_), channel_id=1, source_target_pairs={{0,384},{128,0},{256,128},{384,256},{1,385},{129,1},{257,129},{385... | collective-permute-start | bytes 2359304 | tf_op jit(solution)/shard_map/ppermute | solution.py:168
  211.5 11.8 %collective-permute-done.17.refs_10_ = bf16[8,96,512]{2,1,0:T(8,128)(2,1)S(1)} collective-permute-done((bf16[8,96,512]{2,1,0:T(8,128)(2,1)S(1)}, bf16[8,96,512]{2,1,0:T(8,128)(2,1)S(1)}, u32[]{:S(2)}, u32[]{:S(2)}) %collective-permute-start.17) | collective-permute-done | bytes 786464 | tf_op jit(solution)/shard_map/ppermute | solution.py:168
  223.4 3.2 %collective-permute-start.18 = (bf16[4,96,512]{2,1,0:T(8,128)(2,1)S(1)}, bf16[4,96,512]{2,1,0:T(8,128)(2,1)S(1)}, u32[]{:S(2)}, u32[]{:S(2)}) collective-permute-start(bf16[4,96,512]{2,1,0:T(8,128)(2,1)S(1)} %slice.87), channel_id=1, source_target_pairs={{0,128},{128,256},{256,384},{384,0},{1,129},{129,257},{257,385},{3... | collective-permute-start | bytes 1179656 | tf_op jit(solution)/shard_map/ppermute | solution.py:170
  226.7 2.6 collective-permute-start.19
  229.3 3.8 %collective-permute-done.18.refs_8_ = bf16[4,96,512]{2,1,0:T(8,128)(2,1)S(1)} collective-permute-done((bf16[4,96,512]{2,1,0:T(8,128)(2,1)S(1)}, bf16[4,96,512]{2,1,0:T(8,128)(2,1)S(1)}, u32[]{:S(2)}, u32[]{:S(2)}) %collective-permute-start.18) | collective-permute-done | bytes 393248 | tf_op jit(solution)/shard_map/ppermute | solution.py:170
  233.1 4.5 %collective-permute-done.19.refs_9_ = bf16[4,96,512]{2,1,0:T(8,128)(2,1)S(1)} collective-permute-done((bf16[4,96,512]{2,1,0:T(8,128)(2,1)S(1)}, bf16[4,96,512]{2,1,0:T(8,128)(2,1)S(1)}, u32[]{:S(2)}, u32[]{:S(2)}) %collective-permute-start.19) | collective-permute-done | bytes 393248 | tf_op jit(solution)/shard_map/ppermute | solution.py:171
  237.6 10.4 %shard_map.56 = bf16[8,96,512]{2,1,0:T(8,128)(2,1)S(1)} custom-call(s32[258]{0:T(512)S(1)} %pad_add_fusion.index_ref, bf16[8,96,512]{2,1,0:T(8,128)(2,1)S(1)} %get-tuple-element.23.prior_ref.refs_6_, bf16[768,1024]{1,0:T(8,128)(2,1)S(1)} %constant_dynamic-update-slice_fusion.refs_0_, bf16[512,1024]{1,0:T(8,128)(2,1)S(1)} %constant_dynamic-update-slice_fusion.3.refs_1_, ...), custom_call_target="tpu_custom_call" | custom-call | flops 3221225472 | bytes 11534336 | tf_op jit(solution)/shard_map/pallas_call | solution.py:120
  248.0 28.2 %all_to_all.32 = bf16[8,96,512]{2,1,0:T(8,128)(2,1)S(1)} all-to-all(bf16[8,96,512]{2,1,0:T(8,128)(2,1)S(1)} %shard_map.56), channel_id=1, replica_groups=mesh['x'=4,'y'=8,'z'=8,'c'=2] {'y'}, dimensions={0} | all-to-all | bytes 1572864 | tf_op jit(solution)/shard_map/all_to_all | solution.py:268
  276.5 1.6 copy.61
  (67 shorter events, 3.4 us)
Async XLA Ops:
  0.0 15.7 %copy-start.1 = (bf16[512,1280]{1,0:T(8,128)(2,1)S(1)}, bf16[512,1280]{1,0:T(8,128)(2,1)}, u32[]{:S(2)}) copy-start(bf16[512,1280]{1,0:T(8,128)(2,1)} %param.5) | copy-start | bytes 3932164
  0.0 15.3 %copy-start = (bf16[512,768]{1,0:T(8,128)(2,1)S(1)}, bf16[512,768]{1,0:T(8,128)(2,1)}, u32[]{:S(2)}) copy-start(bf16[512,768]{1,0:T(8,128)(2,1)} %param.7) | copy-start | bytes 2359300
  0.0 15.3 %copy-start.2 = (f32[768]{0:T(1024)S(1)}, f32[768]{0:T(1024)}, u32[]{:S(2)}) copy-start(f32[768]{0:T(1024)} %param.6) | copy-start | bytes 9220
  4.4 21.9 %all-to-all-start = ((bf16[32,4,1280]{2,1,0:T(4,128)(2,1)}), bf16[32,4,1280]{2,1,0:T(4,128)(2,1)S(1)}, u32[]{:S(2)}, u32[]{:S(2)}) async-start(bf16[32,4,1280]{2,1,0:T(4,128)(2,1)} %reshape.106), calls=%async_computation | async-start | bytes 655360 | tf_op jit(solution)/shard_map/all_to_all | solution.py:205
  28.2 15.1 %all-to-all-start.1 = ((bf16[32,4,512]{2,1,0:T(4,128)(2,1)}), bf16[32,4,512]{2,1,0:T(4,128)(2,1)S(1)}, u32[]{:S(2)}, u32[]{:S(2)}) async-start(bf16[32,4,512]{2,1,0:T(4,128)(2,1)} %reshape.107), calls=%async_computation.1 | async-start | bytes 262144 | tf_op jit(solution)/shard_map/all_to_all | solution.py:216
  71.3 55.3 %all-to-all-start.3 = ((bf16[8,96,512]{2,1,0:T(8,128)(2,1)}), bf16[8,96,512]{2,1,0:T(8,128)(2,1)S(1)}, u32[]{:S(2)}, u32[]{:S(2)}) async-start(bf16[8,96,512]{2,1,0:T(8,128)(2,1)} %bitcast.9), calls=%async_computation.3 | async-start | bytes 1572864 | tf_op jit(solution)/shard_map/all_to_all | solution.py:239
  76.0 26.3 %collective-permute-start.1 = (bf16[256,1024]{1,0:T(8,128)(2,1)S(1)}, bf16[256,1024]{1,0:T(8,128)(2,1)}, u32[]{:S(2)}, u32[]{:S(2)}) collective-permute-start(bf16[256,1024]{1,0:T(8,128)(2,1)S(1)} %reshape.117), channel_id=1, source_target_pairs={{0,16},{16,32},{32,48},{48,64},{64,80},{80,96},{96,112},{112,0},{1... | collective-permute-start | bytes 1572872 | tf_op jit(solution)/shard_map/ppermute | solution.py:150
  79.8 24.5 %collective-permute-start.2 = (bf16[256,1024]{1,0:T(8,128)(2,1)S(1)}, bf16[256,1024]{1,0:T(8,128)(2,1)S(1)}, u32[]{:S(2)}, u32[]{:S(2)}) collective-permute-start(bf16[256,1024]{1,0:T(8,128)(2,1)S(1)} %reshape.117), channel_id=1, source_target_pairs={{0,112},{16,0},{32,16},{48,32},{64,48},{80,64},{96,80},{112,96},{1... | collective-permute-start | bytes 1572872 | tf_op jit(solution)/shard_map/ppermute | solution.py:151
  102.3 14.3 %collective-permute-start.3 = (bf16[256,1024]{1,0:T(8,128)(2,1)}, bf16[256,1024]{1,0:T(8,128)(2,1)}, u32[]{:S(2)}, u32[]{:S(2)}) collective-permute-start(bf16[256,1024]{1,0:T(8,128)(2,1)} %collective-permute-done.1), channel_id=1, source_target_pairs={{0,16},{16,32},{32,48},{48,64},{64,80},{80,96},{96,112},{112,0},{1... | collective-permute-start | bytes 1572872 | tf_op jit(solution)/shard_map/ppermute | solution.py:150
  104.3 17.3 %collective-permute-start.4 = (bf16[256,1024]{1,0:T(8,128)(2,1)S(1)}, bf16[256,1024]{1,0:T(8,128)(2,1)}, u32[]{:S(2)}, u32[]{:S(2)}) collective-permute-start(bf16[256,1024]{1,0:T(8,128)(2,1)S(1)} %collective-permute-done.2), channel_id=1, source_target_pairs={{0,112},{16,0},{32,16},{48,32},{64,48},{80,64},{96,80},{112,96},{1... | collective-permute-start | bytes 1572872 | tf_op jit(solution)/shard_map/ppermute | solution.py:151
  109.4 3.1 %collective-permute-start = (f32[512]{0:T(512)S(1)}, f32[512]{0:T(512)S(1)}, u32[]{:S(2)}, u32[]{:S(2)}) collective-permute-start(f32[512]{0:T(512)S(1)} %bitcast.62), channel_id=1, source_target_pairs={{0,1},{1,0},{2,3},{3,2},{4,5},{5,4},{6,7},{7,6},{8,9},{9,8},{10,11... | collective-permute-start | bytes 6152 | tf_op jit(solution)/shard_map/ppermute | solution.py:242
  116.6 28.6 %collective-permute-start.5 = (bf16[256,1024]{1,0:T(8,128)(2,1)}, bf16[256,1024]{1,0:T(8,128)(2,1)}, u32[]{:S(2)}, u32[]{:S(2)}) collective-permute-start(bf16[256,1024]{1,0:T(8,128)(2,1)} %collective-permute-done.3), channel_id=1, source_target_pairs={{0,16},{16,32},{32,48},{48,64},{64,80},{80,96},{96,112},{112,0},{1... | collective-permute-start | bytes 1572872 | tf_op jit(solution)/shard_map/ppermute | solution.py:150
  119.6 75.6 %collective-permute-start.9 = (bf16[768,1024]{1,0:T(8,128)(2,1)S(1)}, bf16[768,1024]{1,0:T(8,128)(2,1)}, u32[]{:S(2)}, u32[]{:S(2)}) collective-permute-start(bf16[768,1024]{1,0:T(8,128)(2,1)S(1)} %constant_dynamic-update-slice_fusion.refs_0_), channel_id=1, source_target_pairs={{0,1},{1,0},{2,3},{3,2},{4,5},{5,4},{6,7},{7,6},{8,9},{9,8},{10,11... | collective-permute-start | bytes 4718600 | tf_op jit(solution)/shard_map/ppermute | solution.py:162
  121.5 29.3 %collective-permute-start.6 = (bf16[256,1024]{1,0:T(8,128)(2,1)}, bf16[256,1024]{1,0:T(8,128)(2,1)}, u32[]{:S(2)}, u32[]{:S(2)}) collective-permute-start(bf16[256,1024]{1,0:T(8,128)(2,1)} %collective-permute-done.4), channel_id=1, source_target_pairs={{0,112},{16,0},{32,16},{48,32},{64,48},{80,64},{96,80},{112,96},{1... | collective-permute-start | bytes 1572872 | tf_op jit(solution)/shard_map/ppermute | solution.py:151
  127.4 17.8 %all-to-all-start.4 = ((f32[32,1,640]{2,1,0:T(1,128)}), f32[32,1,640]{2,1,0:T(1,128)S(1)}, u32[]{:S(2)}, u32[]{:S(2)}) async-start(f32[32,1,640]{2,1,0:T(1,128)} %broadcast_in_dim.32), calls=%async_computation.4 | async-start | bytes 163840 | tf_op jit(solution)/shard_map/all_to_all | solution.py:245
  139.1 56.1 %collective-permute-start.10 = (bf16[512,1024]{1,0:T(8,128)(2,1)S(1)}, bf16[512,1024]{1,0:T(8,128)(2,1)}, u32[]{:S(2)}, u32[]{:S(2)}) collective-permute-start(bf16[512,1024]{1,0:T(8,128)(2,1)S(1)} %constant_dynamic-update-slice_fusion.3.refs_1_), channel_id=1, source_target_pairs={{0,1},{1,0},{2,3},{3,2},{4,5},{5,4},{6,7},{7,6},{8,9},{9,8},{10,11... | collective-permute-start | bytes 3145736 | tf_op jit(solution)/shard_map/ppermute | solution.py:162
  141.1 23.7 %collective-permute-start.13 = (bf16[8,96,512]{2,1,0:T(8,128)(2,1)S(1)}, bf16[8,96,512]{2,1,0:T(8,128)(2,1)}, u32[]{:S(2)}, u32[]{:S(2)}) collective-permute-start(bf16[8,96,512]{2,1,0:T(8,128)(2,1)S(1)} %all-to-all-done.3), channel_id=1, source_target_pairs={{0,384},{128,0},{256,128},{384,256},{1,385},{129,1},{257,129},{385... | collective-permute-start | bytes 2359304 | tf_op jit(solution)/shard_map/ppermute | solution.py:168
  146.9 10.5 %collective-permute-start.7 = (bf16[128,1024]{1,0:T(8,128)(2,1)}, bf16[128,1024]{1,0:T(8,128)(2,1)}, u32[]{:S(2)}, u32[]{:S(2)}) collective-permute-start(bf16[128,1024]{1,0:T(8,128)(2,1)} %slice.81), channel_id=1, source_target_pairs={{0,16},{16,32},{32,48},{48,64},{64,80},{80,96},{96,112},{112,0},{1... | collective-permute-start | bytes 786440 | tf_op jit(solution)/shard_map/ppermute | solution.py:154
  151.8 10.8 %collective-permute-start.8 = (bf16[128,1024]{1,0:T(8,128)(2,1)S(1)}, bf16[128,1024]{1,0:T(8,128)(2,1)S(1)}, u32[]{:S(2)}, u32[]{:S(2)}) collective-permute-start(bf16[128,1024]{1,0:T(8,128)(2,1)S(1)} %slice.82), channel_id=1, source_target_pairs={{0,112},{16,0},{32,16},{48,32},{64,48},{80,64},{96,80},{112,96},{1... | collective-permute-start | bytes 786440 | tf_op jit(solution)/shard_map/ppermute | solution.py:155
  157.4 19.6 %collective-permute-start.12 = (bf16[8,96,512]{2,1,0:T(8,128)(2,1)S(1)}, bf16[8,96,512]{2,1,0:T(8,128)(2,1)S(1)}, u32[]{:S(2)}, u32[]{:S(2)}) collective-permute-start(bf16[8,96,512]{2,1,0:T(8,128)(2,1)S(1)} %all-to-all-done.3), channel_id=1, source_target_pairs={{0,128},{128,256},{256,384},{384,0},{1,129},{129,257},{257,385},{3... | collective-permute-start | bytes 2359304 | tf_op jit(solution)/shard_map/ppermute | solution.py:168
  162.7 32.5 %collective-permute-start.11 = (bf16[768,1024]{1,0:T(8,128)(2,1)S(1)}, bf16[768,1024]{1,0:T(8,128)(2,1)S(1)}, u32[]{:S(2)}, u32[]{:S(2)}) collective-permute-start(bf16[768,1024]{1,0:T(8,128)(2,1)S(1)} %constant_dynamic-update-slice_fusion.5.refs_2_), channel_id=1, source_target_pairs={{0,1},{1,0},{2,3},{3,2},{4,5},{5,4},{6,7},{7,6},{8,9},{9,8},{10,11... | collective-permute-start | bytes 4718600 | tf_op jit(solution)/shard_map/ppermute | solution.py:162
  178.0 11.5 %collective-permute-start.14 = (bf16[4,96,512]{2,1,0:T(8,128)(2,1)S(1)}, bf16[4,96,512]{2,1,0:T(8,128)(2,1)S(1)}, u32[]{:S(2)}, u32[]{:S(2)}) collective-permute-start(bf16[4,96,512]{2,1,0:T(8,128)(2,1)S(1)} %slice.67), channel_id=1, source_target_pairs={{0,128},{128,256},{256,384},{384,0},{1,129},{129,257},{257,385},{3... | collective-permute-start | bytes 1179656 | tf_op jit(solution)/shard_map/ppermute | solution.py:170
  183.6 11.2 %collective-permute-start.15 = (bf16[4,96,512]{2,1,0:T(8,128)(2,1)S(1)}, bf16[4,96,512]{2,1,0:T(8,128)(2,1)S(1)}, u32[]{:S(2)}, u32[]{:S(2)}) collective-permute-start(bf16[4,96,512]{2,1,0:T(8,128)(2,1)S(1)} %slice.69), channel_id=1, source_target_pairs={{0,384},{128,0},{256,128},{384,256},{1,385},{129,1},{257,129},{385... | collective-permute-start | bytes 1179656 | tf_op jit(solution)/shard_map/ppermute | solution.py:171
  205.7 17.7 %collective-permute-start.17 = (bf16[8,96,512]{2,1,0:T(8,128)(2,1)S(1)}, bf16[8,96,512]{2,1,0:T(8,128)(2,1)S(1)}, u32[]{:S(2)}, u32[]{:S(2)}) collective-permute-start(bf16[8,96,512]{2,1,0:T(8,128)(2,1)S(1)} %shard_map.55.refs_6_), channel_id=1, source_target_pairs={{0,128},{128,256},{256,384},{384,0},{1,129},{129,257},{257,385},{3... | collective-permute-start | bytes 2359304 | tf_op jit(solution)/shard_map/ppermute | solution.py:168
  207.6 19.0 %collective-permute-start.16 = (bf16[8,96,512]{2,1,0:T(8,128)(2,1)S(1)}, bf16[8,96,512]{2,1,0:T(8,128)(2,1)S(1)}, u32[]{:S(2)}, u32[]{:S(2)}) collective-permute-start(bf16[8,96,512]{2,1,0:T(8,128)(2,1)S(1)} %shard_map.55.refs_6_), channel_id=1, source_target_pairs={{0,384},{128,0},{256,128},{384,256},{1,385},{129,1},{257,129},{385... | collective-permute-start | bytes 2359304 | tf_op jit(solution)/shard_map/ppermute | solution.py:168
  223.4 9.7 %collective-permute-start.18 = (bf16[4,96,512]{2,1,0:T(8,128)(2,1)S(1)}, bf16[4,96,512]{2,1,0:T(8,128)(2,1)S(1)}, u32[]{:S(2)}, u32[]{:S(2)}) collective-permute-start(bf16[4,96,512]{2,1,0:T(8,128)(2,1)S(1)} %slice.87), channel_id=1, source_target_pairs={{0,128},{128,256},{256,384},{384,0},{1,129},{129,257},{257,385},{3... | collective-permute-start | bytes 1179656 | tf_op jit(solution)/shard_map/ppermute | solution.py:170
  226.7 10.9 %collective-permute-start.19 = (bf16[4,96,512]{2,1,0:T(8,128)(2,1)S(1)}, bf16[4,96,512]{2,1,0:T(8,128)(2,1)S(1)}, u32[]{:S(2)}, u32[]{:S(2)}) collective-permute-start(bf16[4,96,512]{2,1,0:T(8,128)(2,1)S(1)} %slice.88), channel_id=1, source_target_pairs={{0,384},{128,0},{256,128},{384,256},{1,385},{129,1},{257,129},{385... | collective-permute-start | bytes 1179656 | tf_op jit(solution)/shard_map/ppermute | solution.py:171

commit v8 on v6

--- a/solution.py
+++ b/solution.py
@@ -82,7 +82,7 @@
         out_ref[0, :, at] = (picked + (1.0 - ALPHA) * prior).astype(BF)
 
 
-def sweep(index, weights, prior, pieces):
+def sweep(index, weights, prior, pieces, grant):
     ny, classes, rows = prior.shape
     return pl.pallas_call(
         sweep_kernel,
@@ -101,7 +101,7 @@
             ],
         ),
         out_shape=jax.ShapeDtypeStruct(prior.shape, BF),
-        compiler_params=pltpu.CompilerParams(vmem_limit_bytes=48 << 20),
+        compiler_params=pltpu.CompilerParams(vmem_limit_bytes=grant << 20),
         cost_estimate=pl.CostEstimate(
             flops=2 * ny * rows * NT * TILE * classes * 4,
             bytes_accessed=weights.size * 2 + 4 * prior.size * 2,
@@ -110,10 +110,11 @@
     )(index, weights, prior, *pieces)
 
 
-def around_x(mine, beside=lambda *near: near):
+def around_x(mine):
     forward = [(i, (i + 1) % NX) for i in range(NX)]
     backward = [(i, (i - 1) % NX) for i in range(NX)]
-    before, after = beside(lax.ppermute(mine, "x", forward), lax.ppermute(mine, "x", backward))
+    before = lax.ppermute(mine, "x", forward)
+    after = lax.ppermute(mine, "x", backward)
     half = NY // 2
     oppa = lax.ppermute(before[:half], "x", forward)
     oppb = lax.ppermute(after[half:], "x", backward)
@@ -193,7 +194,7 @@
     known = lax.all_to_all(
         jnp.broadcast_to(known, (TILES,) + known.shape), ("x", "y"), 0, 0, tiled=True
     )
-    raw = around_x(raw, lambda *near: lax.optimization_barrier((*near, known))[:2])
+    raw = around_x(raw)
     known = known.reshape(NX, NY, -1)
     known = lax.dynamic_slice_in_dim(jnp.concatenate([known, known]), x, NX, axis=0)
     totals = known[:, :, :rows]
@@ -209,8 +210,8 @@
     named = known[0, :, rows : rows + PER].astype(jnp.int32).reshape(NY * PER)
     index = (named // NY - x) % NX * NY + named % NY
 
-    labels = sweep(index, weights, priors[0], priors)
-    spread = sweep(index, weights, priors[0], around_x(labels))
+    labels = sweep(index, weights, priors[0], priors, 48)
+    spread = sweep(index, weights, priors[0], around_x(labels), 16)
     spread = lax.all_to_all(spread, "y", 0, 0, tiled=True)
     return jnp.log(spread.reshape(classes, rows).T.astype(F32))
 

time: 237 us -> 233 us (0.983)
  transfers between devices with their start and end apart: 14 -> 14, of which waited for: 12 -> 11; matrix products, arithmetic and copies ran while one was open for 2% -> 2% of each run, Pallas kernels for 0% -> 0%
where the time goes in v8:
time: 233 us
  waiting for transfers between devices  79.7 us (34%)
  starting transfers between devices  52.6 us (23%)
  blocking collectives  48.9 us (21%)
  Pallas kernels  20.4 us (9%)
  between operations  14.5 us (6%)
  local copies, waits for them, and re-layouts  10.1 us (4%)
  other arithmetic  5.11 us (2%)
    all_to_all x1, blocking collectives, on_device(): lax.all_to_all(jnp.broadcast_to(piece, (NZ,) + piece.shape), 'z', 0, 0, t...  26.1 us
    all_to_all x1, waiting for transfers between devices, on_device(): lax.all_to_all(raw.T.reshape(NY, classes // NY, rows), 'y', 0, 0, tiled=T...  24.4 us
    all_to_all x1, blocking collectives, on_device(): spread = lax.all_to_all(spread, 'y', 0, 0, tiled=True)  22.8 us
    pallas_call x2, Pallas kernels, sweep(): pl.pallas_call(sweep_kernel, grid_spec=pltpu.PrefetchScalarGridSpec(num_s...  20.4 us
    ppermute x2, waiting for transfers between devices, around_x(): before = lax.ppermute(mine, 'x', forward)  19.3 us
    all_to_all x1, waiting for transfers between devices, on_device(): lax.all_to_all(outgoing.reshape(TILES, 2 * SUB, width), ('x', 'y'), 0, 0,...  10.3 us
    all_to_all x1, starting transfers between devices, on_device(): lax.all_to_all(outgoing.reshape(TILES, 2 * SUB, width), ('x', 'y'), 0, 0,...  10.2 us
    all_to_all x1, waiting for transfers between devices, on_device(): lax.all_to_all(scored.reshape(TILES, 2 * SUB, TILE), ('x', 'y'), 0, 0, ti...  8.46 us
  transfers between devices with their start and end apart: 14, of which 11 were waited for; matrix products, arithmetic and copies ran while one was open for 2% of the time, Pallas kernels for 0%

profile of v8, /device:TPU:6, one launch (start us, length us, event | category | flops | bytes accessed | tf_op | source)
XLA Modules:
  0.0 232.5 jit_solution(16847684402528403388)
XLA Ops:
  6.5 1.2 constant_dynamic-slice_fusion.1
  7.8 0.8 copy.63
  8.5 0.1 eq.31
  8.6 0.2 convert_reduce_fusion.1
  8.8 0.1 reduce_sum.69
  8.9 0.1 copy.64
  9.0 0.7 multiply_add_fusion
  9.7 0.1 fusion.29
  9.7 0.3 convolution_convert_fusion
  10.0 0.9 reshape.97
  11.0 10.2 %all-to-all-start = ((bf16[32,4,1280]{2,1,0:T(4,128)(2,1)}), bf16[32,4,1280]{2,1,0:T(4,128)(2,1)S(1)}, u32[]{:S(2)}, u32[]{:S(2)}) async-start(bf16[32,4,1280]{2,1,0:T(4,128)(2,1)} %reshape.97), calls=%async_computation | async-start | bytes 655360 | tf_op jit(solution)/shard_map/all_to_all | solution.py:154
  21.9 0.3 exponential_reduce_fusion
  22.2 0.3 fusion
  22.6 10.3 %all-to-all-done = bf16[32,4,1280]{2,1,0:T(4,128)(2,1)S(1)} async-done(((bf16[32,4,1280]{2,1,0:T(4,128)(2,1)}), bf16[32,4,1280]{2,1,0:T(4,128)(2,1)S(1)}, u32[]{:S(2)}, u32[]{:S(2)}) %all-to-all-start) | async-done | bytes 327712 | tf_op jit(solution)/shard_map/all_to_all | solution.py:154
  32.9 0.2 multiply_reduce_fusion
  33.1 0.1 rsqrt.20
  33.3 0.7 fusion.16
  34.0 0.7 reshape.98
  34.7 6.6 %all-to-all-start.1 = ((bf16[32,4,512]{2,1,0:T(4,128)(2,1)}), bf16[32,4,512]{2,1,0:T(4,128)(2,1)S(1)}, u32[]{:S(2)}, u32[]{:S(2)}) async-start(bf16[32,4,512]{2,1,0:T(4,128)(2,1)} %reshape.98), calls=%async_computation.1 | async-start | bytes 262144 | tf_op jit(solution)/shard_map/all_to_all | solution.py:165
  41.3 0.0 all-gather.2.cloned.1.call-start
  41.4 8.5 %all-to-all-done.1 = bf16[32,4,512]{2,1,0:T(4,128)(2,1)S(1)} async-done(((bf16[32,4,512]{2,1,0:T(4,128)(2,1)}), bf16[32,4,512]{2,1,0:T(4,128)(2,1)S(1)}, u32[]{:S(2)}, u32[]{:S(2)}) %all-to-all-start.1) | async-done | bytes 131104 | tf_op jit(solution)/shard_map/all_to_all | solution.py:165
  49.8 0.1 reshape.99
  49.9 0.3 fusion.37
  50.2 0.1 fusion.24
  50.3 0.1 copy.68
  50.4 0.3 broadcast_in_dim.30
  50.7 26.1 %all_to_all.31 = bf16[8,17,2,1024]{3,2,1,0:T(2,128)(2,1)S(1)} all-to-all(bf16[8,17,2,1024]{3,2,1,0:T(2,128)(2,1)S(1)} %broadcast_in_dim.30), channel_id=1, replica_groups=mesh['x'=4,'y'=8,'z'=8,'c'=2] {'z'}, dimensions={0} | all-to-all | bytes 1114112 | tf_op jit(solution)/shard_map/all_to_all | solution.py:178
  76.9 0.4 slice_bitcast_fusion
  77.2 0.5 copy.70
  77.7 1.0 all_gather_reshape.3
  78.7 0.0 all-gather.2.cloned.1.call-update
  78.7 1.2 copy.69
  79.9 3.5 %all-to-all-start.3 = ((bf16[8,96,512]{2,1,0:T(8,128)(2,1)}), bf16[8,96,512]{2,1,0:T(8,128)(2,1)S(1)}, u32[]{:S(2)}, u32[]{:S(2)}) async-start(bf16[8,96,512]{2,1,0:T(8,128)(2,1)} %bitcast.9), calls=%async_computation.3 | async-start | bytes 1572864 | tf_op jit(solution)/shard_map/all_to_all | solution.py:188
  83.5 1.9 collective-permute-start
  85.5 1.1 collective-permute-done
  86.6 0.1 pad_maximum_fusion.2
  86.7 24.4 %all-to-all-done.3 = bf16[8,96,512]{2,1,0:T(8,128)(2,1)S(1)} async-done(((bf16[8,96,512]{2,1,0:T(8,128)(2,1)}), bf16[8,96,512]{2,1,0:T(8,128)(2,1)S(1)}, u32[]{:S(2)}, u32[]{:S(2)}) %all-to-all-start.3) | async-done | bytes 786464 | tf_op jit(solution)/shard_map/all_to_all | solution.py:188
  111.1 0.7 broadcast_in_dim.32
  111.8 6.8 %all-to-all-start.4 = ((f32[32,1,640]{2,1,0:T(1,128)}), f32[32,1,640]{2,1,0:T(1,128)S(1)}, u32[]{:S(2)}, u32[]{:S(2)}) async-start(f32[32,1,640]{2,1,0:T(1,128)} %broadcast_in_dim.32), calls=%async_computation.4 | async-start | bytes 163840 | tf_op jit(solution)/shard_map/all_to_all | solution.py:194
  118.6 0.1 reshape.105
  118.6 2.1 collective-permute-start.2
  120.7 3.7 %collective-permute-start.1 = (bf16[8,96,512]{2,1,0:T(8,128)(2,1)S(1)}, bf16[8,96,512]{2,1,0:T(8,128)(2,1)S(1)}, u32[]{:S(2)}, u32[]{:S(2)}) collective-permute-start(bf16[8,96,512]{2,1,0:T(8,128)(2,1)S(1)} %all-to-all-done.3), channel_id=1, source_target_pairs={{0,384},{128,0},{256,128},{384,256},{1,385},{129,1},{257,129},{385... | collective-permute-start | bytes 2359304 | tf_op jit(solution)/shard_map/ppermute | solution.py:117
  124.5 2.7 %all-to-all-done.4 = f32[32,1,640]{2,1,0:T(1,128)S(1)} async-done(((f32[32,1,640]{2,1,0:T(1,128)}), f32[32,1,640]{2,1,0:T(1,128)S(1)}, u32[]{:S(2)}, u32[]{:S(2)}) %all-to-all-start.4) | async-done | bytes 81952 | tf_op jit(solution)/shard_map/all_to_all | solution.py:194
  127.2 0.1 convert_element_type.127
  127.4 9.1 %collective-permute-done.2 = bf16[8,96,512]{2,1,0:T(8,128)(2,1)S(1)} collective-permute-done((bf16[8,96,512]{2,1,0:T(8,128)(2,1)S(1)}, bf16[8,96,512]{2,1,0:T(8,128)(2,1)S(1)}, u32[]{:S(2)}, u32[]{:S(2)}) %collective-permute-start.2) | collective-permute-done | bytes 786464 | tf_op jit(solution)/shard_map/ppermute | solution.py:116
  136.5 2.2 collective-permute-start.3
  138.8 3.6 %collective-permute-start.4 = (bf16[4,96,512]{2,1,0:T(8,128)(2,1)S(1)}, bf16[4,96,512]{2,1,0:T(8,128)(2,1)S(1)}, u32[]{:S(2)}, u32[]{:S(2)}) collective-permute-start(bf16[4,96,512]{2,1,0:T(8,128)(2,1)S(1)} %slice.76), channel_id=1, source_target_pairs={{0,384},{128,0},{256,128},{384,256},{1,385},{129,1},{257,129},{385... | collective-permute-start | bytes 1179656 | tf_op jit(solution)/shard_map/ppermute | solution.py:120
  142.5 2.3 %divide_convert_fusion = (bf16[8,96,512]{2,1,0:T(8,128)(2,1)S(1)}, bf16[8,96,512]{2,1,0:T(8,128)(2,1)S(1)}, bf16[8,96,512]{2,1,0:T(8,128)(2,1)S(1)}) fusion(bf16[8,96,512]{2,1,0:T(8,128)(2,1)} %copy-done.2, f32[8,512]{1,0:T(8,128)S(1)} %get-tuple-element.9, f32[96]{0:T(128)S(1)} %fusion.35, f32[8,512]{1,0:T(8,128)S(1)} %get-tuple-element.10, ...), kind=kLoop, calls=%fused_computation.7 | loop fusion | flops 4718592 | bytes 4768128 | tf_op jit(solution)/shard_map/convert_element_type | solution.py:207
  144.8 1.4 collective-permute-done.3
  146.2 3.5 %collective-permute-done.4 = bf16[4,96,512]{2,1,0:T(8,128)(2,1)S(1)} collective-permute-done((bf16[4,96,512]{2,1,0:T(8,128)(2,1)S(1)}, bf16[4,96,512]{2,1,0:T(8,128)(2,1)S(1)}, u32[]{:S(2)}, u32[]{:S(2)}) %collective-permute-start.4) | collective-permute-done | bytes 393248 | tf_op jit(solution)/shard_map/ppermute | solution.py:120
  149.7 0.4 divide_convert_fusion.3
  150.0 0.0 all-gather.2.cloned.1.call-done.w_ref
  150.1 11.3 %shard_map.55.own = bf16[8,96,512]{2,1,0:T(8,128)(2,1)S(1)} custom-call(s32[256]{0:T(256)S(1)} %fusion.33.index_ref, bf16[16,256,1024]{2,1,0:T(8,128)(2,1)} %all-gather.2.cloned.1.call-done.w_ref, bf16[8,96,512]{2,1,0:T(8,128)(2,1)S(1)} %get-tuple-element.19.prior_ref.own, bf16[8,96,512]{2,1,0:T(8,128)(2,1)S(1)} %get-tuple-element.19.prior_ref.own, ...), custom_call_target="tpu_custom_call" | custom-call | flops 3221225472 | bytes 11534336 | tf_op jit(solution)/shard_map/pallas_call | solution.py:87
  161.4 1.9 collective-permute-start.6
  163.4 3.9 %collective-permute-start.5 = (bf16[8,96,512]{2,1,0:T(8,128)(2,1)S(1)}, bf16[8,96,512]{2,1,0:T(8,128)(2,1)S(1)}, u32[]{:S(2)}, u32[]{:S(2)}) collective-permute-start(bf16[8,96,512]{2,1,0:T(8,128)(2,1)S(1)} %shard_map.55.own), channel_id=1, source_target_pairs={{0,384},{128,0},{256,128},{384,256},{1,385},{129,1},{257,129},{385... | collective-permute-start | bytes 2359304 | tf_op jit(solution)/shard_map/ppermute | solution.py:117
  167.3 10.2 %collective-permute-done.6.before = bf16[8,96,512]{2,1,0:T(8,128)(2,1)S(1)} collective-permute-done((bf16[8,96,512]{2,1,0:T(8,128)(2,1)S(1)}, bf16[8,96,512]{2,1,0:T(8,128)(2,1)S(1)}, u32[]{:S(2)}, u32[]{:S(2)}) %collective-permute-start.6) | collective-permute-done | bytes 786464 | tf_op jit(solution)/shard_map/ppermute | solution.py:116
  177.5 3.5 %collective-permute-start.7 = (bf16[4,96,512]{2,1,0:T(8,128)(2,1)S(1)}, bf16[4,96,512]{2,1,0:T(8,128)(2,1)S(1)}, u32[]{:S(2)}, u32[]{:S(2)}) collective-permute-start(bf16[4,96,512]{2,1,0:T(8,128)(2,1)S(1)} %slice.79), channel_id=1, source_target_pairs={{0,128},{128,256},{256,384},{384,0},{1,129},{129,257},{257,385},{3... | collective-permute-start | bytes 1179656 | tf_op jit(solution)/shard_map/ppermute | solution.py:119
  181.1 2.4 %collective-permute-start.8 = (bf16[4,96,512]{2,1,0:T(8,128)(2,1)S(1)}, bf16[4,96,512]{2,1,0:T(8,128)(2,1)S(1)}, u32[]{:S(2)}, u32[]{:S(2)}) collective-permute-start(bf16[4,96,512]{2,1,0:T(8,128)(2,1)S(1)} %slice.80), channel_id=1, source_target_pairs={{0,384},{128,0},{256,128},{384,256},{1,385},{129,1},{257,129},{385... | collective-permute-start | bytes 1179656 | tf_op jit(solution)/shard_map/ppermute | solution.py:120
  183.6 3.8 %collective-permute-done.7.oppa = bf16[4,96,512]{2,1,0:T(8,128)(2,1)S(1)} collective-permute-done((bf16[4,96,512]{2,1,0:T(8,128)(2,1)S(1)}, bf16[4,96,512]{2,1,0:T(8,128)(2,1)S(1)}, u32[]{:S(2)}, u32[]{:S(2)}) %collective-permute-start.7) | collective-permute-done | bytes 393248 | tf_op jit(solution)/shard_map/ppermute | solution.py:119
  187.3 4.7 %collective-permute-done.8.oppb = bf16[4,96,512]{2,1,0:T(8,128)(2,1)S(1)} collective-permute-done((bf16[4,96,512]{2,1,0:T(8,128)(2,1)S(1)}, bf16[4,96,512]{2,1,0:T(8,128)(2,1)S(1)}, u32[]{:S(2)}, u32[]{:S(2)}) %collective-permute-start.8) | collective-permute-done | bytes 393248 | tf_op jit(solution)/shard_map/ppermute | solution.py:120
  192.0 9.0 %shard_map.56 = bf16[8,96,512]{2,1,0:T(8,128)(2,1)S(1)} custom-call(s32[256]{0:T(256)S(1)} %fusion.33.index_ref, bf16[16,256,1024]{2,1,0:T(8,128)(2,1)S(1)} %copy-done, bf16[8,96,512]{2,1,0:T(8,128)(2,1)S(1)} %get-tuple-element.19.prior_ref.own, bf16[8,96,512]{2,1,0:T(8,128)(2,1)S(1)} %shard_map.55.own, ...), custom_call_target="tpu_custom_call" | custom-call | flops 3221225472 | bytes 11534336 | tf_op jit(solution)/shard_map/pallas_call | solution.py:87
  201.0 22.8 %all_to_all.32 = bf16[8,96,512]{2,1,0:T(8,128)(2,1)S(1)} all-to-all(bf16[8,96,512]{2,1,0:T(8,128)(2,1)S(1)} %shard_map.56), channel_id=1, replica_groups=mesh['x'=4,'y'=8,'z'=8,'c'=2] {'y'}, dimensions={0} | all-to-all | bytes 1572864 | tf_op jit(solution)/shard_map/all_to_all | solution.py:215
  223.8 0.2 convert_log_fusion
  224.1 1.6 copy.71
  (42 shorter events, 0.4 us)
Async XLA Ops:
  6.5 15.7 %copy-start.4 = (bf16[512,1280]{1,0:T(8,128)(2,1)S(1)}, bf16[512,1280]{1,0:T(8,128)(2,1)}, u32[]{:S(2)}) copy-start(bf16[512,1280]{1,0:T(8,128)(2,1)} %param.5) | copy-start | bytes 3932164
  6.5 15.3 %copy-start.5 = (f32[768]{0:T(1024)S(1)}, f32[768]{0:T(1024)}, u32[]{:S(2)}) copy-start(f32[768]{0:T(1024)} %param.6) | copy-start | bytes 9220
  6.5 15.3 %copy-start.1 = (bf16[512,768]{1,0:T(8,128)(2,1)S(1)}, bf16[512,768]{1,0:T(8,128)(2,1)}, u32[]{:S(2)}) copy-start(bf16[512,768]{1,0:T(8,128)(2,1)} %param.7) | copy-start | bytes 2359300
  11.0 21.9 %all-to-all-start = ((bf16[32,4,1280]{2,1,0:T(4,128)(2,1)}), bf16[32,4,1280]{2,1,0:T(4,128)(2,1)S(1)}, u32[]{:S(2)}, u32[]{:S(2)}) async-start(bf16[32,4,1280]{2,1,0:T(4,128)(2,1)} %reshape.97), calls=%async_computation | async-start | bytes 655360 | tf_op jit(solution)/shard_map/all_to_all | solution.py:154
  34.7 15.1 %all-to-all-start.1 = ((bf16[32,4,512]{2,1,0:T(4,128)(2,1)}), bf16[32,4,512]{2,1,0:T(4,128)(2,1)S(1)}, u32[]{:S(2)}, u32[]{:S(2)}) async-start(bf16[32,4,512]{2,1,0:T(4,128)(2,1)} %reshape.98), calls=%async_computation.1 | async-start | bytes 262144 | tf_op jit(solution)/shard_map/all_to_all | solution.py:165
  41.3 108.8 %all-gather.2.cloned.1.call-start = ((), (), s32[]{:S(2)}) async-start(), calls=%async_computation.6 | async-start | bytes 8912896 | tf_op jit(solution)/shard_map/all_gather | solution.py:183
  79.9 31.2 %all-to-all-start.3 = ((bf16[8,96,512]{2,1,0:T(8,128)(2,1)}), bf16[8,96,512]{2,1,0:T(8,128)(2,1)S(1)}, u32[]{:S(2)}, u32[]{:S(2)}) async-start(bf16[8,96,512]{2,1,0:T(8,128)(2,1)} %bitcast.9), calls=%async_computation.3 | async-start | bytes 1572864 | tf_op jit(solution)/shard_map/all_to_all | solution.py:188
  83.5 3.1 %collective-permute-start = (f32[512]{0:T(512)S(1)}, f32[512]{0:T(512)S(1)}, u32[]{:S(2)}, u32[]{:S(2)}) collective-permute-start(f32[512]{0:T(512)S(1)} %bitcast.60), channel_id=1, source_target_pairs={{0,1},{1,0},{2,3},{3,2},{4,5},{5,4},{6,7},{7,6},{8,9},{9,8},{10,11... | collective-permute-start | bytes 6152 | tf_op jit(solution)/shard_map/ppermute | solution.py:191
  111.8 15.4 %all-to-all-start.4 = ((f32[32,1,640]{2,1,0:T(1,128)}), f32[32,1,640]{2,1,0:T(1,128)S(1)}, u32[]{:S(2)}, u32[]{:S(2)}) async-start(f32[32,1,640]{2,1,0:T(1,128)} %broadcast_in_dim.32), calls=%async_computation.4 | async-start | bytes 163840 | tf_op jit(solution)/shard_map/all_to_all | solution.py:194
  118.6 17.9 %collective-permute-start.2 = (bf16[8,96,512]{2,1,0:T(8,128)(2,1)S(1)}, bf16[8,96,512]{2,1,0:T(8,128)(2,1)S(1)}, u32[]{:S(2)}, u32[]{:S(2)}) collective-permute-start(bf16[8,96,512]{2,1,0:T(8,128)(2,1)S(1)} %all-to-all-done.3), channel_id=1, source_target_pairs={{0,128},{128,256},{256,384},{384,0},{1,129},{129,257},{257,385},{3... | collective-permute-start | bytes 2359304 | tf_op jit(solution)/shard_map/ppermute | solution.py:116
  120.7 18.0 %collective-permute-start.1 = (bf16[8,96,512]{2,1,0:T(8,128)(2,1)S(1)}, bf16[8,96,512]{2,1,0:T(8,128)(2,1)S(1)}, u32[]{:S(2)}, u32[]{:S(2)}) collective-permute-start(bf16[8,96,512]{2,1,0:T(8,128)(2,1)S(1)} %all-to-all-done.3), channel_id=1, source_target_pairs={{0,384},{128,0},{256,128},{384,256},{1,385},{129,1},{257,129},{385... | collective-permute-start | bytes 2359304 | tf_op jit(solution)/shard_map/ppermute | solution.py:117
  136.5 5.9 %copy-start.2 = (bf16[8,96,512]{2,1,0:T(8,128)(2,1)}, bf16[8,96,512]{2,1,0:T(8,128)(2,1)S(1)}, u32[]{:S(2)}) copy-start(bf16[8,96,512]{2,1,0:T(8,128)(2,1)S(1)} %collective-permute-done.2) | copy-start | bytes 2359300
  136.5 9.7 %collective-permute-start.3 = (bf16[4,96,512]{2,1,0:T(8,128)(2,1)S(1)}, bf16[4,96,512]{2,1,0:T(8,128)(2,1)S(1)}, u32[]{:S(2)}, u32[]{:S(2)}) collective-permute-start(bf16[4,96,512]{2,1,0:T(8,128)(2,1)S(1)} %slice.74), channel_id=1, source_target_pairs={{0,128},{128,256},{256,384},{384,0},{1,129},{129,257},{257,385},{3... | collective-permute-start | bytes 1179656 | tf_op jit(solution)/shard_map/ppermute | solution.py:119
  138.8 3.7 %copy-start.3 = (bf16[8,96,512]{2,1,0:T(8,128)(2,1)}, bf16[8,96,512]{2,1,0:T(8,128)(2,1)S(1)}, u32[]{:S(2)}) copy-start(bf16[8,96,512]{2,1,0:T(8,128)(2,1)S(1)} %collective-permute-done.1) | copy-start | bytes 2359300
  138.8 10.9 %collective-permute-start.4 = (bf16[4,96,512]{2,1,0:T(8,128)(2,1)S(1)}, bf16[4,96,512]{2,1,0:T(8,128)(2,1)S(1)}, u32[]{:S(2)}, u32[]{:S(2)}) collective-permute-start(bf16[4,96,512]{2,1,0:T(8,128)(2,1)S(1)} %slice.76), channel_id=1, source_target_pairs={{0,384},{128,0},{256,128},{384,256},{1,385},{129,1},{257,129},{385... | collective-permute-start | bytes 1179656 | tf_op jit(solution)/shard_map/ppermute | solution.py:120
  150.1 41.9 %copy-start = (bf16[16,256,1024]{2,1,0:T(8,128)(2,1)S(1)}, bf16[16,256,1024]{2,1,0:T(8,128)(2,1)}, u32[]{:S(2)}) copy-start(bf16[16,256,1024]{2,1,0:T(8,128)(2,1)} %all-gather.2.cloned.1.call-done.w_ref) | copy-start | bytes 25165828
  161.4 16.1 %collective-permute-start.6 = (bf16[8,96,512]{2,1,0:T(8,128)(2,1)S(1)}, bf16[8,96,512]{2,1,0:T(8,128)(2,1)S(1)}, u32[]{:S(2)}, u32[]{:S(2)}) collective-permute-start(bf16[8,96,512]{2,1,0:T(8,128)(2,1)S(1)} %shard_map.55.own), channel_id=1, source_target_pairs={{0,128},{128,256},{256,384},{384,0},{1,129},{129,257},{257,385},{3... | collective-permute-start | bytes 2359304 | tf_op jit(solution)/shard_map/ppermute | solution.py:116
  163.4 17.7 %collective-permute-start.5 = (bf16[8,96,512]{2,1,0:T(8,128)(2,1)S(1)}, bf16[8,96,512]{2,1,0:T(8,128)(2,1)S(1)}, u32[]{:S(2)}, u32[]{:S(2)}) collective-permute-start(bf16[8,96,512]{2,1,0:T(8,128)(2,1)S(1)} %shard_map.55.own), channel_id=1, source_target_pairs={{0,384},{128,0},{256,128},{384,256},{1,385},{129,1},{257,129},{385... | collective-permute-start | bytes 2359304 | tf_op jit(solution)/shard_map/ppermute | solution.py:117
  177.5 9.8 %collective-permute-start.7 = (bf16[4,96,512]{2,1,0:T(8,128)(2,1)S(1)}, bf16[4,96,512]{2,1,0:T(8,128)(2,1)S(1)}, u32[]{:S(2)}, u32[]{:S(2)}) collective-permute-start(bf16[4,96,512]{2,1,0:T(8,128)(2,1)S(1)} %slice.79), channel_id=1, source_target_pairs={{0,128},{128,256},{256,384},{384,0},{1,129},{129,257},{257,385},{3... | collective-permute-start | bytes 1179656 | tf_op jit(solution)/shard_map/ppermute | solution.py:119
  181.1 10.9 %collective-permute-start.8 = (bf16[4,96,512]{2,1,0:T(8,128)(2,1)S(1)}, bf16[4,96,512]{2,1,0:T(8,128)(2,1)S(1)}, u32[]{:S(2)}, u32[]{:S(2)}) collective-permute-start(bf16[4,96,512]{2,1,0:T(8,128)(2,1)S(1)} %slice.80), channel_id=1, source_target_pairs={{0,384},{128,0},{256,128},{384,256},{1,385},{129,1},{257,129},{385... | collective-permute-start | bytes 1179656 | tf_op jit(solution)/shard_map/ppermute | solution.py:120
Sparse Core Ops, SparseCore 0:
  78.9 63.8 all-gather.1

commit v9 on v8

--- a/solution.py
+++ b/solution.py
@@ -172,6 +172,7 @@
     scaled = scaled.transpose(0, 2, 1, 3).reshape(NBLK, SUB, NT * TILE)
 
     part = jnp.sum(jnp.exp(logits.astype(F32) + class_bias[None, :]), axis=1)
+    part = part + lax.ppermute(part, "c", [(0, 1), (1, 0)])
     high, middle, low = split_terms(part)
     terms = jnp.concatenate([high, middle, low, jnp.zeros_like(low)])
     piece = jnp.concatenate([scaled, terms.reshape(1, SUB, NT * TILE)])
@@ -180,34 +181,20 @@
     )
 
     piece = over_z[:, :NBLK].transpose(1, 0, 2, 3).reshape(NBLK * ROWS_C, NT * TILE)
+    names = jnp.zeros((16, NT * TILE), BF).at[0, :PER].set(owners.astype(BF))
+    piece = jnp.concatenate([piece, names])
     weights = lax.all_gather(piece, ("y", "c"), axis=0, tiled=False)
 
     terms = jnp.sum(over_z[:, NBLK].astype(F32), axis=0).reshape(4, rows)
     totals = terms[0] + terms[1] + terms[2]
-    raw, _ = lax.optimization_barrier((logits, over_z))
-    raw = lax.all_to_all(
-        raw.T.reshape(NY, classes // NY, rows), "y", 0, 0, tiled=True
-    )
-    totals = totals + lax.ppermute(totals, "c", [(0, 1), (1, 0)])
-    known = jnp.concatenate([totals, owners.astype(F32), jnp.zeros((128 - PER,), F32)])
-    known, _ = lax.optimization_barrier((known, raw))
-    known = lax.all_to_all(
-        jnp.broadcast_to(known, (TILES,) + known.shape), ("x", "y"), 0, 0, tiled=True
-    )
-    raw = around_x(raw)
-    known = known.reshape(NX, NY, -1)
-    known = lax.dynamic_slice_in_dim(jnp.concatenate([known, known]), x, NX, axis=0)
-    totals = known[:, :, :rows]
-
-    bias = lax.dynamic_slice_in_dim(class_bias.reshape(NY, classes // NY), y, 1, axis=0)
-    bias = bias.reshape(1, classes // NY, 1)
-    half = NY // 2
-    sums = totals[0], totals[1], totals[2, :half], totals[2, half:], totals[3]
-    priors = tuple(
-        (jnp.exp(r.astype(F32) + bias) / t[:, None, :]).astype(BF) for r, t in zip(raw, sums)
-    )
-
-    named = known[0, :, rows : rows + PER].astype(jnp.int32).reshape(NY * PER)
+    adjusted = logits.astype(F32) + class_bias[None, :]
+    prior = (jnp.exp(adjusted) / totals[:, None]).astype(BF)
+    prior = lax.all_to_all(
+        prior.T.reshape(NY, classes // NY, rows), "y", 0, 0, tiled=True
+    )
+    priors = around_x(prior)
+
+    named = weights[::NC, NBLK * ROWS_C, :PER].astype(jnp.int32).reshape(NY * PER)
     index = (named // NY - x) % NX * NY + named % NY
 
     labels = sweep(index, weights, priors[0], priors, 48)

time: 233 us -> 241 us (1.034)
  blocking collectives: 48.9 us -> 56.5 us
  starting transfers between devices: 52.6 us -> 55.5 us
    all_to_all x2 -> x1, waiting for transfers between devices: 27.1 us -> 15.7 us  [on_device(): lax.all_to_all(jnp.broadcast_to(piece, (NZ,) + piece.shape), 'z', 0, 0, t...]
    all_gather x1, waiting for transfers between devices: 0.02 us -> 6.5 us  [on_device(): weights = lax.all_gather(piece, ('y', 'c'), axis=0, tiled=False)]
    ppermute x2, waiting for transfers between devices: 19.3 us -> 25.8 us  [around_x(): before = lax.ppermute(mine, 'x', forward)]
    ppermute x2, starting transfers between devices: 5.74 us -> 10.5 us  [around_x(): oppa = lax.ppermute(before[:half], 'x', forward)]
    all_to_all x1, blocking collectives: 26.1 us -> 30.6 us  [on_device(): lax.all_to_all(prior.T.reshape(NY, classes // NY, rows), 'y', 0, 0, tiled...]
    all_to_all x1, blocking collectives: 22.8 us -> 25.9 us  [on_device(): spread = lax.all_to_all(spread, 'y', 0, 0, tiled=True)]
    ppermute x2, starting transfers between devices: 4.01 us -> 6.49 us  [around_x(): before = lax.ppermute(mine, 'x', forward)]
    all_to_all x2 -> x1, starting transfers between devices: 10.3 us -> 10.3 us  [on_device(): lax.all_to_all(jnp.broadcast_to(piece, (NZ,) + piece.shape), 'z', 0, 0, t...]
  transfers between devices with their start and end apart: 14 -> 13, of which waited for: 11 -> 9; matrix products, arithmetic and copies ran while one was open for 2% -> 2% of each run, Pallas kernels for 0% -> 0%
where the time goes in v9:
time: 241 us; the launch traced here: 240 us
  waiting for transfers between devices  78 us (32%)
  blocking collectives  56.5 us (23%)
  starting transfers between devices  55.5 us (23%)
  Pallas kernels  20.7 us (9%)
  between operations  14.4 us (6%)
  local copies, waits for them, and re-layouts  9.42 us (4%)
  other arithmetic  4.28 us (2%)
    all_to_all x1, blocking collectives, on_device(): lax.all_to_all(prior.T.reshape(NY, classes // NY, rows), 'y', 0, 0, tiled...  30.6 us
    all_to_all x1, blocking collectives, on_device(): spread = lax.all_to_all(spread, 'y', 0, 0, tiled=True)  25.9 us
    ppermute x2, waiting for transfers between devices, around_x(): before = lax.ppermute(mine, 'x', forward)  25.8 us
    pallas_call x2, Pallas kernels, sweep(): pl.pallas_call(sweep_kernel, grid_spec=pltpu.PrefetchScalarGridSpec(num_s...  20.7 us
    all_to_all x1, waiting for transfers between devices, on_device(): lax.all_to_all(jnp.broadcast_to(piece, (NZ,) + piece.shape), 'z', 0, 0, t...  15.7 us
    ppermute x2, starting transfers between devices, around_x(): oppa = lax.ppermute(before[:half], 'x', forward)  10.5 us
    all_to_all x1, starting transfers between devices, on_device(): lax.all_to_all(jnp.broadcast_to(piece, (NZ,) + piece.shape), 'z', 0, 0, t...  10.3 us
    all_to_all x1, starting transfers between devices, on_device(): lax.all_to_all(outgoing.reshape(TILES, 2 * SUB, width), ('x', 'y'), 0, 0,...  10.2 us
  transfers between devices with their start and end apart: 13, of which 9 were waited for; matrix products, arithmetic and copies ran while one was open for 2% of the time, Pallas kernels for 0%

profile of v9, /device:TPU:6, one launch (start us, length us, event | category | flops | bytes accessed | tf_op | source)
XLA Modules:
  0.0 240.0 jit_solution(13627381772344695369)
XLA Ops:
  6.5 0.9 copy.69
  7.4 0.1 eq.31
  7.5 0.2 convert_reduce_fusion.1
  7.7 0.1 reduce_sum.69
  7.8 0.1 copy.70
  7.9 0.8 multiply_add_fusion
  8.7 0.1 fusion.32
  8.7 1.1 constant_dynamic-slice_fusion
  9.8 0.3 convolution_convert_fusion
  10.1 0.9 reshape.133
  11.0 10.2 %all-to-all-start = ((bf16[32,4,1280]{2,1,0:T(4,128)(2,1)}), bf16[32,4,1280]{2,1,0:T(4,128)(2,1)S(1)}, u32[]{:S(2)}, u32[]{:S(2)}) async-start(bf16[32,4,1280]{2,1,0:T(4,128)(2,1)} %reshape.133), calls=%async_computation | async-start | bytes 655360 | tf_op jit(solution)/shard_map/all_to_all | solution.py:154
  21.3 0.3 fusion.3
  21.6 1.9 collective-permute-start
  24.2 0.3 fusion
  24.6 8.4 %all-to-all-done = bf16[32,4,1280]{2,1,0:T(4,128)(2,1)S(1)} async-done(((bf16[32,4,1280]{2,1,0:T(4,128)(2,1)}), bf16[32,4,1280]{2,1,0:T(4,128)(2,1)S(1)}, u32[]{:S(2)}, u32[]{:S(2)}) %all-to-all-start) | async-done | bytes 327712 | tf_op jit(solution)/shard_map/all_to_all | solution.py:154
  32.9 0.2 multiply_reduce_fusion
  33.2 0.1 rsqrt.20
  33.4 0.7 fusion.17
  34.1 0.7 reshape.134
  34.7 6.6 %all-to-all-start.1 = ((bf16[32,4,512]{2,1,0:T(4,128)(2,1)}), bf16[32,4,512]{2,1,0:T(4,128)(2,1)S(1)}, u32[]{:S(2)}, u32[]{:S(2)}) async-start(bf16[32,4,512]{2,1,0:T(4,128)(2,1)} %reshape.134), calls=%async_computation.1 | async-start | bytes 262144 | tf_op jit(solution)/shard_map/all_to_all | solution.py:165
  41.3 0.0 collective-permute-done
  41.4 8.4 %all-to-all-done.1 = bf16[32,4,512]{2,1,0:T(4,128)(2,1)S(1)} async-done(((bf16[32,4,512]{2,1,0:T(4,128)(2,1)}), bf16[32,4,512]{2,1,0:T(4,128)(2,1)S(1)}, u32[]{:S(2)}, u32[]{:S(2)}) %all-to-all-start.1) | async-done | bytes 131104 | tf_op jit(solution)/shard_map/all_to_all | solution.py:165
  49.8 0.1 reshape.135
  49.9 0.3 fusion.39
  50.2 0.1 fusion.27
  50.3 0.1 copy.74
  50.4 1.1 broadcast_in_dim.15
  51.5 10.3 %all-to-all-start.2 = ((bf16[8,17,2,1024]{3,2,1,0:T(2,128)(2,1)}), bf16[8,17,2,1024]{3,2,1,0:T(2,128)(2,1)S(1)}, u32[]{:S(2)}, u32[]{:S(2)}) async-start(bf16[8,17,2,1024]{3,2,1,0:T(2,128)(2,1)} %broadcast_in_dim.15), calls=%async_computation.2 | async-start | bytes 1114112 | tf_op jit(solution)/shard_map/all_to_all | solution.py:179
  61.8 0.0 all-gather.3.cloned.1.call-start
  61.9 0.1 copy.76
  62.0 0.1 convert_element_type.107
  62.1 15.7 %all-to-all-done.2 = bf16[8,17,2,1024]{3,2,1,0:T(2,128)(2,1)S(1)} async-done(((bf16[8,17,2,1024]{3,2,1,0:T(2,128)(2,1)}), bf16[8,17,2,1024]{3,2,1,0:T(2,128)(2,1)S(1)}, u32[]{:S(2)}, u32[]{:S(2)}) %all-to-all-start.2) | async-done | bytes 557088 | tf_op jit(solution)/shard_map/all_to_all | solution.py:179
  77.8 0.4 slice_bitcast_fusion
  78.1 0.5 copy.75
  78.6 0.2 reshape.138
  78.8 0.8 fusion.22
  79.7 0.0 all-gather.3.cloned.1.call-update
  79.8 0.3 fusion.21
  80.1 0.3 copy.77
  80.4 30.6 %all_to_all.25.prior_ref.own = bf16[8,96,512]{2,1,0:T(8,128)(2,1)S(1)} all-to-all(bf16[8,96,512]{2,1,0:T(8,128)(2,1)S(1)} %bitcast.43), channel_id=1, replica_groups=mesh['x'=4,'y'=8,'z'=8,'c'=2] {'y'}, dimensions={0} | all-to-all | bytes 1572864 | tf_op jit(solution)/shard_map/all_to_all | solution.py:192
  111.0 4.3 %collective-permute-start.2 = (bf16[8,96,512]{2,1,0:T(8,128)(2,1)S(1)}, bf16[8,96,512]{2,1,0:T(8,128)(2,1)S(1)}, u32[]{:S(2)}, u32[]{:S(2)}) collective-permute-start(bf16[8,96,512]{2,1,0:T(8,128)(2,1)S(1)} %all_to_all.25.prior_ref.own), channel_id=1, source_target_pairs={{0,128},{128,256},{256,384},{384,0},{1,129},{129,257},{257,385},{3... | collective-permute-start | bytes 2359304 | tf_op jit(solution)/shard_map/ppermute | solution.py:116
  115.3 1.9 collective-permute-start.1
  117.2 11.8 %collective-permute-done.2.before = bf16[8,96,512]{2,1,0:T(8,128)(2,1)S(1)} collective-permute-done((bf16[8,96,512]{2,1,0:T(8,128)(2,1)S(1)}, bf16[8,96,512]{2,1,0:T(8,128)(2,1)S(1)}, u32[]{:S(2)}, u32[]{:S(2)}) %collective-permute-start.2) | collective-permute-done | bytes 786464 | tf_op jit(solution)/shard_map/ppermute | solution.py:116
  129.1 5.3 %collective-permute-start.3 = (bf16[4,96,512]{2,1,0:T(8,128)(2,1)S(1)}, bf16[4,96,512]{2,1,0:T(8,128)(2,1)S(1)}, u32[]{:S(2)}, u32[]{:S(2)}) collective-permute-start(bf16[4,96,512]{2,1,0:T(8,128)(2,1)S(1)} %slice.61), channel_id=1, source_target_pairs={{0,128},{128,256},{256,384},{384,0},{1,129},{129,257},{257,385},{3... | collective-permute-start | bytes 1179656 | tf_op jit(solution)/shard_map/ppermute | solution.py:119
  134.5 0.0 collective-permute-done.1.after
  134.5 0.8 slice.62
  135.3 1.9 collective-permute-start.4
  137.2 6.5 %all-gather.3.cloned.1.call-done = bf16[4352,1024]{1,0:T(8,128)(2,1)} async-done(((bf16[272,1024]{1,0:T(8,128)(2,1)}), bf16[4352,1024]{1,0:T(8,128)(2,1)}) %all-gather.3.cloned.1.call-update) | async-done | bytes 8912912 | tf_op jit(solution)/shard_map/all_gather | solution.py:186
  143.7 0.7 convert_reduce_fusion.2
  144.4 0.1 reshape.142
  144.6 0.0 collective-permute-done.3.oppa
  144.6 1.8 collective-permute-done.4.oppb
  146.4 11.4 %shard_map.55.own = bf16[8,96,512]{2,1,0:T(8,128)(2,1)S(1)} custom-call(s32[256]{0:T(256)S(1)} %fusion.36.index_ref, bf16[16,272,1024]{2,1,0:T(8,128)(2,1)} %bitcast.40, bf16[8,96,512]{2,1,0:T(8,128)(2,1)S(1)} %all_to_all.25.prior_ref.own, bf16[8,96,512]{2,1,0:T(8,128)(2,1)S(1)} %all_to_all.25.prior_ref.own, ...), custom_call_target="tpu_custom_call" | custom-call | flops 3221225472 | bytes 12058624 | tf_op jit(solution)/shard_map/pallas_call | solution.py:87
  157.8 2.2 collective-permute-start.6
  160.0 3.7 %collective-permute-start.5 = (bf16[8,96,512]{2,1,0:T(8,128)(2,1)S(1)}, bf16[8,96,512]{2,1,0:T(8,128)(2,1)S(1)}, u32[]{:S(2)}, u32[]{:S(2)}) collective-permute-start(bf16[8,96,512]{2,1,0:T(8,128)(2,1)S(1)} %shard_map.55.own), channel_id=1, source_target_pairs={{0,384},{128,0},{256,128},{384,256},{1,385},{129,1},{257,129},{385... | collective-permute-start | bytes 2359304 | tf_op jit(solution)/shard_map/ppermute | solution.py:117
  163.7 14.0 %collective-permute-done.6.before = bf16[8,96,512]{2,1,0:T(8,128)(2,1)S(1)} collective-permute-done((bf16[8,96,512]{2,1,0:T(8,128)(2,1)S(1)}, bf16[8,96,512]{2,1,0:T(8,128)(2,1)S(1)}, u32[]{:S(2)}, u32[]{:S(2)}) %collective-permute-start.6) | collective-permute-done | bytes 786464 | tf_op jit(solution)/shard_map/ppermute | solution.py:116
  177.7 5.2 %collective-permute-start.7 = (bf16[4,96,512]{2,1,0:T(8,128)(2,1)S(1)}, bf16[4,96,512]{2,1,0:T(8,128)(2,1)S(1)}, u32[]{:S(2)}, u32[]{:S(2)}) collective-permute-start(bf16[4,96,512]{2,1,0:T(8,128)(2,1)S(1)} %slice.63), channel_id=1, source_target_pairs={{0,128},{128,256},{256,384},{384,0},{1,129},{129,257},{257,385},{3... | collective-permute-start | bytes 1179656 | tf_op jit(solution)/shard_map/ppermute | solution.py:119
  182.9 1.9 collective-permute-start.8
  184.8 6.0 %collective-permute-done.7.oppa = bf16[4,96,512]{2,1,0:T(8,128)(2,1)S(1)} collective-permute-done((bf16[4,96,512]{2,1,0:T(8,128)(2,1)S(1)}, bf16[4,96,512]{2,1,0:T(8,128)(2,1)S(1)}, u32[]{:S(2)}, u32[]{:S(2)}) %collective-permute-start.7) | collective-permute-done | bytes 393248 | tf_op jit(solution)/shard_map/ppermute | solution.py:119
  190.8 5.4 %collective-permute-done.8.oppb = bf16[4,96,512]{2,1,0:T(8,128)(2,1)S(1)} collective-permute-done((bf16[4,96,512]{2,1,0:T(8,128)(2,1)S(1)}, bf16[4,96,512]{2,1,0:T(8,128)(2,1)S(1)}, u32[]{:S(2)}, u32[]{:S(2)}) %collective-permute-start.8) | collective-permute-done | bytes 393248 | tf_op jit(solution)/shard_map/ppermute | solution.py:120
  196.2 9.2 %shard_map.56 = bf16[8,96,512]{2,1,0:T(8,128)(2,1)S(1)} custom-call(s32[256]{0:T(256)S(1)} %fusion.36.index_ref, bf16[16,272,1024]{2,1,0:T(8,128)(2,1)S(1)} %bitcast.41, bf16[8,96,512]{2,1,0:T(8,128)(2,1)S(1)} %all_to_all.25.prior_ref.own, bf16[8,96,512]{2,1,0:T(8,128)(2,1)S(1)} %shard_map.55.own, bf16[8,96,512]{2,1,0:T(8,128)(2,1)S(1)} %collective-permute-done.5.after, ...), custom_call_target="tpu_custom_call" | custom-call | flops 3221225472 | bytes 12058624 | tf_op jit(solution)/shard_map/pallas_call | solution.py:87
  205.4 25.9 %all_to_all.26 = bf16[8,96,512]{2,1,0:T(8,128)(2,1)S(1)} all-to-all(bf16[8,96,512]{2,1,0:T(8,128)(2,1)S(1)} %shard_map.56), channel_id=1, replica_groups=mesh['x'=4,'y'=8,'z'=8,'c'=2] {'y'}, dimensions={0} | all-to-all | bytes 1572864 | tf_op jit(solution)/shard_map/all_to_all | solution.py:202
  231.3 0.2 convert_log_fusion
  231.5 1.6 copy.78
  (27 shorter events, 0.3 us)
Async XLA Ops:
  6.5 17.7 %copy-start.2 = (bf16[512,1280]{1,0:T(8,128)(2,1)S(1)}, bf16[512,1280]{1,0:T(8,128)(2,1)}, u32[]{:S(2)}) copy-start(bf16[512,1280]{1,0:T(8,128)(2,1)} %param.7) | copy-start | bytes 3932164
  6.5 14.7 %copy-start.1 = (bf16[512,768]{1,0:T(8,128)(2,1)S(1)}, bf16[512,768]{1,0:T(8,128)(2,1)}, u32[]{:S(2)}) copy-start(bf16[512,768]{1,0:T(8,128)(2,1)} %param.9) | copy-start | bytes 2359300
  6.5 14.7 %copy-start.3 = (f32[768]{0:T(1024)S(1)}, f32[768]{0:T(1024)}, u32[]{:S(2)}) copy-start(f32[768]{0:T(1024)} %param.8) | copy-start | bytes 9220
  11.0 21.9 %all-to-all-start = ((bf16[32,4,1280]{2,1,0:T(4,128)(2,1)}), bf16[32,4,1280]{2,1,0:T(4,128)(2,1)S(1)}, u32[]{:S(2)}, u32[]{:S(2)}) async-start(bf16[32,4,1280]{2,1,0:T(4,128)(2,1)} %reshape.133), calls=%async_computation | async-start | bytes 655360 | tf_op jit(solution)/shard_map/all_to_all | solution.py:154
  21.6 19.7 %collective-permute-start = (f32[512]{0:T(512)S(1)}, f32[512]{0:T(512)S(1)}, u32[]{:S(2)}, u32[]{:S(2)}) collective-permute-start(f32[512]{0:T(512)S(1)} %fusion.3), channel_id=1, source_target_pairs={{0,1},{1,0},{2,3},{3,2},{4,5},{5,4},{6,7},{7,6},{8,9},{9,8},{10,11... | collective-permute-start | bytes 6152 | tf_op jit(solution)/shard_map/ppermute | solution.py:175
  34.7 15.1 %all-to-all-start.1 = ((bf16[32,4,512]{2,1,0:T(4,128)(2,1)}), bf16[32,4,512]{2,1,0:T(4,128)(2,1)S(1)}, u32[]{:S(2)}, u32[]{:S(2)}) async-start(bf16[32,4,512]{2,1,0:T(4,128)(2,1)} %reshape.134), calls=%async_computation.1 | async-start | bytes 262144 | tf_op jit(solution)/shard_map/all_to_all | solution.py:165
  51.5 26.3 %all-to-all-start.2 = ((bf16[8,17,2,1024]{3,2,1,0:T(2,128)(2,1)}), bf16[8,17,2,1024]{3,2,1,0:T(2,128)(2,1)S(1)}, u32[]{:S(2)}, u32[]{:S(2)}) async-start(bf16[8,17,2,1024]{3,2,1,0:T(2,128)(2,1)} %broadcast_in_dim.15), calls=%async_computation.2 | async-start | bytes 1114112 | tf_op jit(solution)/shard_map/all_to_all | solution.py:179
  61.8 81.9 %all-gather.3.cloned.1.call-start = ((), (), s32[]{:S(2)}) async-start(), calls=%async_computation.5 | async-start | bytes 9469952 | tf_op jit(solution)/shard_map/all_gather | solution.py:186
  111.0 18.1 %collective-permute-start.2 = (bf16[8,96,512]{2,1,0:T(8,128)(2,1)S(1)}, bf16[8,96,512]{2,1,0:T(8,128)(2,1)S(1)}, u32[]{:S(2)}, u32[]{:S(2)}) collective-permute-start(bf16[8,96,512]{2,1,0:T(8,128)(2,1)S(1)} %all_to_all.25.prior_ref.own), channel_id=1, source_target_pairs={{0,128},{128,256},{256,384},{384,0},{1,129},{129,257},{257,385},{3... | collective-permute-start | bytes 2359304 | tf_op jit(solution)/shard_map/ppermute | solution.py:116
  115.3 19.2 %collective-permute-start.1 = (bf16[8,96,512]{2,1,0:T(8,128)(2,1)S(1)}, bf16[8,96,512]{2,1,0:T(8,128)(2,1)S(1)}, u32[]{:S(2)}, u32[]{:S(2)}) collective-permute-start(bf16[8,96,512]{2,1,0:T(8,128)(2,1)S(1)} %all_to_all.25.prior_ref.own), channel_id=1, source_target_pairs={{0,384},{128,0},{256,128},{384,256},{1,385},{129,1},{257,129},{385... | collective-permute-start | bytes 2359304 | tf_op jit(solution)/shard_map/ppermute | solution.py:117
  129.1 15.4 %collective-permute-start.3 = (bf16[4,96,512]{2,1,0:T(8,128)(2,1)S(1)}, bf16[4,96,512]{2,1,0:T(8,128)(2,1)S(1)}, u32[]{:S(2)}, u32[]{:S(2)}) collective-permute-start(bf16[4,96,512]{2,1,0:T(8,128)(2,1)S(1)} %slice.61), channel_id=1, source_target_pairs={{0,128},{128,256},{256,384},{384,0},{1,129},{129,257},{257,385},{3... | collective-permute-start | bytes 1179656 | tf_op jit(solution)/shard_map/ppermute | solution.py:119
  135.3 11.1 %collective-permute-start.4 = (bf16[4,96,512]{2,1,0:T(8,128)(2,1)}, bf16[4,96,512]{2,1,0:T(8,128)(2,1)S(1)}, u32[]{:S(2)}, u32[]{:S(2)}) collective-permute-start(bf16[4,96,512]{2,1,0:T(8,128)(2,1)} %slice.62), channel_id=1, source_target_pairs={{0,384},{128,0},{256,128},{384,256},{1,385},{129,1},{257,129},{385... | collective-permute-start | bytes 1179656 | tf_op jit(solution)/shard_map/ppermute | solution.py:120
  146.4 49.8 %copy-start = (bf16[4352,1024]{1,0:T(8,128)(2,1)S(1)}, bf16[4352,1024]{1,0:T(8,128)(2,1)}, u32[]{:S(2)}) copy-start(bf16[4352,1024]{1,0:T(8,128)(2,1)} %all-gather.3.cloned.1.call-done) | copy-start | bytes 26738692
  157.8 19.8 %collective-permute-start.6 = (bf16[8,96,512]{2,1,0:T(8,128)(2,1)S(1)}, bf16[8,96,512]{2,1,0:T(8,128)(2,1)S(1)}, u32[]{:S(2)}, u32[]{:S(2)}) collective-permute-start(bf16[8,96,512]{2,1,0:T(8,128)(2,1)S(1)} %shard_map.55.own), channel_id=1, source_target_pairs={{0,128},{128,256},{256,384},{384,0},{1,129},{129,257},{257,385},{3... | collective-permute-start | bytes 2359304 | tf_op jit(solution)/shard_map/ppermute | solution.py:116
  160.0 22.8 %collective-permute-start.5 = (bf16[8,96,512]{2,1,0:T(8,128)(2,1)S(1)}, bf16[8,96,512]{2,1,0:T(8,128)(2,1)S(1)}, u32[]{:S(2)}, u32[]{:S(2)}) collective-permute-start(bf16[8,96,512]{2,1,0:T(8,128)(2,1)S(1)} %shard_map.55.own), channel_id=1, source_target_pairs={{0,384},{128,0},{256,128},{384,256},{1,385},{129,1},{257,129},{385... | collective-permute-start | bytes 2359304 | tf_op jit(solution)/shard_map/ppermute | solution.py:117
  177.7 13.2 %collective-permute-start.7 = (bf16[4,96,512]{2,1,0:T(8,128)(2,1)S(1)}, bf16[4,96,512]{2,1,0:T(8,128)(2,1)S(1)}, u32[]{:S(2)}, u32[]{:S(2)}) collective-permute-start(bf16[4,96,512]{2,1,0:T(8,128)(2,1)S(1)} %slice.63), channel_id=1, source_target_pairs={{0,128},{128,256},{256,384},{384,0},{1,129},{129,257},{257,385},{3... | collective-permute-start | bytes 1179656 | tf_op jit(solution)/shard_map/ppermute | solution.py:119
  182.9 13.3 %collective-permute-start.8 = (bf16[4,96,512]{2,1,0:T(8,128)(2,1)S(1)}, bf16[4,96,512]{2,1,0:T(8,128)(2,1)S(1)}, u32[]{:S(2)}, u32[]{:S(2)}) collective-permute-start(bf16[4,96,512]{2,1,0:T(8,128)(2,1)S(1)} %slice.64), channel_id=1, source_target_pairs={{0,384},{128,0},{256,128},{384,256},{1,385},{129,1},{257,129},{385... | collective-permute-start | bytes 1179656 | tf_op jit(solution)/shard_map/ppermute | solution.py:120
Sparse Core Ops, SparseCore 0:
  79.8 63.8 all-gather.2

commit v10 on v8

--- a/solution.py
+++ b/solution.py
@@ -190,11 +190,11 @@
     )
     totals = totals + lax.ppermute(totals, "c", [(0, 1), (1, 0)])
     known = jnp.concatenate([totals, owners.astype(F32), jnp.zeros((128 - PER,), F32)])
-    known, _ = lax.optimization_barrier((known, raw))
+    raw = around_x(raw)
+    known, _ = lax.optimization_barrier((known, (raw[1], raw[4])))
     known = lax.all_to_all(
         jnp.broadcast_to(known, (TILES,) + known.shape), ("x", "y"), 0, 0, tiled=True
     )
-    raw = around_x(raw)
     known = known.reshape(NX, NY, -1)
     known = lax.dynamic_slice_in_dim(jnp.concatenate([known, known]), x, NX, axis=0)
     totals = known[:, :, :rows]

time: 233 us -> 235 us (level)
  blocking collectives: 48.9 us -> 80.4 us
  waiting for transfers between devices: 79.7 us -> 49.1 us
    all_to_all x0 -> x1, blocking collectives: none -> 30.5 us  [on_device(): lax.all_to_all(raw.T.reshape(NY, classes // NY, rows), 'y', 0, 0, tiled=T...]
    all_to_all x1 -> x0, waiting for transfers between devices: 24.4 us -> none  [on_device(): lax.all_to_all(raw.T.reshape(NY, classes // NY, rows), 'y', 0, 0, tiled=T...]
    ppermute x2, waiting for transfers between devices: 19.3 us -> 13.3 us  [around_x(): before = lax.ppermute(mine, 'x', forward)]
    ppermute x2, waiting for transfers between devices: 0.01 us -> 4.82 us  [around_x(): after = lax.ppermute(mine, 'x', backward)]
    all_to_all x1 -> x0, starting transfers between devices: 3.55 us -> none  [on_device(): lax.all_to_all(raw.T.reshape(NY, classes // NY, rows), 'y', 0, 0, tiled=T...]
    ppermute x2, starting transfers between devices: 4.01 us -> 6.87 us  [around_x(): before = lax.ppermute(mine, 'x', forward)]
    ppermute x2, waiting for transfers between devices: 8.14 us -> 5.42 us  [around_x(): oppb = lax.ppermute(after[half:], 'x', backward)]
  transfers between devices with their start and end apart: 14 -> 13, of which waited for: 11 -> 10; matrix products, arithmetic and copies ran while one was open for 2% -> 3% of each run, Pallas kernels for 0% -> 0%
where the time goes in v10:
time: 235 us; the launch traced here: 234 us
  blocking collectives  80.4 us (34%)
  starting transfers between devices  50.7 us (22%)
  waiting for transfers between devices  49.1 us (21%)
  Pallas kernels  20.4 us (9%)
  between operations  14.4 us (6%)
  local copies, waits for them, and re-layouts  11.4 us (5%)
  other arithmetic  6.23 us (3%)
    all_to_all x1, blocking collectives, on_device(): lax.all_to_all(raw.T.reshape(NY, classes // NY, rows), 'y', 0, 0, tiled=T...  30.5 us
    all_to_all x1, blocking collectives, on_device(): lax.all_to_all(jnp.broadcast_to(piece, (NZ,) + piece.shape), 'z', 0, 0, t...  26.1 us
    all_to_all x1, blocking collectives, on_device(): spread = lax.all_to_all(spread, 'y', 0, 0, tiled=True)  23.8 us
    pallas_call x2, Pallas kernels, sweep(): pl.pallas_call(sweep_kernel, grid_spec=pltpu.PrefetchScalarGridSpec(num_s...  20.4 us
    ppermute x2, waiting for transfers between devices, around_x(): before = lax.ppermute(mine, 'x', forward)  13.3 us
    all_to_all x1, waiting for transfers between devices, on_device(): lax.all_to_all(outgoing.reshape(TILES, 2 * SUB, width), ('x', 'y'), 0, 0,...  10.3 us
    all_to_all x1, starting transfers between devices, on_device(): lax.all_to_all(outgoing.reshape(TILES, 2 * SUB, width), ('x', 'y'), 0, 0,...  10.2 us
    all_to_all x1, waiting for transfers between devices, on_device(): lax.all_to_all(scored.reshape(TILES, 2 * SUB, TILE), ('x', 'y'), 0, 0, ti...  8.46 us
  transfers between devices with their start and end apart: 13, of which 10 were waited for; matrix products, arithmetic and copies ran while one was open for 3% of the time, Pallas kernels for 0%

profile of v10, /device:TPU:6, one launch (start us, length us, event | category | flops | bytes accessed | tf_op | source)
XLA Modules:
  0.0 233.8 jit_solution(1676935150989445244)
XLA Ops:
  6.5 1.2 constant_dynamic-slice_fusion.1
  7.8 0.8 copy.63
  8.5 0.1 eq.31
  8.6 0.2 convert_reduce_fusion.1
  8.8 0.1 reduce_sum.69
  8.9 0.1 copy.64
  9.0 0.7 multiply_add_fusion
  9.7 0.1 fusion.29
  9.7 0.3 convolution_convert_fusion
  10.0 0.9 reshape.97
  11.0 10.2 %all-to-all-start = ((bf16[32,4,1280]{2,1,0:T(4,128)(2,1)}), bf16[32,4,1280]{2,1,0:T(4,128)(2,1)S(1)}, u32[]{:S(2)}, u32[]{:S(2)}) async-start(bf16[32,4,1280]{2,1,0:T(4,128)(2,1)} %reshape.97), calls=%async_computation | async-start | bytes 655360 | tf_op jit(solution)/shard_map/all_to_all | solution.py:154
  21.9 0.3 exponential_reduce_fusion
  22.2 0.3 fusion
  22.6 10.3 %all-to-all-done = bf16[32,4,1280]{2,1,0:T(4,128)(2,1)S(1)} async-done(((bf16[32,4,1280]{2,1,0:T(4,128)(2,1)}), bf16[32,4,1280]{2,1,0:T(4,128)(2,1)S(1)}, u32[]{:S(2)}, u32[]{:S(2)}) %all-to-all-start) | async-done | bytes 327712 | tf_op jit(solution)/shard_map/all_to_all | solution.py:154
  32.9 0.2 multiply_reduce_fusion
  33.1 0.1 rsqrt.20
  33.3 0.7 fusion.16
  34.0 0.7 reshape.98
  34.7 6.6 %all-to-all-start.1 = ((bf16[32,4,512]{2,1,0:T(4,128)(2,1)}), bf16[32,4,512]{2,1,0:T(4,128)(2,1)S(1)}, u32[]{:S(2)}, u32[]{:S(2)}) async-start(bf16[32,4,512]{2,1,0:T(4,128)(2,1)} %reshape.98), calls=%async_computation.1 | async-start | bytes 262144 | tf_op jit(solution)/shard_map/all_to_all | solution.py:165
  41.3 0.0 all-gather.2.cloned.1.call-start
  41.4 8.5 %all-to-all-done.1 = bf16[32,4,512]{2,1,0:T(4,128)(2,1)S(1)} async-done(((bf16[32,4,512]{2,1,0:T(4,128)(2,1)}), bf16[32,4,512]{2,1,0:T(4,128)(2,1)S(1)}, u32[]{:S(2)}, u32[]{:S(2)}) %all-to-all-start.1) | async-done | bytes 131104 | tf_op jit(solution)/shard_map/all_to_all | solution.py:165
  49.8 0.1 reshape.99
  49.9 0.3 fusion.37
  50.2 0.1 fusion.24
  50.3 0.1 copy.68
  50.4 0.3 broadcast_in_dim.30
  50.7 26.1 %all_to_all.31 = bf16[8,17,2,1024]{3,2,1,0:T(2,128)(2,1)S(1)} all-to-all(bf16[8,17,2,1024]{3,2,1,0:T(2,128)(2,1)S(1)} %broadcast_in_dim.30), channel_id=1, replica_groups=mesh['x'=4,'y'=8,'z'=8,'c'=2] {'z'}, dimensions={0} | all-to-all | bytes 1114112 | tf_op jit(solution)/shard_map/all_to_all | solution.py:178
  76.9 0.4 slice_bitcast_fusion
  77.2 0.5 copy.70
  77.7 1.0 all_gather_reshape.3
  78.7 0.3 copy.69
  79.0 30.5 %all_to_all.32 = bf16[8,96,512]{2,1,0:T(8,128)(2,1)S(1)} all-to-all(bf16[8,96,512]{2,1,0:T(8,128)(2,1)S(1)} %bitcast.54), channel_id=1, replica_groups=mesh['x'=4,'y'=8,'z'=8,'c'=2] {'y'}, dimensions={0} | all-to-all | bytes 1572864 | tf_op jit(solution)/shard_map/all_to_all | solution.py:188
  109.5 2.6 %collective-permute-start.1 = (bf16[8,96,512]{2,1,0:T(8,128)(2,1)S(1)}, bf16[8,96,512]{2,1,0:T(8,128)(2,1)S(1)}, u32[]{:S(2)}, u32[]{:S(2)}) collective-permute-start(bf16[8,96,512]{2,1,0:T(8,128)(2,1)S(1)} %all_to_all.32), channel_id=1, source_target_pairs={{0,384},{128,0},{256,128},{384,256},{1,385},{129,1},{257,129},{385... | collective-permute-start | bytes 2359304 | tf_op jit(solution)/shard_map/ppermute | solution.py:117
  112.1 4.4 %collective-permute-start.2 = (bf16[8,96,512]{2,1,0:T(8,128)(2,1)S(1)}, bf16[8,96,512]{2,1,0:T(8,128)(2,1)S(1)}, u32[]{:S(2)}, u32[]{:S(2)}) collective-permute-start(bf16[8,96,512]{2,1,0:T(8,128)(2,1)S(1)} %all_to_all.32), channel_id=1, source_target_pairs={{0,128},{128,256},{256,384},{384,0},{1,129},{129,257},{257,385},{3... | collective-permute-start | bytes 2359304 | tf_op jit(solution)/shard_map/ppermute | solution.py:116
  116.6 1.9 collective-permute-start
  118.6 1.1 collective-permute-done
  119.7 0.1 pad_maximum_fusion.2
  119.8 4.8 %collective-permute-done.1 = bf16[8,96,512]{2,1,0:T(8,128)(2,1)S(1)} collective-permute-done((bf16[8,96,512]{2,1,0:T(8,128)(2,1)S(1)}, bf16[8,96,512]{2,1,0:T(8,128)(2,1)S(1)}, u32[]{:S(2)}, u32[]{:S(2)}) %collective-permute-start.1) | collective-permute-done | bytes 786464 | tf_op jit(solution)/shard_map/ppermute | solution.py:117
  124.6 1.5 collective-permute-done.2
  126.0 0.7 broadcast_in_dim.32
  126.8 7.3 %all-to-all-start.4 = ((f32[32,1,640]{2,1,0:T(1,128)}), f32[32,1,640]{2,1,0:T(1,128)S(1)}, u32[]{:S(2)}, u32[]{:S(2)}) async-start(f32[32,1,640]{2,1,0:T(1,128)} %broadcast_in_dim.32), calls=%async_computation.4 | async-start | bytes 163840 | tf_op jit(solution)/shard_map/all_to_all | solution.py:195
  134.1 0.1 reshape.105
  134.3 2.1 collective-permute-start.3
  136.4 0.8 slice.76
  137.2 3.7 %collective-permute-start.4 = (bf16[4,96,512]{2,1,0:T(8,128)(2,1)}, bf16[4,96,512]{2,1,0:T(8,128)(2,1)}, u32[]{:S(2)}, u32[]{:S(2)}) collective-permute-start(bf16[4,96,512]{2,1,0:T(8,128)(2,1)} %slice.76), channel_id=1, source_target_pairs={{0,384},{128,0},{256,128},{384,256},{1,385},{129,1},{257,129},{385... | collective-permute-start | bytes 1179656 | tf_op jit(solution)/shard_map/ppermute | solution.py:120
  140.9 1.8 all-to-all-done.4
  142.8 0.1 convert_element_type.127
  142.9 0.5 copy-done.5
  143.4 2.3 divide_convert_fusion
  145.8 0.8 slice_bitcast_fusion.4
  146.6 1.8 collective-permute-done.4
  148.4 1.5 divide_convert_fusion.3
  149.9 11.3 %shard_map.55.own = bf16[8,96,512]{2,1,0:T(8,128)(2,1)S(1)} custom-call(s32[256]{0:T(256)S(1)} %fusion.33.index_ref, bf16[16,256,1024]{2,1,0:T(8,128)(2,1)} %all-gather.2.cloned.1.call-done.w_ref, bf16[8,96,512]{2,1,0:T(8,128)(2,1)S(1)} %get-tuple-element.19.prior_ref.own, bf16[8,96,512]{2,1,0:T(8,128)(2,1)S(1)} %get-tuple-element.19.prior_ref.own, ...), custom_call_target="tpu_custom_call" | custom-call | flops 3221225472 | bytes 11534336 | tf_op jit(solution)/shard_map/pallas_call | solution.py:87
  161.2 2.4 %collective-permute-start.6 = (bf16[8,96,512]{2,1,0:T(8,128)(2,1)S(1)}, bf16[8,96,512]{2,1,0:T(8,128)(2,1)S(1)}, u32[]{:S(2)}, u32[]{:S(2)}) collective-permute-start(bf16[8,96,512]{2,1,0:T(8,128)(2,1)S(1)} %shard_map.55.own), channel_id=1, source_target_pairs={{0,128},{128,256},{256,384},{384,0},{1,129},{129,257},{257,385},{3... | collective-permute-start | bytes 2359304 | tf_op jit(solution)/shard_map/ppermute | solution.py:116
  163.7 3.4 %collective-permute-start.5 = (bf16[8,96,512]{2,1,0:T(8,128)(2,1)S(1)}, bf16[8,96,512]{2,1,0:T(8,128)(2,1)S(1)}, u32[]{:S(2)}, u32[]{:S(2)}) collective-permute-start(bf16[8,96,512]{2,1,0:T(8,128)(2,1)S(1)} %shard_map.55.own), channel_id=1, source_target_pairs={{0,384},{128,0},{256,128},{384,256},{1,385},{129,1},{257,129},{385... | collective-permute-start | bytes 2359304 | tf_op jit(solution)/shard_map/ppermute | solution.py:117
  167.1 11.8 %collective-permute-done.6.before = bf16[8,96,512]{2,1,0:T(8,128)(2,1)S(1)} collective-permute-done((bf16[8,96,512]{2,1,0:T(8,128)(2,1)S(1)}, bf16[8,96,512]{2,1,0:T(8,128)(2,1)S(1)}, u32[]{:S(2)}, u32[]{:S(2)}) %collective-permute-start.6) | collective-permute-done | bytes 786464 | tf_op jit(solution)/shard_map/ppermute | solution.py:116
  179.0 2.4 %collective-permute-start.7 = (bf16[4,96,512]{2,1,0:T(8,128)(2,1)S(1)}, bf16[4,96,512]{2,1,0:T(8,128)(2,1)S(1)}, u32[]{:S(2)}, u32[]{:S(2)}) collective-permute-start(bf16[4,96,512]{2,1,0:T(8,128)(2,1)S(1)} %slice.79), channel_id=1, source_target_pairs={{0,128},{128,256},{256,384},{384,0},{1,129},{129,257},{257,385},{3... | collective-permute-start | bytes 1179656 | tf_op jit(solution)/shard_map/ppermute | solution.py:119
  181.4 3.4 %collective-permute-start.8 = (bf16[4,96,512]{2,1,0:T(8,128)(2,1)S(1)}, bf16[4,96,512]{2,1,0:T(8,128)(2,1)S(1)}, u32[]{:S(2)}, u32[]{:S(2)}) collective-permute-start(bf16[4,96,512]{2,1,0:T(8,128)(2,1)S(1)} %slice.80), channel_id=1, source_target_pairs={{0,384},{128,0},{256,128},{384,256},{1,385},{129,1},{257,129},{385... | collective-permute-start | bytes 1179656 | tf_op jit(solution)/shard_map/ppermute | solution.py:120
  184.9 3.8 %collective-permute-done.7.oppa = bf16[4,96,512]{2,1,0:T(8,128)(2,1)S(1)} collective-permute-done((bf16[4,96,512]{2,1,0:T(8,128)(2,1)S(1)}, bf16[4,96,512]{2,1,0:T(8,128)(2,1)S(1)}, u32[]{:S(2)}, u32[]{:S(2)}) %collective-permute-start.7) | collective-permute-done | bytes 393248 | tf_op jit(solution)/shard_map/ppermute | solution.py:119
  188.6 3.7 %collective-permute-done.8.oppb = bf16[4,96,512]{2,1,0:T(8,128)(2,1)S(1)} collective-permute-done((bf16[4,96,512]{2,1,0:T(8,128)(2,1)S(1)}, bf16[4,96,512]{2,1,0:T(8,128)(2,1)S(1)}, u32[]{:S(2)}, u32[]{:S(2)}) %collective-permute-start.8) | collective-permute-done | bytes 393248 | tf_op jit(solution)/shard_map/ppermute | solution.py:120
  192.3 9.0 %shard_map.56 = bf16[8,96,512]{2,1,0:T(8,128)(2,1)S(1)} custom-call(s32[256]{0:T(256)S(1)} %fusion.33.index_ref, bf16[16,256,1024]{2,1,0:T(8,128)(2,1)S(1)} %copy-done, bf16[8,96,512]{2,1,0:T(8,128)(2,1)S(1)} %get-tuple-element.19.prior_ref.own, bf16[8,96,512]{2,1,0:T(8,128)(2,1)S(1)} %shard_map.55.own, ...), custom_call_target="tpu_custom_call" | custom-call | flops 3221225472 | bytes 11534336 | tf_op jit(solution)/shard_map/pallas_call | solution.py:87
  201.3 23.8 %all_to_all.33 = bf16[8,96,512]{2,1,0:T(8,128)(2,1)S(1)} all-to-all(bf16[8,96,512]{2,1,0:T(8,128)(2,1)S(1)} %shard_map.56), channel_id=1, replica_groups=mesh['x'=4,'y'=8,'z'=8,'c'=2] {'y'}, dimensions={0} | all-to-all | bytes 1572864 | tf_op jit(solution)/shard_map/all_to_all | solution.py:215
  225.1 0.2 convert_log_fusion
  225.4 1.6 copy.71
  (43 shorter events, 0.4 us)
Async XLA Ops:
  6.5 15.7 %copy-start.4 = (bf16[512,1280]{1,0:T(8,128)(2,1)S(1)}, bf16[512,1280]{1,0:T(8,128)(2,1)}, u32[]{:S(2)}) copy-start(bf16[512,1280]{1,0:T(8,128)(2,1)} %param.5) | copy-start | bytes 3932164
  6.5 15.3 %copy-start.6 = (f32[768]{0:T(1024)S(1)}, f32[768]{0:T(1024)}, u32[]{:S(2)}) copy-start(f32[768]{0:T(1024)} %param.6) | copy-start | bytes 9220
  6.5 15.3 %copy-start.1 = (bf16[512,768]{1,0:T(8,128)(2,1)S(1)}, bf16[512,768]{1,0:T(8,128)(2,1)}, u32[]{:S(2)}) copy-start(bf16[512,768]{1,0:T(8,128)(2,1)} %param.7) | copy-start | bytes 2359300
  11.0 21.9 %all-to-all-start = ((bf16[32,4,1280]{2,1,0:T(4,128)(2,1)}), bf16[32,4,1280]{2,1,0:T(4,128)(2,1)S(1)}, u32[]{:S(2)}, u32[]{:S(2)}) async-start(bf16[32,4,1280]{2,1,0:T(4,128)(2,1)} %reshape.97), calls=%async_computation | async-start | bytes 655360 | tf_op jit(solution)/shard_map/all_to_all | solution.py:154
  34.7 15.1 %all-to-all-start.1 = ((bf16[32,4,512]{2,1,0:T(4,128)(2,1)}), bf16[32,4,512]{2,1,0:T(4,128)(2,1)S(1)}, u32[]{:S(2)}, u32[]{:S(2)}) async-start(bf16[32,4,512]{2,1,0:T(4,128)(2,1)} %reshape.98), calls=%async_computation.1 | async-start | bytes 262144 | tf_op jit(solution)/shard_map/all_to_all | solution.py:165
  41.3 108.6 %all-gather.2.cloned.1.call-start = ((), (), s32[]{:S(2)}) async-start(), calls=%async_computation.6 | async-start | bytes 8912896 | tf_op jit(solution)/shard_map/all_gather | solution.py:183
  109.5 15.1 %collective-permute-start.1 = (bf16[8,96,512]{2,1,0:T(8,128)(2,1)S(1)}, bf16[8,96,512]{2,1,0:T(8,128)(2,1)S(1)}, u32[]{:S(2)}, u32[]{:S(2)}) collective-permute-start(bf16[8,96,512]{2,1,0:T(8,128)(2,1)S(1)} %all_to_all.32), channel_id=1, source_target_pairs={{0,384},{128,0},{256,128},{384,256},{1,385},{129,1},{257,129},{385... | collective-permute-start | bytes 2359304 | tf_op jit(solution)/shard_map/ppermute | solution.py:117
  112.1 13.9 %collective-permute-start.2 = (bf16[8,96,512]{2,1,0:T(8,128)(2,1)S(1)}, bf16[8,96,512]{2,1,0:T(8,128)(2,1)S(1)}, u32[]{:S(2)}, u32[]{:S(2)}) collective-permute-start(bf16[8,96,512]{2,1,0:T(8,128)(2,1)S(1)} %all_to_all.32), channel_id=1, source_target_pairs={{0,128},{128,256},{256,384},{384,0},{1,129},{129,257},{257,385},{3... | collective-permute-start | bytes 2359304 | tf_op jit(solution)/shard_map/ppermute | solution.py:116
  116.6 3.1 %collective-permute-start = (f32[512]{0:T(512)S(1)}, f32[512]{0:T(512)S(1)}, u32[]{:S(2)}, u32[]{:S(2)}) collective-permute-start(f32[512]{0:T(512)S(1)} %bitcast.61), channel_id=1, source_target_pairs={{0,1},{1,0},{2,3},{3,2},{4,5},{5,4},{6,7},{7,6},{8,9},{9,8},{10,11... | collective-permute-start | bytes 6152 | tf_op jit(solution)/shard_map/ppermute | solution.py:191
  124.6 18.3 %copy-start.2 = (bf16[8,96,512]{2,1,0:T(8,128)(2,1)}, bf16[8,96,512]{2,1,0:T(8,128)(2,1)S(1)}, u32[]{:S(2)}) copy-start(bf16[8,96,512]{2,1,0:T(8,128)(2,1)S(1)} %collective-permute-done.1) | copy-start | bytes 2359300
  126.0 16.9 %copy-start.3 = (bf16[8,96,512]{2,1,0:T(8,128)(2,1)}, bf16[8,96,512]{2,1,0:T(8,128)(2,1)S(1)}, u32[]{:S(2)}) copy-start(bf16[8,96,512]{2,1,0:T(8,128)(2,1)S(1)} %collective-permute-done.2) | copy-start | bytes 2359300
  126.8 16.0 %all-to-all-start.4 = ((f32[32,1,640]{2,1,0:T(1,128)}), f32[32,1,640]{2,1,0:T(1,128)S(1)}, u32[]{:S(2)}, u32[]{:S(2)}) async-start(f32[32,1,640]{2,1,0:T(1,128)} %broadcast_in_dim.32), calls=%async_computation.4 | async-start | bytes 163840 | tf_op jit(solution)/shard_map/all_to_all | solution.py:195
  134.3 12.3 %collective-permute-start.3 = (bf16[4,96,512]{2,1,0:T(8,128)(2,1)S(1)}, bf16[4,96,512]{2,1,0:T(8,128)(2,1)}, u32[]{:S(2)}, u32[]{:S(2)}) collective-permute-start(bf16[4,96,512]{2,1,0:T(8,128)(2,1)S(1)} %slice.74), channel_id=1, source_target_pairs={{0,128},{128,256},{256,384},{384,0},{1,129},{129,257},{257,385},{3... | collective-permute-start | bytes 1179656 | tf_op jit(solution)/shard_map/ppermute | solution.py:119
  137.2 11.2 %collective-permute-start.4 = (bf16[4,96,512]{2,1,0:T(8,128)(2,1)}, bf16[4,96,512]{2,1,0:T(8,128)(2,1)}, u32[]{:S(2)}, u32[]{:S(2)}) collective-permute-start(bf16[4,96,512]{2,1,0:T(8,128)(2,1)} %slice.76), channel_id=1, source_target_pairs={{0,384},{128,0},{256,128},{384,256},{1,385},{129,1},{257,129},{385... | collective-permute-start | bytes 1179656 | tf_op jit(solution)/shard_map/ppermute | solution.py:120
  142.8 0.6 copy-start.5
  149.9 42.4 %copy-start = (bf16[16,256,1024]{2,1,0:T(8,128)(2,1)S(1)}, bf16[16,256,1024]{2,1,0:T(8,128)(2,1)}, u32[]{:S(2)}) copy-start(bf16[16,256,1024]{2,1,0:T(8,128)(2,1)} %all-gather.2.cloned.1.call-done.w_ref) | copy-start | bytes 25165828
  161.2 17.7 %collective-permute-start.6 = (bf16[8,96,512]{2,1,0:T(8,128)(2,1)S(1)}, bf16[8,96,512]{2,1,0:T(8,128)(2,1)S(1)}, u32[]{:S(2)}, u32[]{:S(2)}) collective-permute-start(bf16[8,96,512]{2,1,0:T(8,128)(2,1)S(1)} %shard_map.55.own), channel_id=1, source_target_pairs={{0,128},{128,256},{256,384},{384,0},{1,129},{129,257},{257,385},{3... | collective-permute-start | bytes 2359304 | tf_op jit(solution)/shard_map/ppermute | solution.py:116
  163.7 17.7 %collective-permute-start.5 = (bf16[8,96,512]{2,1,0:T(8,128)(2,1)S(1)}, bf16[8,96,512]{2,1,0:T(8,128)(2,1)S(1)}, u32[]{:S(2)}, u32[]{:S(2)}) collective-permute-start(bf16[8,96,512]{2,1,0:T(8,128)(2,1)S(1)} %shard_map.55.own), channel_id=1, source_target_pairs={{0,384},{128,0},{256,128},{384,256},{1,385},{129,1},{257,129},{385... | collective-permute-start | bytes 2359304 | tf_op jit(solution)/shard_map/ppermute | solution.py:117
  179.0 9.7 %collective-permute-start.7 = (bf16[4,96,512]{2,1,0:T(8,128)(2,1)S(1)}, bf16[4,96,512]{2,1,0:T(8,128)(2,1)S(1)}, u32[]{:S(2)}, u32[]{:S(2)}) collective-permute-start(bf16[4,96,512]{2,1,0:T(8,128)(2,1)S(1)} %slice.79), channel_id=1, source_target_pairs={{0,128},{128,256},{256,384},{384,0},{1,129},{129,257},{257,385},{3... | collective-permute-start | bytes 1179656 | tf_op jit(solution)/shard_map/ppermute | solution.py:119
  181.4 10.9 %collective-permute-start.8 = (bf16[4,96,512]{2,1,0:T(8,128)(2,1)S(1)}, bf16[4,96,512]{2,1,0:T(8,128)(2,1)S(1)}, u32[]{:S(2)}, u32[]{:S(2)}) collective-permute-start(bf16[4,96,512]{2,1,0:T(8,128)(2,1)S(1)} %slice.80), channel_id=1, source_target_pairs={{0,384},{128,0},{256,128},{384,256},{1,385},{129,1},{257,129},{385... | collective-permute-start | bytes 1179656 | tf_op jit(solution)/shard_map/ppermute | solution.py:120
Sparse Core Ops, SparseCore 0:
  78.9 62.2 all-gather.1

commit v11 on v8

--- a/solution.py
+++ b/solution.py
@@ -136,18 +136,19 @@
     x, y = lax.axis_index("x"), lax.axis_index("y")
     z, core = lax.axis_index("z"), lax.axis_index("c")
 
+    lists = tile_lists.T
+    order = jnp.arange(PER, dtype=jnp.int32).reshape(NT, NBLK)
+    same = (lists[:, :, None, None] == lists) & (order[:, :, None, None] > order)
+    position = lists * 2 + jnp.sum(same.astype(jnp.int32), axis=(2, 3))
+    hits = position[:, :, None] == jnp.arange(SLOTS, dtype=jnp.int32)
+    hits = hits.astype(BF)
     owners = tile_lists.reshape(PER)
-    order = jnp.arange(PER, dtype=jnp.int32)
-    same = (owners[:, None] == owners[None, :]) & (order[None, :] < order[:, None])
-    position = owners * 2 + jnp.sum(same.astype(jnp.int32), axis=1)
-    hits = position.reshape(NBLK, NT)[:, :, None] == jnp.arange(SLOTS, dtype=jnp.int32)
-    hits = hits.astype(BF)
 
     row = core * ROWS_C + z * SUB
     mine = lax.dynamic_slice_in_dim(features.reshape(NBLK, QB, width), row, SUB, axis=1)
     outgoing = jnp.einsum(
         "bs,bf->sf",
-        hits.sum(axis=1),
+        hits.sum(axis=0),
         mine.reshape(NBLK, SUB * width),
         preferred_element_type=F32,
     ).astype(BF)
@@ -165,7 +166,7 @@
     back = lax.all_to_all(
         scored.reshape(TILES, 2 * SUB, TILE), ("x", "y"), 0, 0, tiled=True
     ).reshape(SLOTS, SUB * TILE)
-    chosen = jnp.einsum("bks,sf->bkf", hits, back, preferred_element_type=F32)
+    chosen = jnp.einsum("kbs,sf->bkf", hits, back, preferred_element_type=F32)
     chosen = chosen.reshape(NBLK, NT, SUB, TILE)
     denominator = jnp.sum(chosen, axis=(1, 3), keepdims=True)
     scaled = (ALPHA * chosen / denominator).astype(BF)

time: 233 us -> 233 us (level)
  transfers between devices with their start and end apart: 14 -> 14, of which waited for: 11 -> 11; matrix products, arithmetic and copies ran while one was open for 2% -> 3% of each run, Pallas kernels for 0% -> 0%
where the time goes in v11:
time: 233 us
  waiting for transfers between devices  79.4 us (34%)
  starting transfers between devices  52.6 us (23%)
  blocking collectives  49 us (21%)
  Pallas kernels  20.4 us (9%)
  between operations  14.5 us (6%)
  local copies, waits for them, and re-layouts  9.41 us (4%)
  other arithmetic  5.96 us (3%)
    all_to_all x1, blocking collectives, on_device(): lax.all_to_all(jnp.broadcast_to(piece, (NZ,) + piece.shape), 'z', 0, 0, t...  26.2 us
    all_to_all x1, waiting for transfers between devices, on_device(): lax.all_to_all(raw.T.reshape(NY, classes // NY, rows), 'y', 0, 0, tiled=T...  24.4 us
    all_to_all x1, blocking collectives, on_device(): spread = lax.all_to_all(spread, 'y', 0, 0, tiled=True)  22.8 us
    pallas_call x2, Pallas kernels, sweep(): pl.pallas_call(sweep_kernel, grid_spec=pltpu.PrefetchScalarGridSpec(num_s...  20.4 us
    ppermute x2, waiting for transfers between devices, around_x(): before = lax.ppermute(mine, 'x', forward)  19.3 us
    all_to_all x1, waiting for transfers between devices, on_device(): lax.all_to_all(outgoing.reshape(TILES, 2 * SUB, width), ('x', 'y'), 0, 0,...  10.3 us
    all_to_all x1, starting transfers between devices, on_device(): lax.all_to_all(outgoing.reshape(TILES, 2 * SUB, width), ('x', 'y'), 0, 0,...  10.2 us
    all_to_all x1, waiting for transfers between devices, on_device(): lax.all_to_all(scored.reshape(TILES, 2 * SUB, TILE), ('x', 'y'), 0, 0, ti...  8.4 us
  transfers between devices with their start and end apart: 14, of which 11 were waited for; matrix products, arithmetic and copies ran while one was open for 3% of the time, Pallas kernels for 0%

profile of v11, /device:TPU:6, one launch (start us, length us, event | category | flops | bytes accessed | tf_op | source)
XLA Modules:
  0.0 232.5 jit_solution(16712485688159808256)
XLA Ops:
  6.6 1.2 constant_dynamic-slice_fusion.1
  7.8 0.9 convert_reduce_fusion.1
  8.7 0.7 multiply_add_fusion.1
  9.4 0.1 fusion.25
  9.5 0.3 convolution_convert_fusion
  9.8 0.9 reshape.115
  10.7 10.2 %all-to-all-start = ((bf16[32,4,1280]{2,1,0:T(4,128)(2,1)}), bf16[32,4,1280]{2,1,0:T(4,128)(2,1)S(1)}, u32[]{:S(2)}, u32[]{:S(2)}) async-start(bf16[32,4,1280]{2,1,0:T(4,128)(2,1)} %reshape.115), calls=%async_computation | async-start | bytes 655360 | tf_op jit(solution)/shard_map/all_to_all | solution.py:155
  21.6 0.3 exponential_reduce_fusion
  22.0 0.3 fusion
  22.3 10.3 %all-to-all-done = bf16[32,4,1280]{2,1,0:T(4,128)(2,1)S(1)} async-done(((bf16[32,4,1280]{2,1,0:T(4,128)(2,1)}), bf16[32,4,1280]{2,1,0:T(4,128)(2,1)S(1)}, u32[]{:S(2)}, u32[]{:S(2)}) %all-to-all-start) | async-done | bytes 327712 | tf_op jit(solution)/shard_map/all_to_all | solution.py:155
  32.6 0.2 multiply_reduce_fusion
  32.9 0.1 rsqrt.20
  33.0 0.7 fusion.16
  33.7 0.7 reshape.116
  34.4 6.6 %all-to-all-start.1 = ((bf16[32,4,512]{2,1,0:T(4,128)(2,1)}), bf16[32,4,512]{2,1,0:T(4,128)(2,1)S(1)}, u32[]{:S(2)}, u32[]{:S(2)}) async-start(bf16[32,4,512]{2,1,0:T(4,128)(2,1)} %reshape.116), calls=%async_computation.1 | async-start | bytes 262144 | tf_op jit(solution)/shard_map/all_to_all | solution.py:166
  41.0 0.0 all-gather.2.cloned.1.call-start
  41.1 8.4 %all-to-all-done.1 = bf16[32,4,512]{2,1,0:T(4,128)(2,1)S(1)} async-done(((bf16[32,4,512]{2,1,0:T(4,128)(2,1)}), bf16[32,4,512]{2,1,0:T(4,128)(2,1)S(1)}, u32[]{:S(2)}, u32[]{:S(2)}) %all-to-all-start.1) | async-done | bytes 131104 | tf_op jit(solution)/shard_map/all_to_all | solution.py:166
  49.5 0.1 reshape.125
  49.6 0.2 broadcast_multiply_fusion
  49.8 0.1 reduce_sum.78
  49.9 0.1 reduce_sum.79
  50.0 0.1 copy.66
  50.1 0.1 fusion.23
  50.2 0.1 copy.60
  50.3 0.3 broadcast_in_dim.31
  50.6 26.2 %all_to_all.31 = bf16[8,17,2,1024]{3,2,1,0:T(2,128)(2,1)S(1)} all-to-all(bf16[8,17,2,1024]{3,2,1,0:T(2,128)(2,1)S(1)} %broadcast_in_dim.31), channel_id=1, replica_groups=mesh['x'=4,'y'=8,'z'=8,'c'=2] {'z'}, dimensions={0} | all-to-all | bytes 1114112 | tf_op jit(solution)/shard_map/all_to_all | solution.py:179
  76.8 0.4 slice_bitcast_fusion
  77.1 0.5 copy.63
  77.6 1.0 all_gather_reshape.3
  78.7 1.2 copy.62
  79.8 3.5 %all-to-all-start.3 = ((bf16[8,96,512]{2,1,0:T(8,128)(2,1)}), bf16[8,96,512]{2,1,0:T(8,128)(2,1)S(1)}, u32[]{:S(2)}, u32[]{:S(2)}) async-start(bf16[8,96,512]{2,1,0:T(8,128)(2,1)} %bitcast.7), calls=%async_computation.3 | async-start | bytes 1572864 | tf_op jit(solution)/shard_map/all_to_all | solution.py:189
  83.5 1.9 collective-permute-start
  85.4 0.1 copy.61
  85.5 0.1 convert_element_type.124
  85.6 0.9 collective-permute-done
  86.5 0.1 pad_maximum_fusion.2
  86.6 24.4 %all-to-all-done.3 = bf16[8,96,512]{2,1,0:T(8,128)(2,1)S(1)} async-done(((bf16[8,96,512]{2,1,0:T(8,128)(2,1)}), bf16[8,96,512]{2,1,0:T(8,128)(2,1)S(1)}, u32[]{:S(2)}, u32[]{:S(2)}) %all-to-all-start.3) | async-done | bytes 786464 | tf_op jit(solution)/shard_map/all_to_all | solution.py:189
  111.0 0.7 broadcast_in_dim.33
  111.7 6.8 %all-to-all-start.4 = ((f32[32,1,640]{2,1,0:T(1,128)}), f32[32,1,640]{2,1,0:T(1,128)S(1)}, u32[]{:S(2)}, u32[]{:S(2)}) async-start(f32[32,1,640]{2,1,0:T(1,128)} %broadcast_in_dim.33), calls=%async_computation.4 | async-start | bytes 163840 | tf_op jit(solution)/shard_map/all_to_all | solution.py:195
  118.5 0.1 reshape.123
  118.6 2.1 collective-permute-start.2
  120.7 3.7 %collective-permute-start.1 = (bf16[8,96,512]{2,1,0:T(8,128)(2,1)S(1)}, bf16[8,96,512]{2,1,0:T(8,128)(2,1)S(1)}, u32[]{:S(2)}, u32[]{:S(2)}) collective-permute-start(bf16[8,96,512]{2,1,0:T(8,128)(2,1)S(1)} %all-to-all-done.3), channel_id=1, source_target_pairs={{0,384},{128,0},{256,128},{384,256},{1,385},{129,1},{257,129},{385... | collective-permute-start | bytes 2359304 | tf_op jit(solution)/shard_map/ppermute | solution.py:117
  124.5 2.7 %all-to-all-done.4 = f32[32,1,640]{2,1,0:T(1,128)S(1)} async-done(((f32[32,1,640]{2,1,0:T(1,128)}), f32[32,1,640]{2,1,0:T(1,128)S(1)}, u32[]{:S(2)}, u32[]{:S(2)}) %all-to-all-start.4) | async-done | bytes 81952 | tf_op jit(solution)/shard_map/all_to_all | solution.py:195
  127.2 0.1 convert_element_type.126
  127.3 9.1 %collective-permute-done.2 = bf16[8,96,512]{2,1,0:T(8,128)(2,1)S(1)} collective-permute-done((bf16[8,96,512]{2,1,0:T(8,128)(2,1)S(1)}, bf16[8,96,512]{2,1,0:T(8,128)(2,1)S(1)}, u32[]{:S(2)}, u32[]{:S(2)}) %collective-permute-start.2) | collective-permute-done | bytes 786464 | tf_op jit(solution)/shard_map/ppermute | solution.py:116
  136.5 2.2 collective-permute-start.3
  138.8 3.7 %collective-permute-start.4 = (bf16[4,96,512]{2,1,0:T(8,128)(2,1)S(1)}, bf16[4,96,512]{2,1,0:T(8,128)(2,1)S(1)}, u32[]{:S(2)}, u32[]{:S(2)}) collective-permute-start(bf16[4,96,512]{2,1,0:T(8,128)(2,1)S(1)} %slice.76), channel_id=1, source_target_pairs={{0,384},{128,0},{256,128},{384,256},{1,385},{129,1},{257,129},{385... | collective-permute-start | bytes 1179656 | tf_op jit(solution)/shard_map/ppermute | solution.py:120
  142.4 2.3 %divide_convert_fusion = (bf16[8,96,512]{2,1,0:T(8,128)(2,1)S(1)}, bf16[8,96,512]{2,1,0:T(8,128)(2,1)S(1)}, bf16[8,96,512]{2,1,0:T(8,128)(2,1)S(1)}) fusion(bf16[8,96,512]{2,1,0:T(8,128)(2,1)} %copy-done.2, f32[8,512]{1,0:T(8,128)S(1)} %get-tuple-element.11, f32[96]{0:T(128)S(1)} %fusion.31, f32[8,512]{1,0:T(8,128)S(1)} %get-tuple-element.12, ...), kind=kLoop, calls=%fused_computation.7 | loop fusion | flops 4718592 | bytes 4768128 | tf_op jit(solution)/shard_map/convert_element_type | solution.py:208
  144.8 1.4 collective-permute-done.3
  146.2 3.5 %collective-permute-done.4 = bf16[4,96,512]{2,1,0:T(8,128)(2,1)S(1)} collective-permute-done((bf16[4,96,512]{2,1,0:T(8,128)(2,1)S(1)}, bf16[4,96,512]{2,1,0:T(8,128)(2,1)S(1)}, u32[]{:S(2)}, u32[]{:S(2)}) %collective-permute-start.4) | collective-permute-done | bytes 393248 | tf_op jit(solution)/shard_map/ppermute | solution.py:120
  149.6 0.4 divide_convert_fusion.3
  150.0 0.0 all-gather.2.cloned.1.call-done.w_ref
  150.0 11.4 %shard_map.55.own = bf16[8,96,512]{2,1,0:T(8,128)(2,1)S(1)} custom-call(s32[256]{0:T(256)S(1)} %fusion.29.index_ref, bf16[16,256,1024]{2,1,0:T(8,128)(2,1)} %all-gather.2.cloned.1.call-done.w_ref, bf16[8,96,512]{2,1,0:T(8,128)(2,1)S(1)} %get-tuple-element.21.prior_ref.own, bf16[8,96,512]{2,1,0:T(8,128)(2,1)S(1)} %get-tuple-element.21.prior_ref.own, ...), custom_call_target="tpu_custom_call" | custom-call | flops 3221225472 | bytes 11534336 | tf_op jit(solution)/shard_map/pallas_call | solution.py:87
  161.4 1.9 collective-permute-start.6
  163.3 3.9 %collective-permute-start.5 = (bf16[8,96,512]{2,1,0:T(8,128)(2,1)S(1)}, bf16[8,96,512]{2,1,0:T(8,128)(2,1)S(1)}, u32[]{:S(2)}, u32[]{:S(2)}) collective-permute-start(bf16[8,96,512]{2,1,0:T(8,128)(2,1)S(1)} %shard_map.55.own), channel_id=1, source_target_pairs={{0,384},{128,0},{256,128},{384,256},{1,385},{129,1},{257,129},{385... | collective-permute-start | bytes 2359304 | tf_op jit(solution)/shard_map/ppermute | solution.py:117
  167.2 10.2 %collective-permute-done.6.before = bf16[8,96,512]{2,1,0:T(8,128)(2,1)S(1)} collective-permute-done((bf16[8,96,512]{2,1,0:T(8,128)(2,1)S(1)}, bf16[8,96,512]{2,1,0:T(8,128)(2,1)S(1)}, u32[]{:S(2)}, u32[]{:S(2)}) %collective-permute-start.6) | collective-permute-done | bytes 786464 | tf_op jit(solution)/shard_map/ppermute | solution.py:116
  177.4 3.6 %collective-permute-start.7 = (bf16[4,96,512]{2,1,0:T(8,128)(2,1)S(1)}, bf16[4,96,512]{2,1,0:T(8,128)(2,1)S(1)}, u32[]{:S(2)}, u32[]{:S(2)}) collective-permute-start(bf16[4,96,512]{2,1,0:T(8,128)(2,1)S(1)} %slice.79), channel_id=1, source_target_pairs={{0,128},{128,256},{256,384},{384,0},{1,129},{129,257},{257,385},{3... | collective-permute-start | bytes 1179656 | tf_op jit(solution)/shard_map/ppermute | solution.py:119
  181.1 2.4 %collective-permute-start.8 = (bf16[4,96,512]{2,1,0:T(8,128)(2,1)S(1)}, bf16[4,96,512]{2,1,0:T(8,128)(2,1)S(1)}, u32[]{:S(2)}, u32[]{:S(2)}) collective-permute-start(bf16[4,96,512]{2,1,0:T(8,128)(2,1)S(1)} %slice.80), channel_id=1, source_target_pairs={{0,384},{128,0},{256,128},{384,256},{1,385},{129,1},{257,129},{385... | collective-permute-start | bytes 1179656 | tf_op jit(solution)/shard_map/ppermute | solution.py:120
  183.5 3.8 %collective-permute-done.7.oppa = bf16[4,96,512]{2,1,0:T(8,128)(2,1)S(1)} collective-permute-done((bf16[4,96,512]{2,1,0:T(8,128)(2,1)S(1)}, bf16[4,96,512]{2,1,0:T(8,128)(2,1)S(1)}, u32[]{:S(2)}, u32[]{:S(2)}) %collective-permute-start.7) | collective-permute-done | bytes 393248 | tf_op jit(solution)/shard_map/ppermute | solution.py:119
  187.3 4.7 %collective-permute-done.8.oppb = bf16[4,96,512]{2,1,0:T(8,128)(2,1)S(1)} collective-permute-done((bf16[4,96,512]{2,1,0:T(8,128)(2,1)S(1)}, bf16[4,96,512]{2,1,0:T(8,128)(2,1)S(1)}, u32[]{:S(2)}, u32[]{:S(2)}) %collective-permute-start.8) | collective-permute-done | bytes 393248 | tf_op jit(solution)/shard_map/ppermute | solution.py:120
  191.9 9.0 %shard_map.56 = bf16[8,96,512]{2,1,0:T(8,128)(2,1)S(1)} custom-call(s32[256]{0:T(256)S(1)} %fusion.29.index_ref, bf16[16,256,1024]{2,1,0:T(8,128)(2,1)S(1)} %copy-done, bf16[8,96,512]{2,1,0:T(8,128)(2,1)S(1)} %get-tuple-element.21.prior_ref.own, bf16[8,96,512]{2,1,0:T(8,128)(2,1)S(1)} %shard_map.55.own, ...), custom_call_target="tpu_custom_call" | custom-call | flops 3221225472 | bytes 11534336 | tf_op jit(solution)/shard_map/pallas_call | solution.py:87
  201.0 22.8 %all_to_all.32 = bf16[8,96,512]{2,1,0:T(8,128)(2,1)S(1)} all-to-all(bf16[8,96,512]{2,1,0:T(8,128)(2,1)S(1)} %shard_map.56), channel_id=1, replica_groups=mesh['x'=4,'y'=8,'z'=8,'c'=2] {'y'}, dimensions={0} | all-to-all | bytes 1572864 | tf_op jit(solution)/shard_map/all_to_all | solution.py:216
  223.8 0.2 convert_log_fusion
  224.0 1.6 copy.64
  (46 shorter events, 0.5 us)
Async XLA Ops:
  6.5 15.4 %copy-start.4 = (bf16[512,1280]{1,0:T(8,128)(2,1)S(1)}, bf16[512,1280]{1,0:T(8,128)(2,1)}, u32[]{:S(2)}) copy-start(bf16[512,1280]{1,0:T(8,128)(2,1)} %param.5) | copy-start | bytes 3932164
  6.5 15.1 %copy-start.5 = (f32[768]{0:T(1024)S(1)}, f32[768]{0:T(1024)}, u32[]{:S(2)}) copy-start(f32[768]{0:T(1024)} %param.6) | copy-start | bytes 9220
  6.5 15.1 %copy-start.1 = (bf16[512,768]{1,0:T(8,128)(2,1)S(1)}, bf16[512,768]{1,0:T(8,128)(2,1)}, u32[]{:S(2)}) copy-start(bf16[512,768]{1,0:T(8,128)(2,1)} %param.7) | copy-start | bytes 2359300
  10.7 21.9 %all-to-all-start = ((bf16[32,4,1280]{2,1,0:T(4,128)(2,1)}), bf16[32,4,1280]{2,1,0:T(4,128)(2,1)S(1)}, u32[]{:S(2)}, u32[]{:S(2)}) async-start(bf16[32,4,1280]{2,1,0:T(4,128)(2,1)} %reshape.115), calls=%async_computation | async-start | bytes 655360 | tf_op jit(solution)/shard_map/all_to_all | solution.py:155
  34.4 15.1 %all-to-all-start.1 = ((bf16[32,4,512]{2,1,0:T(4,128)(2,1)}), bf16[32,4,512]{2,1,0:T(4,128)(2,1)S(1)}, u32[]{:S(2)}, u32[]{:S(2)}) async-start(bf16[32,4,512]{2,1,0:T(4,128)(2,1)} %reshape.116), calls=%async_computation.1 | async-start | bytes 262144 | tf_op jit(solution)/shard_map/all_to_all | solution.py:166
  41.0 109.0 %all-gather.2.cloned.1.call-start = ((), (), s32[]{:S(2)}) async-start(), calls=%async_computation.6 | async-start | bytes 8912896 | tf_op jit(solution)/shard_map/all_gather | solution.py:184
  78.7 6.7 %copy-start.6 = (s32[16,2]{0,1:T(2,128)S(1)}, s32[16,2]{0,1:T(2,128)}, u32[]{:S(2)}) copy-start(s32[16,2]{0,1:T(2,128)} %param.8) | copy-start | bytes 388
  79.8 31.2 %all-to-all-start.3 = ((bf16[8,96,512]{2,1,0:T(8,128)(2,1)}), bf16[8,96,512]{2,1,0:T(8,128)(2,1)S(1)}, u32[]{:S(2)}, u32[]{:S(2)}) async-start(bf16[8,96,512]{2,1,0:T(8,128)(2,1)} %bitcast.7), calls=%async_computation.3 | async-start | bytes 1572864 | tf_op jit(solution)/shard_map/all_to_all | solution.py:189
  83.5 3.1 %collective-permute-start = (f32[512]{0:T(512)S(1)}, f32[512]{0:T(512)S(1)}, u32[]{:S(2)}, u32[]{:S(2)}) collective-permute-start(f32[512]{0:T(512)S(1)} %bitcast.54), channel_id=1, source_target_pairs={{0,1},{1,0},{2,3},{3,2},{4,5},{5,4},{6,7},{7,6},{8,9},{9,8},{10,11... | collective-permute-start | bytes 6152 | tf_op jit(solution)/shard_map/ppermute | solution.py:192
  111.7 15.4 %all-to-all-start.4 = ((f32[32,1,640]{2,1,0:T(1,128)}), f32[32,1,640]{2,1,0:T(1,128)S(1)}, u32[]{:S(2)}, u32[]{:S(2)}) async-start(f32[32,1,640]{2,1,0:T(1,128)} %broadcast_in_dim.33), calls=%async_computation.4 | async-start | bytes 163840 | tf_op jit(solution)/shard_map/all_to_all | solution.py:195
  118.6 17.9 %collective-permute-start.2 = (bf16[8,96,512]{2,1,0:T(8,128)(2,1)S(1)}, bf16[8,96,512]{2,1,0:T(8,128)(2,1)S(1)}, u32[]{:S(2)}, u32[]{:S(2)}) collective-permute-start(bf16[8,96,512]{2,1,0:T(8,128)(2,1)S(1)} %all-to-all-done.3), channel_id=1, source_target_pairs={{0,128},{128,256},{256,384},{384,0},{1,129},{129,257},{257,385},{3... | collective-permute-start | bytes 2359304 | tf_op jit(solution)/shard_map/ppermute | solution.py:116
  120.7 18.0 %collective-permute-start.1 = (bf16[8,96,512]{2,1,0:T(8,128)(2,1)S(1)}, bf16[8,96,512]{2,1,0:T(8,128)(2,1)S(1)}, u32[]{:S(2)}, u32[]{:S(2)}) collective-permute-start(bf16[8,96,512]{2,1,0:T(8,128)(2,1)S(1)} %all-to-all-done.3), channel_id=1, source_target_pairs={{0,384},{128,0},{256,128},{384,256},{1,385},{129,1},{257,129},{385... | collective-permute-start | bytes 2359304 | tf_op jit(solution)/shard_map/ppermute | solution.py:117
  136.5 5.9 %copy-start.2 = (bf16[8,96,512]{2,1,0:T(8,128)(2,1)}, bf16[8,96,512]{2,1,0:T(8,128)(2,1)S(1)}, u32[]{:S(2)}) copy-start(bf16[8,96,512]{2,1,0:T(8,128)(2,1)S(1)} %collective-permute-done.2) | copy-start | bytes 2359300
  136.5 9.7 %collective-permute-start.3 = (bf16[4,96,512]{2,1,0:T(8,128)(2,1)S(1)}, bf16[4,96,512]{2,1,0:T(8,128)(2,1)S(1)}, u32[]{:S(2)}, u32[]{:S(2)}) collective-permute-start(bf16[4,96,512]{2,1,0:T(8,128)(2,1)S(1)} %slice.74), channel_id=1, source_target_pairs={{0,128},{128,256},{256,384},{384,0},{1,129},{129,257},{257,385},{3... | collective-permute-start | bytes 1179656 | tf_op jit(solution)/shard_map/ppermute | solution.py:119
  138.7 3.7 %copy-start.3 = (bf16[8,96,512]{2,1,0:T(8,128)(2,1)}, bf16[8,96,512]{2,1,0:T(8,128)(2,1)S(1)}, u32[]{:S(2)}) copy-start(bf16[8,96,512]{2,1,0:T(8,128)(2,1)S(1)} %collective-permute-done.1) | copy-start | bytes 2359300
  138.8 10.9 %collective-permute-start.4 = (bf16[4,96,512]{2,1,0:T(8,128)(2,1)S(1)}, bf16[4,96,512]{2,1,0:T(8,128)(2,1)S(1)}, u32[]{:S(2)}, u32[]{:S(2)}) collective-permute-start(bf16[4,96,512]{2,1,0:T(8,128)(2,1)S(1)} %slice.76), channel_id=1, source_target_pairs={{0,384},{128,0},{256,128},{384,256},{1,385},{129,1},{257,129},{385... | collective-permute-start | bytes 1179656 | tf_op jit(solution)/shard_map/ppermute | solution.py:120
  150.0 41.9 %copy-start = (bf16[16,256,1024]{2,1,0:T(8,128)(2,1)S(1)}, bf16[16,256,1024]{2,1,0:T(8,128)(2,1)}, u32[]{:S(2)}) copy-start(bf16[16,256,1024]{2,1,0:T(8,128)(2,1)} %all-gather.2.cloned.1.call-done.w_ref) | copy-start | bytes 25165828
  161.4 16.0 %collective-permute-start.6 = (bf16[8,96,512]{2,1,0:T(8,128)(2,1)S(1)}, bf16[8,96,512]{2,1,0:T(8,128)(2,1)S(1)}, u32[]{:S(2)}, u32[]{:S(2)}) collective-permute-start(bf16[8,96,512]{2,1,0:T(8,128)(2,1)S(1)} %shard_map.55.own), channel_id=1, source_target_pairs={{0,128},{128,256},{256,384},{384,0},{1,129},{129,257},{257,385},{3... | collective-permute-start | bytes 2359304 | tf_op jit(solution)/shard_map/ppermute | solution.py:116
  163.3 17.7 %collective-permute-start.5 = (bf16[8,96,512]{2,1,0:T(8,128)(2,1)S(1)}, bf16[8,96,512]{2,1,0:T(8,128)(2,1)S(1)}, u32[]{:S(2)}, u32[]{:S(2)}) collective-permute-start(bf16[8,96,512]{2,1,0:T(8,128)(2,1)S(1)} %shard_map.55.own), channel_id=1, source_target_pairs={{0,384},{128,0},{256,128},{384,256},{1,385},{129,1},{257,129},{385... | collective-permute-start | bytes 2359304 | tf_op jit(solution)/shard_map/ppermute | solution.py:117
  177.4 9.8 %collective-permute-start.7 = (bf16[4,96,512]{2,1,0:T(8,128)(2,1)S(1)}, bf16[4,96,512]{2,1,0:T(8,128)(2,1)S(1)}, u32[]{:S(2)}, u32[]{:S(2)}) collective-permute-start(bf16[4,96,512]{2,1,0:T(8,128)(2,1)S(1)} %slice.79), channel_id=1, source_target_pairs={{0,128},{128,256},{256,384},{384,0},{1,129},{129,257},{257,385},{3... | collective-permute-start | bytes 1179656 | tf_op jit(solution)/shard_map/ppermute | solution.py:119
  181.1 10.9 %collective-permute-start.8 = (bf16[4,96,512]{2,1,0:T(8,128)(2,1)S(1)}, bf16[4,96,512]{2,1,0:T(8,128)(2,1)S(1)}, u32[]{:S(2)}, u32[]{:S(2)}) collective-permute-start(bf16[4,96,512]{2,1,0:T(8,128)(2,1)S(1)} %slice.80), channel_id=1, source_target_pairs={{0,384},{128,0},{256,128},{384,256},{1,385},{129,1},{257,129},{385... | collective-permute-start | bytes 1179656 | tf_op jit(solution)/shard_map/ppermute | solution.py:120
Sparse Core Ops, SparseCore 0:
  78.8 63.8 all-gather.1
